TPU v7x, 32 devices: a whole 2x2x4 slice. The times are simulated.
32 devices in a mesh: ens: 2 (over x), lon: 4 (over y, core), lat: 4 (over z).
Axes of the slice: x: 2, y: 2, z: 4, core: 2. Of those that a mesh axis runs over, the one named last changes fastest.
Arguments:
- members: float32 [2, 80, 32, 640], P('ens', 'lat', 'lon'), may hold values from -6 to 6
- analysis: float32 [80, 32, 640], P('lat', 'lon', 'ens'), may hold values from -6 to 6
- stencils: float32 [7, 7, 7, 80], replicated, may hold values from -0.84 to 0.84
- mixing: float32 [7, 640, 640], replicated, may hold values from -0.09375 to 0.09375
Outputs:
- members_grad: float32 [2, 80, 32, 640], P('ens', 'lat', 'lon')
- crps_field: float32 [80, 32, 640], P('lat', 'lon', 'ens')
All inputs are finite; a program needn't handle non-finite values.
Results may differ from a plain program's by a relative error of at most 0.00016.
Values sent between devices are 32-bit elements; how exact they have to be, the bound alone decides.
No kernel may reach another device: no remote copies, remote signals or barrier semaphores. Data moves between devices by JAX's collectives and lax.ppermute only.
A program may use at most 128 MiB of HBM per device.

v0:
```python
import functools

import jax
import jax.numpy as jnp
from jax import lax
from jax.experimental import pallas as pl
from jax.experimental.pallas import tpu as pltpu
from jax.sharding import PartitionSpec as P

SMOOTH = 0.01
SLOTS = 16
DEPTH = 256
EDGE = 256
VMEM = pl.BlockSpec(memory_space=pltpu.VMEM)
SMEM = pl.BlockSpec(memory_space=pltpu.SMEM)


def f32(*shape):
    return jax.ShapeDtypeStruct(shape, jnp.float32)


def b16(*shape):
    return jax.ShapeDtypeStruct(shape, jnp.bfloat16)


def split(value):
    high = value.astype(jnp.bfloat16)
    low = (value - high.astype(jnp.float32)).astype(jnp.bfloat16)
    return high, low


def product(left, right, axis):
    return lax.dot_general(
        left, right, (((1,), (axis,)), ((), ())), preferred_element_type=jnp.float32
    )


def product3(left_high, left_low, right_high, right_low, axis):
    rows = left_high.shape[0]
    both = product(jnp.concatenate([left_high, left_low], 0), right_high, axis)
    return both[:rows] + both[rows:] + product(left_high, right_low, axis)


def call(body, name, out_shape, operands, specs=None, scratch=(), flops=0, size=0, limit=24):
    return pl.pallas_call(
        body,
        out_shape=out_shape,
        in_specs=specs or [VMEM] * len(operands),
        out_specs=[VMEM] * len(out_shape),
        scratch_shapes=scratch,
        cost_estimate=pl.CostEstimate(flops=flops, bytes_accessed=size, transcendentals=0),
        compiler_params=pltpu.CompilerParams(vmem_limit_bytes=limit << 20),
        name=name,
    )(*operands)


def band_kernel(place_ref, stencils_ref, high_ref, low_ref, table_ref, band_ref, *, rows, forward):
    bases, span, _, total = stencils_ref.shape
    blocks = high_ref.shape[0]
    margin = span // 2
    breadth = high_ref.shape[1] // (bases * rows)
    first_row = place_ref[0]
    iota = lambda shape, axis: lax.broadcasted_iota(jnp.int32, shape, axis)

    table_ref[...] = jnp.zeros_like(table_ref)
    for base in range(bases):
        for tap in range(span):
            at = (base * 8 + tap) * 8
            table_ref[at : at + span, :total] = stencils_ref[base, tap]
    table = split(table_ref[...])

    group = blocks * SLOTS
    shifts = [margin] if forward else list(range(span))
    count = group * len(shifts)
    line, latitude = iota((count, table_ref.shape[1]), 0), iota((count, table_ref.shape[1]), 1)
    local_row = line % SLOTS
    shift = shifts[0] if forward else line // group
    wanted = first_row + (line % group) // SLOTS * rows + local_row + shift - margin
    picks = ((latitude == wanted) & (local_row < rows)).astype(jnp.float32).astype(jnp.bfloat16)

    width = table_ref.shape[0]
    tap_of = iota((group, width), 1) // 8 % 8
    stacked = []
    for part in table:
        picked = product(picks, part, 1)
        if forward:
            line = iota((group, width), 0)
            reach = first_row + line // SLOTS * rows + line % SLOTS + tap_of - margin
            taps = jnp.where((reach >= 0) & (reach < total), picked, 0.0)
        else:
            taps = jnp.zeros((group, width), jnp.float32)
            for tap in range(span):
                here = picked[tap * group : (tap + 1) * group]
                taps = jnp.where(tap_of == span - 1 - tap, here, taps)
        stacked += [taps[:, at : at + 128] for at in range(0, width, 128)]
    left = jnp.concatenate(stacked, 0).astype(jnp.bfloat16)
    pairs = width // 128

    source, target = iota((128, 256), 0), iota((128, 256), 1)
    slot = target % SLOTS
    column = jnp.where(
        slot < breadth,
        slot,
        jnp.where(slot < breadth + margin, slot - breadth - margin, slot - margin),
    )
    row_tap, column_tap = source // 8 % 8, source % 8
    to_row = target % 128 // SLOTS
    if not forward:
        row_tap, column_tap = span - 1 - row_tap, span - 1 - column_tap
    same = (row_tap == to_row) & (source // 64 == target // 128) & (slot < breadth + 2 * margin)
    same = same & (source % 8 < span) & (source // 8 % 8 < span)
    offset = jnp.where(same, column_tap - column, 1000)
    zeros = jnp.zeros((left.shape[0], 128), jnp.float32)
    for j in range(breadth):
        spread = (offset == margin - j).astype(jnp.float32).astype(jnp.bfloat16)
        both = product(left, spread, 0)
        for odd in range(2):
            wide = jnp.concatenate([both[:, odd * 128 : odd * 128 + 128], zeros], 1)
            wide = pltpu.roll(wide, 0, 1, stride=SLOTS, stride_axis=0)
            for part in range(2):
                for pair in range(pairs):
                    base = 2 * pair + odd
                    if base >= bases:
                        continue
                    for block in range(blocks):
                        at = ((part * pairs + pair) * blocks + block) * SLOTS
                        lines = pl.ds(base * rows * breadth + j, rows, stride=breadth)
                        for half in range(2):
                            band_ref[part, half, block, lines, :] = wide[
                                at : at + rows, half * 128 : half * 128 + 128
                            ]
    for half in range(2):
        lanes = slice(half * 128, half * 128 + 128)
        high_ref[:, :, lanes] = band_ref[0, half].astype(jnp.bfloat16)
        low_ref[:, :, lanes] = band_ref[1, half].astype(jnp.bfloat16)


def bands(place, stencils, rows, blocks, breadth, forward):
    bases, span, _, total = stencils.shape
    lines = bases * rows * breadth
    return call(
        functools.partial(band_kernel, rows=rows, forward=forward),
        "band_forward" if forward else "band_backward",
        [b16(blocks, lines, DEPTH)] * 2,
        [place, stencils],
        [SMEM, VMEM],
        [
            pltpu.VMEM(((bases + 1) // 2 * 128, -(-total // 128) * 128), jnp.float32),
            pltpu.VMEM((2, DEPTH // 128, blocks, lines, 128), jnp.float32),
        ],
        flops=10**9, size=4 << 20,
    )


def pack_sides(field_ref, up_ref, down_ref, breadth):
    height = field_ref.shape[0] // breadth
    margin = up_ref.shape[0] // height
    for row in range(height):
        at = slice(row * margin, (row + 1) * margin)
        up_ref[at, :] = field_ref[(row + 1) * breadth - margin : (row + 1) * breadth, :]
        down_ref[at, :] = field_ref[row * breadth : row * breadth + margin, :]


def sides(flat, breadth, margin):
    shape = f32(flat.shape[0] // breadth * margin, flat.shape[1])
    return call(
        functools.partial(pack_sides, breadth=breadth), "sides", [shape] * 2, [flat],
        size=1 << 20, limit=8,
    )


def assemble_kernel(place_ref, field_ref, left_ref, right_ref, wide_ref, first_ref, second_ref, *, breadth):
    height = field_ref.shape[0] // breadth
    margin = left_ref.shape[0] // height
    spare = jnp.zeros((SLOTS - breadth - 2 * margin, field_ref.shape[1]), jnp.float32)
    for row in range(height):
        at = row * SLOTS
        here = slice(row * margin, (row + 1) * margin)
        wide_ref[at : at + breadth, :] = field_ref[row * breadth : (row + 1) * breadth, :]
        wide_ref[at + breadth : at + SLOTS, :] = jnp.concatenate(
            [left_ref[here, :], right_ref[here, :], spare], 0
        )
    low = wide_ref[: margin * SLOTS, :]
    high = wide_ref[(height - margin) * SLOTS :, :]
    odd = place_ref[1] == 1
    first_ref[...] = jnp.where(odd, low, high)
    second_ref[...] = jnp.where(odd, high, low)


def assemble(place, flat, left, right, breadth):
    cells, channels = flat.shape
    height = cells // breadth
    edge = f32(left.shape[0] // height * SLOTS, channels)
    return call(
        functools.partial(assemble_kernel, breadth=breadth), "assemble",
        [f32(height * SLOTS, channels), edge, edge],
        [place, flat, left, right], [SMEM, VMEM, VMEM, VMEM], size=2 << 20, limit=8,
    )


def ring(up, down):
    count = lax.axis_size("lon")
    there = [(i, (i + 1) % count) for i in range(count)]
    back = [(b, a) for a, b in there]
    return lax.ppermute(up, "lon", there), lax.ppermute(down, "lon", back)


def swap(first, second):
    count = lax.axis_size("lat")

    def one(piece, lows):
        table = {i: i for i in range(count)}
        for low in lows:
            if low + 1 < count:
                table[low], table[low + 1] = low + 1, low
        return lax.ppermute(piece, "lat", sorted(table.items()))

    return one(first, range(0, count, 2)), one(second, range(1, count, 2))


def stencil(place_ref, wide_ref, first_ref, second_ref, bhigh_ref, blow_ref, shigh_ref, slow_ref, xhigh_ref, xlow_ref):
    bases, total, channels = shigh_ref.shape
    blocks = bhigh_ref.shape[0]
    cells = total // blocks

    def fill(at, ref):
        high, low = split(ref[...])
        xhigh_ref[pl.ds(at, ref.shape[0]), :] = high
        xlow_ref[pl.ds(at, ref.shape[0]), :] = low

    edge = first_ref.shape[0]
    fill(edge, wide_ref)
    fill(pl.multiple_of(place_ref[2], SLOTS), first_ref)
    fill(pl.multiple_of(place_ref[3], SLOTS), second_ref)
    stride = (wide_ref.shape[0]) // blocks
    for block in range(blocks):
        window = slice(block * stride, block * stride + DEPTH)
        got = product3(bhigh_ref[block], blow_ref[block], xhigh_ref[window], xlow_ref[window], 0)
        high, low = split(got)
        here = slice(block * cells, (block + 1) * cells)
        shigh_ref[:, here, :] = high.reshape(bases, cells, channels)
        slow_ref[:, here, :] = low.reshape(bases, cells, channels)


def contract(shigh_ref, slow_ref, mixing_ref, acc_ref, lanes, axis):
    acc_ref[...] = jnp.zeros_like(acc_ref)

    def step(base, _):
        weight_high, weight_low = split(mixing_ref[base, :, lanes])
        acc_ref[...] += product3(shigh_ref[base], slow_ref[base], weight_high, weight_low, axis)

    lax.fori_loop(0, mixing_ref.shape[0], step, None)


def forward_first(place_ref, wide_ref, first_ref, second_ref, bhigh_ref, blow_ref, mixing_ref, field_ref,
                  predicted_ref, bounded_ref, shigh_ref, slow_ref, xhigh_ref, xlow_ref, acc_ref):
    stencil(place_ref, wide_ref, first_ref, second_ref, bhigh_ref, blow_ref, shigh_ref, slow_ref, xhigh_ref, xlow_ref)
    lanes = slice(0, acc_ref.shape[1])
    contract(shigh_ref, slow_ref, mixing_ref, acc_ref, lanes, 0)
    bounded = jnp.tanh(acc_ref[...])
    bounded_ref[...] = bounded
    predicted_ref[...] = field_ref[:, lanes] + bounded


def forward_rest(shigh_ref, slow_ref, mixing_ref, field_ref, predicted_ref, bounded_ref, acc_ref):
    lanes = slice(field_ref.shape[1] - acc_ref.shape[1], field_ref.shape[1])
    contract(shigh_ref, slow_ref, mixing_ref, acc_ref, lanes, 0)
    bounded = jnp.tanh(acc_ref[...])
    bounded_ref[...] = bounded
    predicted_ref[...] = field_ref[:, lanes] + bounded


def backward_all(place_ref, wide_ref, first_ref, second_ref, bhigh_ref, blow_ref, mixing_ref, grad_ref, tail_ref,
                 out_ref, shigh_ref, slow_ref, xhigh_ref, xlow_ref, acc_ref):
    stencil(place_ref, wide_ref, first_ref, second_ref, bhigh_ref, blow_ref, shigh_ref, slow_ref, xhigh_ref, xlow_ref)
    contract(shigh_ref, slow_ref, mixing_ref, acc_ref, slice(None), 1)
    edge = grad_ref.shape[1]
    out_ref[:, :edge] = acc_ref[:, :edge] + grad_ref[...]
    out_ref[:, edge:] = acc_ref[:, edge:] + tail_ref[...]


def slope(value):
    return value * lax.rsqrt(value * value + SMOOTH)


def soft(value):
    return jnp.sqrt(value * value + SMOOTH)


def loss_first(own_ref, other_ref, bounded_ref, analysis_ref, grad_ref, inner_ref):
    analysis = analysis_ref[:, : own_ref.shape[1]]
    own = own_ref[...] - analysis
    grad = slope(own) - slope(own - (other_ref[...] - analysis))
    grad_ref[...] = grad
    inner_ref[...] = grad * (1.0 - bounded_ref[...] * bounded_ref[...])


def loss_rest(own_ref, other_ref, bounded_ref, analysis_ref, before_ref, grad_ref, inner_ref, up_ref, down_ref, *, breadth):
    edge = before_ref.shape[1]
    analysis = analysis_ref[:, edge:]
    own = own_ref[...] - analysis
    grad = slope(own) - slope(own - (other_ref[...] - analysis))
    grad_ref[...] = grad
    inner_ref[:, :edge] = before_ref[...]
    inner_ref[:, edge:] = grad * (1.0 - bounded_ref[...] * bounded_ref[...])
    pack_sides(inner_ref, up_ref, down_ref, breadth)


def whole_analysis(place_ref, mine_ref, theirs_ref, out_ref):
    half = mine_ref.shape[1]
    first = place_ref[4] == 0
    mine, theirs = mine_ref[...], theirs_ref[...]
    out_ref[:, :half] = jnp.where(first, mine, theirs)
    out_ref[:, half:] = jnp.where(first, theirs, mine)


def crps_kernel(place_ref, own1_ref, own2_ref, other1_ref, other2_ref, mine_ref, out_ref):
    half = mine_ref.shape[1]
    edge = own1_ref.shape[1]
    for part in range(2):
        @pl.when(place_ref[4] == part)
        def _():
            low, high = part * half, (part + 1) * half
            pieces = []
            if low < edge:
                pieces.append((own1_ref, other1_ref, slice(low, min(high, edge)), 0))
            if high > edge:
                start = max(low, edge)
                pieces.append((own2_ref, other2_ref, slice(start - edge, high - edge), start - low))
            for own_ref, other_ref, lanes, at in pieces:
                here = slice(at, at + lanes.stop - lanes.start)
                mine = mine_ref[:, here]
                own = own_ref[:, lanes] - mine
                other = other_ref[:, lanes] - mine
                gap = own - other
                pair = 2.0 * (soft(gap) + jnp.sqrt(jnp.full_like(gap, SMOOTH)))
                out_ref[:, here] = 0.5 * (soft(own) + soft(other)) - pair / 4.0


def loss_many(predicted, bounded, analysis):
    grouped = lax.all_to_all(predicted[None], "ens", split_axis=2, concat_axis=0, tiled=True)
    misfit = grouped - analysis[None]
    count = misfit.shape[0]

    def step(other, totals):
        differ = misfit - lax.dynamic_index_in_dim(misfit, other, 0)
        smooth_abs = jnp.sqrt(differ * differ + SMOOTH)
        return totals[0] + smooth_abs.sum(0), totals[1] + differ / smooth_abs

    sums, slopes = lax.fori_loop(
        0, count, step, (jnp.zeros_like(misfit[0]), jnp.zeros_like(misfit))
    )
    own = jnp.sqrt(misfit * misfit + SMOOTH)
    crps = jnp.mean(own, 0) - sums / (2.0 * count * (count - 1))
    grad = misfit / own - slopes / (count - 1.0)
    grad = lax.all_to_all(grad, "ens", split_axis=0, concat_axis=2, tiled=True)[0]
    return grad, grad * (1.0 - bounded * bounded), crps


def local(members, analysis, stencils, mixing):
    _, height, breadth, channels = members.shape
    bases, span = stencils.shape[:2]
    margin = span // 2
    blocks = next(
        n for n in range(1, height + 1)
        if height % n == 0 and height // n + 2 * margin <= DEPTH // SLOTS
    )
    rows = height // blocks
    cells = height * breadth
    pair = lax.axis_size("ens") == 2
    flat = members.reshape(cells, channels)
    mine = analysis.reshape(cells, analysis.shape[2])

    odd = lax.axis_index("lat") % 2
    end = (height + margin) * SLOTS
    place = jnp.stack([
        lax.axis_index("lat") * height, odd, (1 - odd) * end, odd * end, lax.axis_index("ens")
    ]).astype(jnp.int32)

    left, right = ring(*sides(flat, breadth, margin))
    if pair:
        theirs = lax.ppermute(mine, "ens", [(0, 1), (1, 0)])
    band = bands(place, stencils, rows, blocks, breadth, True)
    wide, first, second = assemble(place, flat, left, right, breadth)
    first, second = swap(first, second)

    window = pltpu.VMEM(((height + 2 * margin) * SLOTS, channels), jnp.bfloat16)
    taps = [b16(bases, cells, channels)] * 2
    stencil_flops = 6 * blocks * bases * rows * breadth * DEPTH * channels
    mix_flops = 6 * cells * bases * channels * channels
    rest = channels - EDGE
    predicted1, bounded1, shigh, slow = call(
        forward_first, "forward_first", [f32(cells, EDGE)] * 2 + taps,
        [place, wide, first, second, *band, mixing, flat], [SMEM] + [VMEM] * 7,
        [window, window, pltpu.VMEM((cells, EDGE), jnp.float32)],
        flops=stencil_flops + mix_flops * EDGE // channels,
    )
    if pair:
        other1 = lax.ppermute(predicted1, "ens", [(0, 1), (1, 0)])
    predicted2, bounded2 = call(
        forward_rest, "forward_rest", [f32(cells, rest)] * 2, [shigh, slow, mixing, flat],
        scratch=[pltpu.VMEM((cells, rest), jnp.float32)], flops=mix_flops * rest // channels,
    )
    back = bands(place, stencils, rows, blocks, breadth, False)
    if pair:
        other2 = lax.ppermute(predicted2, "ens", [(0, 1), (1, 0)])
        (known,) = call(
            whole_analysis, "whole_analysis", [f32(cells, channels)], [place, mine, theirs],
            [SMEM, VMEM, VMEM], size=1 << 20, limit=8,
        )
        grad1, inner1 = call(
            loss_first, "loss_first", [f32(cells, EDGE)] * 2,
            [predicted1, other1, bounded1, known], size=1 << 20, limit=8,
        )
        side = f32(height * margin, channels)
        grad2, inner, up, down = call(
            functools.partial(loss_rest, breadth=breadth), "loss_rest",
            [f32(cells, rest), f32(cells, channels), side, side],
            [predicted2, other2, bounded2, known, inner1], size=2 << 20, limit=8,
        )
        (crps,) = call(
            crps_kernel, "crps", [f32(*mine.shape)],
            [place, predicted1, predicted2, other1, other2, mine], [SMEM] + [VMEM] * 5,
            size=1 << 20, limit=8,
        )
    else:
        predicted = jnp.concatenate([predicted1, predicted2], 1)
        bounded = jnp.concatenate([bounded1, bounded2], 1)
        grad, inner, crps = loss_many(predicted, bounded, mine)
        grad1, grad2 = grad[:, :EDGE], grad[:, EDGE:]
        up, down = sides(inner, breadth, margin)

    left, right = ring(up, down)
    wide, first, second = assemble(place, inner, left, right, breadth)
    first, second = swap(first, second)
    (result,) = call(
        backward_all, "backward_all", [f32(cells, channels)],
        [place, wide, first, second, *back, mixing, grad1, grad2], [SMEM] + [VMEM] * 8,
        [pltpu.VMEM(s.shape, s.dtype) for s in taps]
        + [window, window, pltpu.VMEM((cells, channels), jnp.float32)],
        flops=stencil_flops + mix_flops,
    )
    return result.reshape(members.shape), crps.reshape(analysis.shape)


def solution(mesh):
    in_specs = (P("ens", "lat", "lon", None), P("lat", "lon", "ens"), P(), P())
    out_specs = (P("ens", "lat", "lon", None), P("lat", "lon", "ens"))
    return jax.shard_map(local, mesh=mesh, in_specs=in_specs, out_specs=out_specs, check_vma=False)
```

profile of v0, /device:TPU:10, one launch (start us, length us, event | category | flops | bytes accessed | tf_op | source)
XLA Modules:
  0.0 72.6 jit_solution(14958753734078072975)
XLA Ops:
  0.6 0.0 copy-start.2
  0.6 1.0 %copy-done.2 = f32[1,20,8,640]{3,2,1,0:T(8,128)S(1)} copy-done((f32[1,20,8,640]{3,2,1,0:T(8,128)S(1)}, f32[1,20,8,640]{3,2,1,0:T(8,128)}, u32[]{:S(2)}) %copy-start.2) | copy-done | bytes 409624
  1.6 0.1 sides.1
  1.7 0.1 collective-permute-start
  1.8 1.7 %collective-permute-start.1 = (f32[60,640]{1,0:T(8,128)S(1)}, f32[60,640]{1,0:T(8,128)S(1)}, u32[]{:S(2)}, u32[]{:S(2)}) collective-permute-start(f32[60,640]{1,0:T(8,128)S(1)} %get-tuple-element.27), channel_id=1, source_target_pairs={{4,0},{8,4},{12,8},{0,12},{5,1},{9,5},{13,9},{1,13},{6,2},{10,6},{... | collective-permute-start | bytes 460808 | tf_op jit(solution)/shard_map/ppermute | solution.py:205
  3.5 0.1 stack.23.place_ref
  3.6 2.9 %collective-permute-done.left_ref = f32[60,640]{1,0:T(8,128)S(1)} collective-permute-done((f32[60,640]{1,0:T(8,128)S(1)}, f32[60,640]{1,0:T(8,128)S(1)}, u32[]{:S(2)}, u32[]{:S(2)}) %collective-permute-start) | collective-permute-done | bytes 153632 | tf_op jit(solution)/shard_map/ppermute | solution.py:205
  6.5 0.8 %collective-permute-done.1.right_ref = f32[60,640]{1,0:T(8,128)S(1)} collective-permute-done((f32[60,640]{1,0:T(8,128)S(1)}, f32[60,640]{1,0:T(8,128)S(1)}, u32[]{:S(2)}, u32[]{:S(2)}) %collective-permute-start.1) | collective-permute-done | bytes 153632 | tf_op jit(solution)/shard_map/ppermute | solution.py:205
  7.3 0.0 copy-start.3
  7.3 1.0 %copy-done.3 = f32[1,20,8,640]{3,2,1,0:T(8,128)S(1)} copy-done((f32[1,20,8,640]{3,2,1,0:T(8,128)S(1)}, f32[1,20,8,640]{3,2,1,0:T(8,128)}, u32[]{:S(2)}) %copy-start.3) | copy-done | bytes 409624
  8.3 0.7 assemble.2
  9.0 0.5 collective-permute-start.2
  9.5 0.0 copy-start.4
  9.5 4.7 %collective-permute-start.3 = (f32[48,640]{1,0:T(8,128)S(1)}, f32[48,640]{1,0:T(8,128)S(1)}, u32[]{:S(2)}, u32[]{:S(2)}) collective-permute-start(f32[48,640]{1,0:T(8,128)S(1)} %get-tuple-element.30), channel_id=1, source_target_pairs={{0,0},{1,2},{2,1},{3,3},{4,4},{5,6},{6,5},{7,7},{8,8},{9,10},{10,9... | collective-permute-start | bytes 368648 | tf_op jit(solution)/shard_map/ppermute | solution.py:216
  14.2 0.0 copy-start.6
  14.3 0.9 %copy-done.6 = f32[7,7,7,80]{3,2,1,0:T(8,128)S(1)} copy-done((f32[7,7,7,80]{3,2,1,0:T(8,128)S(1)}, f32[7,7,7,80]{3,2,1,0:T(8,128)}, u32[]{:S(2)}) %copy-start.6) | copy-done | bytes 109784
  15.2 1.6 %band_forward.1 = (bf16[2,560,256]{2,1,0:T(8,128)(2,1)S(1)}, bf16[2,560,256]{2,1,0:T(8,128)(2,1)S(1)}) custom-call(s32[5]{0:T(128)S(1)} %stack.23.place_ref, f32[7,7,7,80]{3,2,1,0:T(8,128)S(1)} %copy-done.6), custom_call_target="tpu_custom_call" | custom-call | flops 1000000000 | bytes 4194304 | tf_op jit(solution)/shard_map/band_forward/pallas_call | solution.py:45
  16.8 0.0 collective-permute-done.2.first_ref
  16.8 1.5 %collective-permute-done.3.second_ref = f32[48,640]{1,0:T(8,128)S(1)} collective-permute-done((f32[48,640]{1,0:T(8,128)S(1)}, f32[48,640]{1,0:T(8,128)S(1)}, u32[]{:S(2)}, u32[]{:S(2)}) %collective-permute-start.3) | collective-permute-done | bytes 122912 | tf_op jit(solution)/shard_map/ppermute | solution.py:216
  18.3 0.0 copy-done.4
  18.3 0.0 copy-start
  18.3 4.3 %copy-done = f32[7,640,640]{2,1,0:T(8,128)S(1)} copy-done((f32[7,640,640]{2,1,0:T(8,128)S(1)}, f32[7,640,640]{2,1,0:T(8,128)}, u32[]{:S(2)}) %copy-start) | copy-done | bytes 11468824
  22.5 0.0 copy-start.1
  22.5 4.8 %forward_first.1 = (f32[160,256]{1,0:T(8,128)S(1)}, f32[160,256]{1,0:T(8,128)S(1)}, bf16[7,160,640]{2,1,0:T(8,128)(2,1)S(1)}, bf16[7,160,640]{2,1,0:T(8,128)(2,1)S(1)}) custom-call(s32[5]{0:T(128)S(1)} %stack.23.place_ref, f32[320,640]{1,0:T(8,128)S(1)} %get-tuple-element.28.wide_ref, f32[48,640]{1,0:T(8,128)S(1)} %collective-permute-done.2.first_ref, ...), custom_call_target="tpu_custom_call" | custom-call | flops 2202009600 | tf_op jit(solution)/shard_map/forward_first/pallas_call | solution.py:45
  27.3 0.0 copy-done.1
  27.3 0.0 copy-start.5
  27.3 3.8 %forward_rest.1 = (f32[160,384]{1,0:T(8,128)S(1)}, f32[160,384]{1,0:T(8,128)S(1)}) custom-call(bf16[7,160,640]{2,1,0:T(8,128)(2,1)S(1)} %get-tuple-element.33.shigh_ref, bf16[7,160,640]{2,1,0:T(8,128)(2,1)S(1)} %get-tuple-element.34.slow_ref, f32[7,640,640]{2,1,0:T(8,128)S(1)} %copy-done.1, f32[160,640]{1,0:T(8,128)S(1)} %bitcast.12), custom_call_target="tpu_custom_call" | custom-call | flops 1651507200 | tf_op jit(solution)/shard_map/forward_rest/pallas_call | solution.py:45
  31.1 0.6 collective-permute-start.4
  31.7 0.0 copy-done.5
  31.7 1.5 %collective-permute-start.5 = (f32[160,320]{1,0:T(8,128)S(1)}, f32[160,320]{1,0:T(8,128)S(1)}, u32[]{:S(2)}, u32[]{:S(2)}) collective-permute-start(f32[160,320]{1,0:T(8,128)S(1)} %bitcast.13), channel_id=1, source_target_pairs={{0,16},{16,0},{1,17},{17,1},{2,18},{18,2},{3,19},{19,3},{4,20},{20... | collective-permute-start | bytes 614408 | tf_op jit(solution)/shard_map/ppermute | solution.py:382
  33.2 0.5 collective-permute-start.6
  33.7 11.5 %collective-permute-done.5.theirs_ref = f32[160,320]{1,0:T(8,128)S(1)} collective-permute-done((f32[160,320]{1,0:T(8,128)S(1)}, f32[160,320]{1,0:T(8,128)S(1)}, u32[]{:S(2)}, u32[]{:S(2)}) %collective-permute-start.5) | collective-permute-done | bytes 204832 | tf_op jit(solution)/shard_map/ppermute | solution.py:382
  45.3 0.7 whole_analysis.1.analysis_ref
  46.0 1.8 %collective-permute-done.6.other_ref.other1_ref = f32[160,256]{1,0:T(8,128)S(1)} collective-permute-done((f32[160,256]{1,0:T(8,128)S(1)}, f32[160,256]{1,0:T(8,128)S(1)}, u32[]{:S(2)}, u32[]{:S(2)}) %collective-permute-start.6) | collective-permute-done | bytes 163872 | tf_op jit(solution)/shard_map/ppermute | solution.py:399
  47.8 0.1 loss_first.1
  47.9 0.0 collective-permute-done.4.other_ref.other2_ref
  47.9 0.3 loss_rest.1
  48.2 0.1 collective-permute-start.7
  48.3 1.7 %collective-permute-start.8 = (f32[60,640]{1,0:T(8,128)S(1)}, f32[60,640]{1,0:T(8,128)S(1)}, u32[]{:S(2)}, u32[]{:S(2)}) collective-permute-start(f32[60,640]{1,0:T(8,128)S(1)} %get-tuple-element.42), channel_id=1, source_target_pairs={{4,0},{8,4},{12,8},{0,12},{5,1},{9,5},{13,9},{1,13},{6,2},{10,6},{... | collective-permute-start | bytes 460808 | tf_op jit(solution)/shard_map/ppermute | solution.py:205
  50.0 3.2 %collective-permute-done.7.left_ref = f32[60,640]{1,0:T(8,128)S(1)} collective-permute-done((f32[60,640]{1,0:T(8,128)S(1)}, f32[60,640]{1,0:T(8,128)S(1)}, u32[]{:S(2)}, u32[]{:S(2)}) %collective-permute-start.7) | collective-permute-done | bytes 153632 | tf_op jit(solution)/shard_map/ppermute | solution.py:205
  53.2 0.3 collective-permute-done.8.right_ref
  53.5 0.7 assemble.3
  54.2 3.4 %collective-permute-start.10 = (f32[48,640]{1,0:T(8,128)S(1)}, f32[48,640]{1,0:T(8,128)S(1)}, u32[]{:S(2)}, u32[]{:S(2)}) collective-permute-start(f32[48,640]{1,0:T(8,128)S(1)} %get-tuple-element.45), channel_id=1, source_target_pairs={{0,0},{1,2},{2,1},{3,3},{4,4},{5,6},{6,5},{7,7},{8,8},{9,10},{10,9... | collective-permute-start | bytes 368648 | tf_op jit(solution)/shard_map/ppermute | solution.py:216
  57.6 0.1 collective-permute-start.9
  57.6 1.7 %band_backward.1 = (bf16[2,560,256]{2,1,0:T(8,128)(2,1)S(1)}, bf16[2,560,256]{2,1,0:T(8,128)(2,1)S(1)}) custom-call(s32[5]{0:T(128)S(1)} %stack.23.place_ref, f32[7,7,7,80]{3,2,1,0:T(8,128)S(1)} %copy-done.6), custom_call_target="tpu_custom_call" | custom-call | flops 1000000000 | bytes 4194304 | tf_op jit(solution)/shard_map/band_backward/pallas_call | solution.py:45
  59.3 1.8 %crps.1 = f32[160,320]{1,0:T(8,128)} custom-call(s32[5]{0:T(128)S(1)} %stack.23.place_ref, f32[160,256]{1,0:T(8,128)S(1)} %get-tuple-element.37.own_ref.own1_ref, f32[160,384]{1,0:T(8,128)S(1)} %get-tuple-element.35.own_ref.own2_ref, f32[160,256]{1,0:T(8,128)S(1)} %collective-permute-done.6.other_ref.other1_ref, ...), custom_call_target="tpu_custom_call" | custom-call | bytes 1048576 | tf_op jit(solution)/shard_map/crps/pallas_call | solution.py:45
  61.1 1.1 %collective-permute-done.10.second_ref = f32[48,640]{1,0:T(8,128)S(1)} collective-permute-done((f32[48,640]{1,0:T(8,128)S(1)}, f32[48,640]{1,0:T(8,128)S(1)}, u32[]{:S(2)}, u32[]{:S(2)}) %collective-permute-start.10) | collective-permute-done | bytes 122912 | tf_op jit(solution)/shard_map/ppermute | solution.py:216
  62.2 1.4 %collective-permute-done.9.first_ref = f32[48,640]{1,0:T(8,128)S(1)} collective-permute-done((f32[48,640]{1,0:T(8,128)S(1)}, f32[48,640]{1,0:T(8,128)S(1)}, u32[]{:S(2)}, u32[]{:S(2)}) %collective-permute-start.9) | collective-permute-done | bytes 122912 | tf_op jit(solution)/shard_map/ppermute | solution.py:216
  63.6 9.0 %backward_all.1 = f32[160,640]{1,0:T(8,128)} custom-call(s32[5]{0:T(128)S(1)} %stack.23.place_ref, f32[320,640]{1,0:T(8,128)S(1)} %get-tuple-element.43.wide_ref, f32[48,640]{1,0:T(8,128)S(1)} %collective-permute-done.9.first_ref, f32[48,640]{1,0:T(8,128)S(1)} %collective-permute-done.10.second_ref, bf16[2,560,256]{2,1,0:T(8,128)(2,1)S(1)} %get-tuple-element.46.bhigh_ref, ...), custom_call_target="tpu_custom_call" | custom-call | flops 3853516800 | tf_op jit(solution)/shard_map/backward_all/pallas_call | solution.py:45
Async XLA Ops:
  0.6 1.0 %copy-start.2 = (f32[1,20,8,640]{3,2,1,0:T(8,128)S(1)}, f32[1,20,8,640]{3,2,1,0:T(8,128)}, u32[]{:S(2)}) copy-start(f32[1,20,8,640]{3,2,1,0:T(8,128)} %param.4) | copy-start | bytes 1228804
  1.7 4.8 %collective-permute-start = (f32[60,640]{1,0:T(8,128)S(1)}, f32[60,640]{1,0:T(8,128)S(1)}, u32[]{:S(2)}, u32[]{:S(2)}) collective-permute-start(f32[60,640]{1,0:T(8,128)S(1)} %get-tuple-element.26), channel_id=1, source_target_pairs={{0,4},{4,8},{8,12},{12,0},{1,5},{5,9},{9,13},{13,1},{2,6},{6,10},{... | collective-permute-start | bytes 460808 | tf_op jit(solution)/shard_map/ppermute | solution.py:205
  1.8 5.5 %collective-permute-start.1 = (f32[60,640]{1,0:T(8,128)S(1)}, f32[60,640]{1,0:T(8,128)S(1)}, u32[]{:S(2)}, u32[]{:S(2)}) collective-permute-start(f32[60,640]{1,0:T(8,128)S(1)} %get-tuple-element.27), channel_id=1, source_target_pairs={{4,0},{8,4},{12,8},{0,12},{5,1},{9,5},{13,9},{1,13},{6,2},{10,6},{... | collective-permute-start | bytes 460808 | tf_op jit(solution)/shard_map/ppermute | solution.py:205
  7.3 1.0 %copy-start.3 = (f32[1,20,8,640]{3,2,1,0:T(8,128)S(1)}, f32[1,20,8,640]{3,2,1,0:T(8,128)}, u32[]{:S(2)}) copy-start(f32[1,20,8,640]{3,2,1,0:T(8,128)} %param.4) | copy-start | bytes 1228804
  9.0 7.8 %collective-permute-start.2 = (f32[48,640]{1,0:T(8,128)S(1)}, f32[48,640]{1,0:T(8,128)S(1)}, u32[]{:S(2)}, u32[]{:S(2)}) collective-permute-start(f32[48,640]{1,0:T(8,128)S(1)} %get-tuple-element.29), channel_id=1, source_target_pairs={{0,1},{1,0},{2,3},{3,2},{4,5},{5,4},{6,7},{7,6},{8,9},{9,8},{10,11... | collective-permute-start | bytes 368648 | tf_op jit(solution)/shard_map/ppermute | solution.py:216
  9.5 8.8 %copy-start.4 = (f32[1,20,8,640]{3,2,1,0:T(8,128)S(1)}, f32[1,20,8,640]{3,2,1,0:T(8,128)}, u32[]{:S(2)}) copy-start(f32[1,20,8,640]{3,2,1,0:T(8,128)} %param.4) | copy-start | bytes 1228804
  9.5 8.8 %collective-permute-start.3 = (f32[48,640]{1,0:T(8,128)S(1)}, f32[48,640]{1,0:T(8,128)S(1)}, u32[]{:S(2)}, u32[]{:S(2)}) collective-permute-start(f32[48,640]{1,0:T(8,128)S(1)} %get-tuple-element.30), channel_id=1, source_target_pairs={{0,0},{1,2},{2,1},{3,3},{4,4},{5,6},{6,5},{7,7},{8,8},{9,10},{10,9... | collective-permute-start | bytes 368648 | tf_op jit(solution)/shard_map/ppermute | solution.py:216
  14.2 0.9 %copy-start.6 = (f32[7,7,7,80]{3,2,1,0:T(8,128)S(1)}, f32[7,7,7,80]{3,2,1,0:T(8,128)}, u32[]{:S(2)}) copy-start(f32[7,7,7,80]{3,2,1,0:T(8,128)} %stencils_ref.3) | copy-start | bytes 329284
  18.3 4.3 %copy-start = (f32[7,640,640]{2,1,0:T(8,128)S(1)}, f32[7,640,640]{2,1,0:T(8,128)}, u32[]{:S(2)}) copy-start(f32[7,640,640]{2,1,0:T(8,128)} %mixing_ref.5) | copy-start | bytes 34406404
  22.5 4.8 %copy-start.1 = (f32[7,640,640]{2,1,0:T(8,128)S(1)}, f32[7,640,640]{2,1,0:T(8,128)}, u32[]{:S(2)}) copy-start(f32[7,640,640]{2,1,0:T(8,128)} %mixing_ref.5) | copy-start | bytes 34406404
  27.3 4.4 %copy-start.5 = (f32[20,8,320]{2,1,0:T(8,128)S(1)}, f32[20,8,320]{2,1,0:T(8,128)}, u32[]{:S(2)}) copy-start(f32[20,8,320]{2,1,0:T(8,128)} %param.5) | copy-start | bytes 614404
  31.1 16.8 %collective-permute-start.4 = (f32[160,384]{1,0:T(8,128)S(1)}, f32[160,384]{1,0:T(8,128)S(1)}, u32[]{:S(2)}, u32[]{:S(2)}) collective-permute-start(f32[160,384]{1,0:T(8,128)S(1)} %get-tuple-element.35.own_ref.own2_ref), channel_id=1, source_target_pairs={{0,16},{16,0},{1,17},{17,1},{2,18},{18,2},{3,19},{19,3},{4,20},{20... | collective-permute-start | bytes 737288 | tf_op jit(solution)/shard_map/ppermute | solution.py:406
  31.7 13.6 %collective-permute-start.5 = (f32[160,320]{1,0:T(8,128)S(1)}, f32[160,320]{1,0:T(8,128)S(1)}, u32[]{:S(2)}, u32[]{:S(2)}) collective-permute-start(f32[160,320]{1,0:T(8,128)S(1)} %bitcast.13), channel_id=1, source_target_pairs={{0,16},{16,0},{1,17},{17,1},{2,18},{18,2},{3,19},{19,3},{4,20},{20... | collective-permute-start | bytes 614408 | tf_op jit(solution)/shard_map/ppermute | solution.py:382
  33.2 14.6 %collective-permute-start.6 = (f32[160,256]{1,0:T(8,128)S(1)}, f32[160,256]{1,0:T(8,128)S(1)}, u32[]{:S(2)}, u32[]{:S(2)}) collective-permute-start(f32[160,256]{1,0:T(8,128)S(1)} %get-tuple-element.37.own_ref.own1_ref), channel_id=1, source_target_pairs={{0,16},{16,0},{1,17},{17,1},{2,18},{18,2},{3,19},{19,3},{4,20},{20... | collective-permute-start | bytes 491528 | tf_op jit(solution)/shard_map/ppermute | solution.py:399
  48.2 5.0 %collective-permute-start.7 = (f32[60,640]{1,0:T(8,128)S(1)}, f32[60,640]{1,0:T(8,128)S(1)}, u32[]{:S(2)}, u32[]{:S(2)}) collective-permute-start(f32[60,640]{1,0:T(8,128)S(1)} %get-tuple-element.41), channel_id=1, source_target_pairs={{0,4},{4,8},{8,12},{12,0},{1,5},{5,9},{9,13},{13,1},{2,6},{6,10},{... | collective-permute-start | bytes 460808 | tf_op jit(solution)/shard_map/ppermute | solution.py:205
  48.3 5.2 %collective-permute-start.8 = (f32[60,640]{1,0:T(8,128)S(1)}, f32[60,640]{1,0:T(8,128)S(1)}, u32[]{:S(2)}, u32[]{:S(2)}) collective-permute-start(f32[60,640]{1,0:T(8,128)S(1)} %get-tuple-element.42), channel_id=1, source_target_pairs={{4,0},{8,4},{12,8},{0,12},{5,1},{9,5},{13,9},{1,13},{6,2},{10,6},{... | collective-permute-start | bytes 460808 | tf_op jit(solution)/shard_map/ppermute | solution.py:205
  54.2 8.0 %collective-permute-start.10 = (f32[48,640]{1,0:T(8,128)S(1)}, f32[48,640]{1,0:T(8,128)S(1)}, u32[]{:S(2)}, u32[]{:S(2)}) collective-permute-start(f32[48,640]{1,0:T(8,128)S(1)} %get-tuple-element.45), channel_id=1, source_target_pairs={{0,0},{1,2},{2,1},{3,3},{4,4},{5,6},{6,5},{7,7},{8,8},{9,10},{10,9... | collective-permute-start | bytes 368648 | tf_op jit(solution)/shard_map/ppermute | solution.py:216
  57.6 6.1 %collective-permute-start.9 = (f32[48,640]{1,0:T(8,128)S(1)}, f32[48,640]{1,0:T(8,128)S(1)}, u32[]{:S(2)}, u32[]{:S(2)}) collective-permute-start(f32[48,640]{1,0:T(8,128)S(1)} %get-tuple-element.44), channel_id=1, source_target_pairs={{0,1},{1,0},{2,3},{3,2},{4,5},{5,4},{6,7},{7,6},{8,9},{9,8},{10,11... | collective-permute-start | bytes 368648 | tf_op jit(solution)/shard_map/ppermute | solution.py:216
where the time goes:
time: 74.1 us; the launch traced here: 72.6 us
  Pallas kernels  25.1 us (34%)
  waiting for transfers between devices  24.6 us (33%)
  starting transfers between devices  14.9 us (20%)
  local copies, waits for them, and re-layouts  7.28 us (10%)
  between operations  0.8 us (1%)
    pallas_call x12, Pallas kernels, call(): pl.pallas_call(body, out_shape=out_shape, in_specs=specs or [VMEM] * len(...  25.1 us
    ppermute x1, waiting for transfers between devices, local(): theirs = lax.ppermute(mine, 'ens', [(0, 1), (1, 0)])  11.5 us
    ppermute x4, starting transfers between devices, one(): return lax.ppermute(piece, 'lat', sorted(table.items()))  8.67 us
    ppermute x4, waiting for transfers between devices, ring(): return (lax.ppermute(up, 'lon', there), lax.ppermute(down, 'lon', back))  7.22 us
    unnamed x14, local copies, waits for them, and re-layouts  7.19 us
    ppermute x4, waiting for transfers between devices, one(): return lax.ppermute(piece, 'lat', sorted(table.items()))  4 us
    ppermute x4, starting transfers between devices, ring(): return (lax.ppermute(up, 'lon', there), lax.ppermute(down, 'lon', back))  3.58 us
    ppermute x1, waiting for transfers between devices, local(): other1 = lax.ppermute(predicted1, 'ens', [(0, 1), (1, 0)])  1.85 us
  transfers between devices with their start and end apart: 11, of which 9 were waited for; matrix products, arithmetic and copies ran while one was open for 0% of the time, Pallas kernels for 8%

commit v1 on v0

--- a/solution.py
+++ b/solution.py
@@ -7,10 +7,12 @@
 from jax.experimental.pallas import tpu as pltpu
 from jax.sharding import PartitionSpec as P
 
+
 SMOOTH = 0.01
 SLOTS = 16
 DEPTH = 256
 EDGE = 256
+SWAP = [(0, 1), (1, 0)]
 VMEM = pl.BlockSpec(memory_space=pltpu.VMEM)
 SMEM = pl.BlockSpec(memory_space=pltpu.SMEM)
 
@@ -41,7 +43,7 @@
     return both[:rows] + both[rows:] + product(left_high, right_low, axis)
 
 
-def call(body, name, out_shape, operands, specs=None, scratch=(), flops=0, size=0, limit=24):
+def call(body, out_shape, operands, specs=None, scratch=(), flops=0, size=0, limit=12):
     return pl.pallas_call(
         body,
         out_shape=out_shape,
@@ -50,7 +52,6 @@
         scratch_shapes=scratch,
         cost_estimate=pl.CostEstimate(flops=flops, bytes_accessed=size, transcendentals=0),
         compiler_params=pltpu.CompilerParams(vmem_limit_bytes=limit << 20),
-        name=name,
     )(*operands)
 
 
@@ -136,11 +137,10 @@
 
 
 def bands(place, stencils, rows, blocks, breadth, forward):
-    bases, span, _, total = stencils.shape
+    bases, _, _, total = stencils.shape
     lines = bases * rows * breadth
     return call(
         functools.partial(band_kernel, rows=rows, forward=forward),
-        "band_forward" if forward else "band_backward",
         [b16(blocks, lines, DEPTH)] * 2,
         [place, stencils],
         [SMEM, VMEM],
@@ -161,11 +161,16 @@
         down_ref[at, :] = field_ref[row * breadth : row * breadth + margin, :]
 
 
+def keep_sides(field_ref, up_ref, down_ref, kept_ref, *, breadth):
+    pack_sides(field_ref, up_ref, down_ref, breadth)
+    kept_ref[...] = field_ref[...]
+
+
 def sides(flat, breadth, margin):
     shape = f32(flat.shape[0] // breadth * margin, flat.shape[1])
     return call(
-        functools.partial(pack_sides, breadth=breadth), "sides", [shape] * 2, [flat],
-        size=1 << 20, limit=8,
+        functools.partial(keep_sides, breadth=breadth), [shape, shape, f32(*flat.shape)],
+        [flat], size=1 << 20, limit=8,
     )
 
 
@@ -192,7 +197,7 @@
     height = cells // breadth
     edge = f32(left.shape[0] // height * SLOTS, channels)
     return call(
-        functools.partial(assemble_kernel, breadth=breadth), "assemble",
+        functools.partial(assemble_kernel, breadth=breadth),
         [f32(height * SLOTS, channels), edge, edge],
         [place, flat, left, right], [SMEM, VMEM, VMEM, VMEM], size=2 << 20, limit=8,
     )
@@ -215,7 +220,7 @@
                 table[low], table[low + 1] = low + 1, low
         return lax.ppermute(piece, "lat", sorted(table.items()))
 
-    return one(first, range(0, count, 2)), one(second, range(1, count, 2))
+    return (one(first, range(0, count, 2)), one(second, range(1, count, 2)))
 
 
 def stencil(place_ref, wide_ref, first_ref, second_ref, bhigh_ref, blow_ref, shigh_ref, slow_ref, xhigh_ref, xlow_ref):
@@ -242,41 +247,59 @@
         slow_ref[:, here, :] = low.reshape(bases, cells, channels)
 
 
-def contract(shigh_ref, slow_ref, mixing_ref, acc_ref, lanes, axis):
-    acc_ref[...] = jnp.zeros_like(acc_ref)
-
-    def step(base, _):
-        weight_high, weight_low = split(mixing_ref[base, :, lanes])
-        acc_ref[...] += product3(shigh_ref[base], slow_ref[base], weight_high, weight_low, axis)
-
-    lax.fori_loop(0, mixing_ref.shape[0], step, None)
-
-
-def forward_first(place_ref, wide_ref, first_ref, second_ref, bhigh_ref, blow_ref, mixing_ref, field_ref,
-                  predicted_ref, bounded_ref, shigh_ref, slow_ref, xhigh_ref, xlow_ref, acc_ref):
-    stencil(place_ref, wide_ref, first_ref, second_ref, bhigh_ref, blow_ref, shigh_ref, slow_ref, xhigh_ref, xlow_ref)
-    lanes = slice(0, acc_ref.shape[1])
-    contract(shigh_ref, slow_ref, mixing_ref, acc_ref, lanes, 0)
-    bounded = jnp.tanh(acc_ref[...])
+def load_mixing(place_ref, mixing_ref, high_ref, low_ref, wide_ref, sem_ref):
+    bases, slots = mixing_ref.shape[0], wide_ref.shape[0]
+
+    def copy(base):
+        slot = base % slots
+        return pltpu.make_async_copy(mixing_ref.at[base], wide_ref.at[slot], sem_ref.at[slot])
+
+    for base in range(min(slots, bases)):
+        copy(base).start()
+    for base in range(bases):
+        copy(base).wait()
+        high_ref[base], low_ref[base] = split(wide_ref[base % slots])
+        if base + slots < bases:
+            copy(base + slots).start()
+
+
+def contract(shigh_ref, slow_ref, mhigh_ref, mlow_ref, lanes, axis):
+    total = None
+    for base in range(mhigh_ref.shape[0]):
+        part = product3(
+            shigh_ref[base], slow_ref[base], mhigh_ref[base, :, lanes], mlow_ref[base, :, lanes], axis
+        )
+        total = part if total is None else total + part
+    return total
+
+
+def finish(total, field_ref, lanes, predicted_ref, bounded_ref):
+    bounded = jnp.tanh(total)
     bounded_ref[...] = bounded
     predicted_ref[...] = field_ref[:, lanes] + bounded
 
 
-def forward_rest(shigh_ref, slow_ref, mixing_ref, field_ref, predicted_ref, bounded_ref, acc_ref):
-    lanes = slice(field_ref.shape[1] - acc_ref.shape[1], field_ref.shape[1])
-    contract(shigh_ref, slow_ref, mixing_ref, acc_ref, lanes, 0)
-    bounded = jnp.tanh(acc_ref[...])
-    bounded_ref[...] = bounded
-    predicted_ref[...] = field_ref[:, lanes] + bounded
-
-
-def backward_all(place_ref, wide_ref, first_ref, second_ref, bhigh_ref, blow_ref, mixing_ref, grad_ref, tail_ref,
-                 out_ref, shigh_ref, slow_ref, xhigh_ref, xlow_ref, acc_ref):
+def forward_first(place_ref, wide_ref, first_ref, second_ref, bhigh_ref, blow_ref, mhigh_ref, mlow_ref, field_ref,
+                  predicted_ref, bounded_ref, shigh_ref, slow_ref, xhigh_ref, xlow_ref):
     stencil(place_ref, wide_ref, first_ref, second_ref, bhigh_ref, blow_ref, shigh_ref, slow_ref, xhigh_ref, xlow_ref)
-    contract(shigh_ref, slow_ref, mixing_ref, acc_ref, slice(None), 1)
+    lanes = slice(0, predicted_ref.shape[1])
+    total = contract(shigh_ref, slow_ref, mhigh_ref, mlow_ref, lanes, 0)
+    finish(total, field_ref, lanes, predicted_ref, bounded_ref)
+
+
+def forward_rest(shigh_ref, slow_ref, mhigh_ref, mlow_ref, field_ref, predicted_ref, bounded_ref):
+    lanes = slice(field_ref.shape[1] - predicted_ref.shape[1], field_ref.shape[1])
+    total = contract(shigh_ref, slow_ref, mhigh_ref, mlow_ref, lanes, 0)
+    finish(total, field_ref, lanes, predicted_ref, bounded_ref)
+
+
+def backward_all(place_ref, wide_ref, first_ref, second_ref, bhigh_ref, blow_ref, mhigh_ref, mlow_ref, grad_ref, tail_ref,
+                 out_ref, shigh_ref, slow_ref, xhigh_ref, xlow_ref):
+    stencil(place_ref, wide_ref, first_ref, second_ref, bhigh_ref, blow_ref, shigh_ref, slow_ref, xhigh_ref, xlow_ref)
+    total = contract(shigh_ref, slow_ref, mhigh_ref, mlow_ref, slice(None), 1)
     edge = grad_ref.shape[1]
-    out_ref[:, :edge] = acc_ref[:, :edge] + grad_ref[...]
-    out_ref[:, edge:] = acc_ref[:, edge:] + tail_ref[...]
+    out_ref[:, :edge] = total[:, :edge] + grad_ref[...]
+    out_ref[:, edge:] = total[:, edge:] + tail_ref[...]
 
 
 def slope(value):
@@ -377,9 +400,17 @@
         lax.axis_index("lat") * height, odd, (1 - odd) * end, odd * end, lax.axis_index("ens")
     ]).astype(jnp.int32)
 
-    left, right = ring(*sides(flat, breadth, margin))
+    up, down, flat = sides(flat, breadth, margin)
+    left, right = ring(up, down)
+    weights = call(
+        load_mixing, [b16(*mixing.shape)] * 2,
+        [place, pltpu.with_memory_space_constraint(mixing, pltpu.HBM)],
+        [SMEM, pl.BlockSpec(memory_space=pltpu.HBM)],
+        [pltpu.VMEM((4, *mixing.shape[1:]), jnp.float32), pltpu.SemaphoreType.DMA((4,))],
+        size=2 * mixing.size * 4, limit=8,
+    )
     if pair:
-        theirs = lax.ppermute(mine, "ens", [(0, 1), (1, 0)])
+        theirs = lax.ppermute(mine, "ens", SWAP)
     band = bands(place, stencils, rows, blocks, breadth, True)
     wide, first, second = assemble(place, flat, left, right, breadth)
     first, second = swap(first, second)
@@ -390,36 +421,36 @@
     mix_flops = 6 * cells * bases * channels * channels
     rest = channels - EDGE
     predicted1, bounded1, shigh, slow = call(
-        forward_first, "forward_first", [f32(cells, EDGE)] * 2 + taps,
-        [place, wide, first, second, *band, mixing, flat], [SMEM] + [VMEM] * 7,
-        [window, window, pltpu.VMEM((cells, EDGE), jnp.float32)],
+        forward_first, [f32(cells, EDGE)] * 2 + taps,
+        [place, wide, first, second, *band, *weights, flat], [SMEM] + [VMEM] * 8,
+        [window, window],
         flops=stencil_flops + mix_flops * EDGE // channels,
     )
     if pair:
-        other1 = lax.ppermute(predicted1, "ens", [(0, 1), (1, 0)])
+        other1 = lax.ppermute(predicted1, "ens", SWAP)
     predicted2, bounded2 = call(
-        forward_rest, "forward_rest", [f32(cells, rest)] * 2, [shigh, slow, mixing, flat],
-        scratch=[pltpu.VMEM((cells, rest), jnp.float32)], flops=mix_flops * rest // channels,
+        forward_rest, [f32(cells, rest)] * 2, [shigh, slow, *weights, flat],
+        flops=mix_flops * rest // channels,
     )
     back = bands(place, stencils, rows, blocks, breadth, False)
     if pair:
-        other2 = lax.ppermute(predicted2, "ens", [(0, 1), (1, 0)])
+        other2 = lax.ppermute(predicted2, "ens", SWAP)
         (known,) = call(
-            whole_analysis, "whole_analysis", [f32(cells, channels)], [place, mine, theirs],
+            whole_analysis, [f32(cells, channels)], [place, mine, theirs],
             [SMEM, VMEM, VMEM], size=1 << 20, limit=8,
         )
         grad1, inner1 = call(
-            loss_first, "loss_first", [f32(cells, EDGE)] * 2,
+            loss_first, [f32(cells, EDGE)] * 2,
             [predicted1, other1, bounded1, known], size=1 << 20, limit=8,
         )
         side = f32(height * margin, channels)
         grad2, inner, up, down = call(
-            functools.partial(loss_rest, breadth=breadth), "loss_rest",
+            functools.partial(loss_rest, breadth=breadth),
             [f32(cells, rest), f32(cells, channels), side, side],
             [predicted2, other2, bounded2, known, inner1], size=2 << 20, limit=8,
         )
         (crps,) = call(
-            crps_kernel, "crps", [f32(*mine.shape)],
+            crps_kernel, [f32(*mine.shape)],
             [place, predicted1, predicted2, other1, other2, mine], [SMEM] + [VMEM] * 5,
             size=1 << 20, limit=8,
         )
@@ -428,16 +459,16 @@
         bounded = jnp.concatenate([bounded1, bounded2], 1)
         grad, inner, crps = loss_many(predicted, bounded, mine)
         grad1, grad2 = grad[:, :EDGE], grad[:, EDGE:]
-        up, down = sides(inner, breadth, margin)
+        up, down, _ = sides(inner, breadth, margin)
 
     left, right = ring(up, down)
     wide, first, second = assemble(place, inner, left, right, breadth)
     first, second = swap(first, second)
     (result,) = call(
-        backward_all, "backward_all", [f32(cells, channels)],
-        [place, wide, first, second, *back, mixing, grad1, grad2], [SMEM] + [VMEM] * 8,
+        backward_all, [f32(cells, channels)],
+        [place, wide, first, second, *back, *weights, grad1, grad2], [SMEM] + [VMEM] * 9,
         [pltpu.VMEM(s.shape, s.dtype) for s in taps]
-        + [window, window, pltpu.VMEM((cells, channels), jnp.float32)],
+        + [window, window],
         flops=stencil_flops + mix_flops,
     )
     return result.reshape(members.shape), crps.reshape(analysis.shape)

time: 74.1 us -> 69.6 us (0.939)
  the two profiles are of different devices: /device:TPU:10 before, /device:TPU:0 now
where the time goes in v1:
time: 69.6 us; the launch traced here: 69.4 us
  Pallas kernels  29 us (42%)
  waiting for transfers between devices  21.8 us (31%)
  starting transfers between devices  16.7 us (24%)
  local copies, waits for them, and re-layouts  1.09 us (2%)
  between operations  0.79 us (1%)
    pallas_call x13, Pallas kernels, call(): pl.pallas_call(body, out_shape=out_shape, in_specs=specs or [VMEM] * len(...  29 us
    ppermute x1, waiting for transfers between devices, local(): theirs = lax.ppermute(mine, 'ens', SWAP)  10.6 us
    ppermute x4, starting transfers between devices, one(): return lax.ppermute(piece, 'lat', sorted(table.items()))  8.81 us
    ppermute x4, waiting for transfers between devices, ring(): return (lax.ppermute(up, 'lon', there), lax.ppermute(down, 'lon', back))  8.16 us
    ppermute x4, starting transfers between devices, ring(): return (lax.ppermute(up, 'lon', there), lax.ppermute(down, 'lon', back))  4.34 us
    ppermute x1, waiting for transfers between devices, local(): other1 = lax.ppermute(predicted1, 'ens', SWAP)  2.43 us
    ppermute x1, starting transfers between devices, local(): other2 = lax.ppermute(predicted2, 'ens', SWAP)  1.55 us
    ppermute x1, starting transfers between devices, local(): other1 = lax.ppermute(predicted1, 'ens', SWAP)  1.49 us
  transfers between devices with their start and end apart: 11, of which 7 were waited for; matrix products, arithmetic and copies ran while one was open for 0% of the time, Pallas kernels for 16%

profile of v1, /device:TPU:0, one launch (start us, length us, event | category | flops | bytes accessed | tf_op | source)
XLA Modules:
  0.0 69.4 jit_solution(14220152482735025478)
XLA Ops:
  0.6 0.0 copy-start.1
  0.6 1.0 %copy-done.1 = f32[1,20,8,640]{3,2,1,0:T(8,128)S(1)} copy-done((f32[1,20,8,640]{3,2,1,0:T(8,128)S(1)}, f32[1,20,8,640]{3,2,1,0:T(8,128)}, u32[]{:S(2)}) %copy-start.1) | copy-done | bytes 409624
  1.6 0.1 shard_map.59
  1.8 0.5 collective-permute-start
  2.3 2.0 %collective-permute-start.1 = (f32[60,640]{1,0:T(8,128)S(1)}, f32[60,640]{1,0:T(8,128)S(1)}, u32[]{:S(2)}, u32[]{:S(2)}) collective-permute-start(f32[60,640]{1,0:T(8,128)S(1)} %get-tuple-element.31), channel_id=1, source_target_pairs={{4,0},{8,4},{12,8},{0,12},{5,1},{9,5},{13,9},{1,13},{6,2},{10,6},{... | collective-permute-start | bytes 460808 | tf_op jit(solution)/shard_map/ppermute | solution.py:210
  4.3 0.1 stack.23.place_ref
  4.4 2.9 %collective-permute-done.left_ref = f32[60,640]{1,0:T(8,128)S(1)} collective-permute-done((f32[60,640]{1,0:T(8,128)S(1)}, f32[60,640]{1,0:T(8,128)S(1)}, u32[]{:S(2)}, u32[]{:S(2)}) %collective-permute-start) | collective-permute-done | bytes 153632 | tf_op jit(solution)/shard_map/ppermute | solution.py:210
  7.2 1.6 %collective-permute-done.1.right_ref = f32[60,640]{1,0:T(8,128)S(1)} collective-permute-done((f32[60,640]{1,0:T(8,128)S(1)}, f32[60,640]{1,0:T(8,128)S(1)}, u32[]{:S(2)}, u32[]{:S(2)}) %collective-permute-start.1) | collective-permute-done | bytes 153632 | tf_op jit(solution)/shard_map/ppermute | solution.py:210
  8.8 0.7 shard_map.60
  9.5 1.6 %collective-permute-start.2 = (f32[48,640]{1,0:T(8,128)S(1)}, f32[48,640]{1,0:T(8,128)S(1)}, u32[]{:S(2)}, u32[]{:S(2)}) collective-permute-start(f32[48,640]{1,0:T(8,128)S(1)} %get-tuple-element.33), channel_id=1, source_target_pairs={{0,1},{1,0},{2,3},{3,2},{4,5},{5,4},{6,7},{7,6},{8,9},{9,8},{10,11... | collective-permute-start | bytes 368648 | tf_op jit(solution)/shard_map/ppermute | solution.py:221
  11.1 0.0 copy-start.2
  11.1 0.8 %collective-permute-start.3 = (f32[48,640]{1,0:T(8,128)S(1)}, f32[48,640]{1,0:T(8,128)S(1)}, u32[]{:S(2)}, u32[]{:S(2)}) collective-permute-start(f32[48,640]{1,0:T(8,128)S(1)} %get-tuple-element.34), channel_id=1, source_target_pairs={{0,0},{1,2},{2,1},{3,3},{4,4},{5,6},{6,5},{7,7},{8,8},{9,10},{10,9... | collective-permute-start | bytes 368648 | tf_op jit(solution)/shard_map/ppermute | solution.py:221
  11.9 5.3 %shard_map.62 = (bf16[7,640,640]{2,1,0:T(8,128)(2,1)S(1)}, bf16[7,640,640]{2,1,0:T(8,128)(2,1)S(1)}) custom-call(s32[5]{0:T(128)S(1)} %stack.23.place_ref, f32[7,640,640]{2,1,0:T(8,128)} %mixing_ref.1), custom_call_target="tpu_custom_call" | custom-call | bytes 22937600 | tf_op jit(solution)/shard_map/pallas_call | solution.py:47
  17.2 0.0 copy-done.2
  17.2 1.6 %shard_map.61 = (bf16[2,560,256]{2,1,0:T(8,128)(2,1)S(1)}, bf16[2,560,256]{2,1,0:T(8,128)(2,1)S(1)}) custom-call(s32[5]{0:T(128)S(1)} %stack.23.place_ref, f32[7,7,7,80]{3,2,1,0:T(8,128)S(1)} %copy-done.2), custom_call_target="tpu_custom_call" | custom-call | flops 1000000000 | bytes 4194304 | tf_op jit(solution)/shard_map/pallas_call | solution.py:47
  18.8 0.0 collective-permute-done.2.first_ref
  18.9 0.0 collective-permute-done.3.second_ref
  18.9 6.0 %shard_map.63 = (f32[160,256]{1,0:T(8,128)S(1)}, f32[160,256]{1,0:T(8,128)S(1)}, bf16[7,160,640]{2,1,0:T(8,128)(2,1)S(1)}, bf16[7,160,640]{2,1,0:T(8,128)(2,1)S(1)}) custom-call(s32[5]{0:T(128)S(1)} %stack.23.place_ref, f32[320,640]{1,0:T(8,128)S(1)} %get-tuple-element.32.wide_ref, f32[48,640]{1,0:T(8,128)S(1)} %collective-permute-done.2.first_ref, ...), custom_call_target="tpu_custom_call" | custom-call | flops 2202009600 | tf_op jit(solution)/shard_map/pallas_call | solution.py:47
  24.9 0.0 copy-start
  24.9 2.7 %shard_map.64 = (f32[160,384]{1,0:T(8,128)S(1)}, f32[160,384]{1,0:T(8,128)S(1)}) custom-call(bf16[7,160,640]{2,1,0:T(8,128)(2,1)S(1)} %get-tuple-element.39.shigh_ref, bf16[7,160,640]{2,1,0:T(8,128)(2,1)S(1)} %get-tuple-element.40.slow_ref, bf16[7,640,640]{2,1,0:T(8,128)(2,1)S(1)} %get-tuple-element.37.mhigh_ref, ...), custom_call_target="tpu_custom_call" | custom-call | flops 1651507200 | tf_op jit(solution)/shard_map/pallas_call | solution.py:47
  27.6 1.6 %collective-permute-start.4 = (f32[160,384]{1,0:T(8,128)S(1)}, f32[160,384]{1,0:T(8,128)S(1)}, u32[]{:S(2)}, u32[]{:S(2)}) collective-permute-start(f32[160,384]{1,0:T(8,128)S(1)} %get-tuple-element.41.own_ref.own2_ref), channel_id=1, source_target_pairs={{0,16},{16,0},{1,17},{17,1},{2,18},{18,2},{3,19},{19,3},{4,20},{20... | collective-permute-start | bytes 737288 | tf_op jit(solution)/shard_map/ppermute | solution.py:437
  29.2 0.0 copy-done
  29.2 0.5 collective-permute-start.5
  29.7 1.5 %collective-permute-start.6 = (f32[160,256]{1,0:T(8,128)S(1)}, f32[160,256]{1,0:T(8,128)S(1)}, u32[]{:S(2)}, u32[]{:S(2)}) collective-permute-start(f32[160,256]{1,0:T(8,128)S(1)} %get-tuple-element.43.own_ref.own1_ref), channel_id=1, source_target_pairs={{0,16},{16,0},{1,17},{17,1},{2,18},{18,2},{3,19},{19,3},{4,20},{20... | collective-permute-start | bytes 491528 | tf_op jit(solution)/shard_map/ppermute | solution.py:430
  31.2 10.6 %collective-permute-done.5.theirs_ref = f32[160,320]{1,0:T(8,128)S(1)} collective-permute-done((f32[160,320]{1,0:T(8,128)S(1)}, f32[160,320]{1,0:T(8,128)S(1)}, u32[]{:S(2)}, u32[]{:S(2)}) %collective-permute-start.5) | collective-permute-done | bytes 204832 | tf_op jit(solution)/shard_map/ppermute | solution.py:413
  41.8 0.7 shard_map.65.analysis_ref
  42.5 2.4 %collective-permute-done.6.other_ref.other1_ref = f32[160,256]{1,0:T(8,128)S(1)} collective-permute-done((f32[160,256]{1,0:T(8,128)S(1)}, f32[160,256]{1,0:T(8,128)S(1)}, u32[]{:S(2)}, u32[]{:S(2)}) %collective-permute-start.6) | collective-permute-done | bytes 163872 | tf_op jit(solution)/shard_map/ppermute | solution.py:430
  44.9 0.1 shard_map.66
  45.0 0.0 collective-permute-done.4.other_ref.other2_ref
  45.0 0.3 shard_map.67
  45.3 0.1 collective-permute-start.7
  45.4 1.7 %collective-permute-start.8 = (f32[60,640]{1,0:T(8,128)S(1)}, f32[60,640]{1,0:T(8,128)S(1)}, u32[]{:S(2)}, u32[]{:S(2)}) collective-permute-start(f32[60,640]{1,0:T(8,128)S(1)} %get-tuple-element.48), channel_id=1, source_target_pairs={{4,0},{8,4},{12,8},{0,12},{5,1},{9,5},{13,9},{1,13},{6,2},{10,6},{... | collective-permute-start | bytes 460808 | tf_op jit(solution)/shard_map/ppermute | solution.py:210
  47.1 3.0 %collective-permute-done.7.left_ref = f32[60,640]{1,0:T(8,128)S(1)} collective-permute-done((f32[60,640]{1,0:T(8,128)S(1)}, f32[60,640]{1,0:T(8,128)S(1)}, u32[]{:S(2)}, u32[]{:S(2)}) %collective-permute-start.7) | collective-permute-done | bytes 153632 | tf_op jit(solution)/shard_map/ppermute | solution.py:210
  50.1 0.7 %collective-permute-done.8.right_ref = f32[60,640]{1,0:T(8,128)S(1)} collective-permute-done((f32[60,640]{1,0:T(8,128)S(1)}, f32[60,640]{1,0:T(8,128)S(1)}, u32[]{:S(2)}, u32[]{:S(2)}) %collective-permute-start.8) | collective-permute-done | bytes 153632 | tf_op jit(solution)/shard_map/ppermute | solution.py:210
  50.8 0.7 shard_map.68
  51.5 0.7 collective-permute-start.10
  52.2 5.7 %collective-permute-start.9 = (f32[48,640]{1,0:T(8,128)S(1)}, f32[48,640]{1,0:T(8,128)S(1)}, u32[]{:S(2)}, u32[]{:S(2)}) collective-permute-start(f32[48,640]{1,0:T(8,128)S(1)} %get-tuple-element.50), channel_id=1, source_target_pairs={{0,1},{1,0},{2,3},{3,2},{4,5},{5,4},{6,7},{7,6},{8,9},{9,8},{10,11... | collective-permute-start | bytes 368648 | tf_op jit(solution)/shard_map/ppermute | solution.py:221
  57.9 1.7 %shard_map.69 = (bf16[2,560,256]{2,1,0:T(8,128)(2,1)S(1)}, bf16[2,560,256]{2,1,0:T(8,128)(2,1)S(1)}) custom-call(s32[5]{0:T(128)S(1)} %stack.23.place_ref, f32[7,7,7,80]{3,2,1,0:T(8,128)S(1)} %copy-done.2), custom_call_target="tpu_custom_call" | custom-call | flops 1000000000 | bytes 4194304 | tf_op jit(solution)/shard_map/pallas_call | solution.py:47
  59.6 1.7 %shard_map.71 = f32[160,320]{1,0:T(8,128)} custom-call(s32[5]{0:T(128)S(1)} %stack.23.place_ref, f32[160,256]{1,0:T(8,128)S(1)} %get-tuple-element.43.own_ref.own1_ref, f32[160,384]{1,0:T(8,128)S(1)} %get-tuple-element.41.own_ref.own2_ref, f32[160,256]{1,0:T(8,128)S(1)} %collective-permute-done.6.other_ref.other1_ref, ...), custom_call_target="tpu_custom_call" | custom-call | bytes 1048576 | tf_op jit(solution)/shard_map/pallas_call | solution.py:47
  61.3 0.0 collective-permute-done.10.second_ref
  61.3 0.7 collective-permute-done.9.first_ref
  61.9 7.5 %shard_map.70 = f32[160,640]{1,0:T(8,128)} custom-call(s32[5]{0:T(128)S(1)} %stack.23.place_ref, f32[320,640]{1,0:T(8,128)S(1)} %get-tuple-element.49.wide_ref, f32[48,640]{1,0:T(8,128)S(1)} %collective-permute-done.9.first_ref, f32[48,640]{1,0:T(8,128)S(1)} %collective-permute-done.10.second_ref, bf16[2,560,256]{2,1,0:T(8,128)(2,1)S(1)} %get-tuple-element.52.bhigh_ref, ...), custom_call_target="tpu_custom_call" | custom-call | flops 3853516800 | tf_op jit(solution)/shard_map/pallas_call | solution.py:47
Async XLA Ops:
  0.6 1.0 %copy-start.1 = (f32[1,20,8,640]{3,2,1,0:T(8,128)S(1)}, f32[1,20,8,640]{3,2,1,0:T(8,128)}, u32[]{:S(2)}) copy-start(f32[1,20,8,640]{3,2,1,0:T(8,128)} %param.4) | copy-start | bytes 1228804
  1.8 5.5 %collective-permute-start = (f32[60,640]{1,0:T(8,128)S(1)}, f32[60,640]{1,0:T(8,128)S(1)}, u32[]{:S(2)}, u32[]{:S(2)}) collective-permute-start(f32[60,640]{1,0:T(8,128)S(1)} %get-tuple-element.30), channel_id=1, source_target_pairs={{0,4},{4,8},{8,12},{12,0},{1,5},{5,9},{9,13},{13,1},{2,6},{6,10},{... | collective-permute-start | bytes 460808 | tf_op jit(solution)/shard_map/ppermute | solution.py:210
  2.3 6.5 %collective-permute-start.1 = (f32[60,640]{1,0:T(8,128)S(1)}, f32[60,640]{1,0:T(8,128)S(1)}, u32[]{:S(2)}, u32[]{:S(2)}) collective-permute-start(f32[60,640]{1,0:T(8,128)S(1)} %get-tuple-element.31), channel_id=1, source_target_pairs={{4,0},{8,4},{12,8},{0,12},{5,1},{9,5},{13,9},{1,13},{6,2},{10,6},{... | collective-permute-start | bytes 460808 | tf_op jit(solution)/shard_map/ppermute | solution.py:210
  9.5 9.4 %collective-permute-start.2 = (f32[48,640]{1,0:T(8,128)S(1)}, f32[48,640]{1,0:T(8,128)S(1)}, u32[]{:S(2)}, u32[]{:S(2)}) collective-permute-start(f32[48,640]{1,0:T(8,128)S(1)} %get-tuple-element.33), channel_id=1, source_target_pairs={{0,1},{1,0},{2,3},{3,2},{4,5},{5,4},{6,7},{7,6},{8,9},{9,8},{10,11... | collective-permute-start | bytes 368648 | tf_op jit(solution)/shard_map/ppermute | solution.py:221
  11.1 6.1 %copy-start.2 = (f32[7,7,7,80]{3,2,1,0:T(8,128)S(1)}, f32[7,7,7,80]{3,2,1,0:T(8,128)}, u32[]{:S(2)}) copy-start(f32[7,7,7,80]{3,2,1,0:T(8,128)} %stencils_ref.3) | copy-start | bytes 329284
  11.1 7.7 %collective-permute-start.3 = (f32[48,640]{1,0:T(8,128)S(1)}, f32[48,640]{1,0:T(8,128)S(1)}, u32[]{:S(2)}, u32[]{:S(2)}) collective-permute-start(f32[48,640]{1,0:T(8,128)S(1)} %get-tuple-element.34), channel_id=1, source_target_pairs={{0,0},{1,2},{2,1},{3,3},{4,4},{5,6},{6,5},{7,7},{8,8},{9,10},{10,9... | collective-permute-start | bytes 368648 | tf_op jit(solution)/shard_map/ppermute | solution.py:221
  24.9 4.3 %copy-start = (f32[20,8,320]{2,1,0:T(8,128)S(1)}, f32[20,8,320]{2,1,0:T(8,128)}, u32[]{:S(2)}) copy-start(f32[20,8,320]{2,1,0:T(8,128)} %param.5) | copy-start | bytes 614404
  27.6 17.4 %collective-permute-start.4 = (f32[160,384]{1,0:T(8,128)S(1)}, f32[160,384]{1,0:T(8,128)S(1)}, u32[]{:S(2)}, u32[]{:S(2)}) collective-permute-start(f32[160,384]{1,0:T(8,128)S(1)} %get-tuple-element.41.own_ref.own2_ref), channel_id=1, source_target_pairs={{0,16},{16,0},{1,17},{17,1},{2,18},{18,2},{3,19},{19,3},{4,20},{20... | collective-permute-start | bytes 737288 | tf_op jit(solution)/shard_map/ppermute | solution.py:437
  29.2 12.6 %collective-permute-start.5 = (f32[160,320]{1,0:T(8,128)S(1)}, f32[160,320]{1,0:T(8,128)S(1)}, u32[]{:S(2)}, u32[]{:S(2)}) collective-permute-start(f32[160,320]{1,0:T(8,128)S(1)} %bitcast.9), channel_id=1, source_target_pairs={{0,16},{16,0},{1,17},{17,1},{2,18},{18,2},{3,19},{19,3},{4,20},{20... | collective-permute-start | bytes 614408 | tf_op jit(solution)/shard_map/ppermute | solution.py:413
  29.7 15.2 %collective-permute-start.6 = (f32[160,256]{1,0:T(8,128)S(1)}, f32[160,256]{1,0:T(8,128)S(1)}, u32[]{:S(2)}, u32[]{:S(2)}) collective-permute-start(f32[160,256]{1,0:T(8,128)S(1)} %get-tuple-element.43.own_ref.own1_ref), channel_id=1, source_target_pairs={{0,16},{16,0},{1,17},{17,1},{2,18},{18,2},{3,19},{19,3},{4,20},{20... | collective-permute-start | bytes 491528 | tf_op jit(solution)/shard_map/ppermute | solution.py:430
  45.3 4.8 %collective-permute-start.7 = (f32[60,640]{1,0:T(8,128)S(1)}, f32[60,640]{1,0:T(8,128)S(1)}, u32[]{:S(2)}, u32[]{:S(2)}) collective-permute-start(f32[60,640]{1,0:T(8,128)S(1)} %get-tuple-element.47), channel_id=1, source_target_pairs={{0,4},{4,8},{8,12},{12,0},{1,5},{5,9},{9,13},{13,1},{2,6},{6,10},{... | collective-permute-start | bytes 460808 | tf_op jit(solution)/shard_map/ppermute | solution.py:210
  45.4 5.5 %collective-permute-start.8 = (f32[60,640]{1,0:T(8,128)S(1)}, f32[60,640]{1,0:T(8,128)S(1)}, u32[]{:S(2)}, u32[]{:S(2)}) collective-permute-start(f32[60,640]{1,0:T(8,128)S(1)} %get-tuple-element.48), channel_id=1, source_target_pairs={{4,0},{8,4},{12,8},{0,12},{5,1},{9,5},{13,9},{1,13},{6,2},{10,6},{... | collective-permute-start | bytes 460808 | tf_op jit(solution)/shard_map/ppermute | solution.py:210
  51.5 9.8 %collective-permute-start.10 = (f32[48,640]{1,0:T(8,128)S(1)}, f32[48,640]{1,0:T(8,128)S(1)}, u32[]{:S(2)}, u32[]{:S(2)}) collective-permute-start(f32[48,640]{1,0:T(8,128)S(1)} %get-tuple-element.51), channel_id=1, source_target_pairs={{0,0},{1,2},{2,1},{3,3},{4,4},{5,6},{6,5},{7,7},{8,8},{9,10},{10,9... | collective-permute-start | bytes 368648 | tf_op jit(solution)/shard_map/ppermute | solution.py:221
  52.2 9.8 %collective-permute-start.9 = (f32[48,640]{1,0:T(8,128)S(1)}, f32[48,640]{1,0:T(8,128)S(1)}, u32[]{:S(2)}, u32[]{:S(2)}) collective-permute-start(f32[48,640]{1,0:T(8,128)S(1)} %get-tuple-element.50), channel_id=1, source_target_pairs={{0,1},{1,0},{2,3},{3,2},{4,5},{5,4},{6,7},{7,6},{8,9},{9,8},{10,11... | collective-permute-start | bytes 368648 | tf_op jit(solution)/shard_map/ppermute | solution.py:221

commit v2 on v1

v2 whole, which is shorter than its diff:
```python
import functools

import jax
import jax.numpy as jnp
from jax import lax
from jax.experimental import pallas as pl
from jax.experimental.pallas import tpu as pltpu
from jax.sharding import PartitionSpec as P


SMOOTH = 0.01
SLOTS = 16
DEPTH = 256
EDGE = 256
SWAP = [(0, 1), (1, 0)]
VMEM = pl.BlockSpec(memory_space=pltpu.VMEM)
SMEM = pl.BlockSpec(memory_space=pltpu.SMEM)


def f32(*shape):
    return jax.ShapeDtypeStruct(shape, jnp.float32)


def b16(*shape):
    return jax.ShapeDtypeStruct(shape, jnp.bfloat16)


def split(value):
    high = value.astype(jnp.bfloat16)
    low = (value - high.astype(jnp.float32)).astype(jnp.bfloat16)
    return high, low


def product(left, right, axis):
    return lax.dot_general(
        left, right, (((1,), (axis,)), ((), ())), preferred_element_type=jnp.float32
    )


def product3(left_high, left_low, right_high, right_low, axis):
    rows = left_high.shape[0]
    both = product(jnp.concatenate([left_high, left_low], 0), right_high, axis)
    return both[:rows] + both[rows:] + product(left_high, right_low, axis)


def call(body, out_shape, operands, specs=None, scratch=(), flops=0, size=0, limit=12):
    return pl.pallas_call(
        body,
        out_shape=out_shape,
        in_specs=specs or [VMEM] * len(operands),
        out_specs=[VMEM] * len(out_shape),
        scratch_shapes=scratch,
        cost_estimate=pl.CostEstimate(flops=flops, bytes_accessed=size, transcendentals=0),
        compiler_params=pltpu.CompilerParams(vmem_limit_bytes=limit << 20),
    )(*operands)


def band_kernel(place_ref, stencils_ref, inner_ref, outer_ref, table_ref, in_ref, out_ref, *, rows, forward):
    bases, span, _, total = stencils_ref.shape
    blocks = inner_ref.shape[0]
    margin = span // 2
    breadth = outer_ref.shape[1] // (2 * bases * margin)
    first_row = place_ref[0]
    iota = lambda shape, axis: lax.broadcasted_iota(jnp.int32, shape, axis)

    table_ref[...] = jnp.zeros_like(table_ref)
    for base in range(bases):
        for tap in range(span):
            at = (base * 8 + tap) * 8
            table_ref[at : at + span, :total] = stencils_ref[base, tap]
    table = split(table_ref[...])

    group = blocks * SLOTS
    shifts = [margin] if forward else list(range(span))
    count = group * len(shifts)
    line, latitude = iota((count, table_ref.shape[1]), 0), iota((count, table_ref.shape[1]), 1)
    local_row = line % SLOTS
    shift = shifts[0] if forward else line // group
    wanted = first_row + (line % group) // SLOTS * rows + local_row + shift - margin
    picks = ((latitude == wanted) & (local_row < rows)).astype(jnp.float32).astype(jnp.bfloat16)

    width = table_ref.shape[0]
    tap_of = iota((group, width), 1) // 8 % 8
    stacked = []
    for part in table:
        picked = product(picks, part, 1)
        if forward:
            line = iota((group, width), 0)
            reach = first_row + line // SLOTS * rows + line % SLOTS + tap_of - margin
            taps = jnp.where((reach >= 0) & (reach < total), picked, 0.0)
        else:
            taps = jnp.zeros((group, width), jnp.float32)
            for tap in range(span):
                here = picked[tap * group : (tap + 1) * group]
                taps = jnp.where(tap_of == span - 1 - tap, here, taps)
        stacked += [taps[:, at : at + 128] for at in range(0, width, 128)]
    left = jnp.concatenate(stacked, 0).astype(jnp.bfloat16)
    pairs = width // 128

    source, target = iota((128, 256), 0), iota((128, 256), 1)
    slot = target % SLOTS
    column = jnp.where(
        slot < breadth,
        slot,
        jnp.where(slot < breadth + margin, slot - breadth - margin, slot - margin),
    )
    row_tap, column_tap = source // 8 % 8, source % 8
    to_row = target % 128 // SLOTS
    if not forward:
        row_tap, column_tap = span - 1 - row_tap, span - 1 - column_tap
    same = (row_tap == to_row) & (source // 64 == target // 128) & (slot < breadth + 2 * margin)
    same = same & (source % 8 < span) & (source // 8 % 8 < span)
    offset = jnp.where(same, column_tap - column, 1000)
    zeros = jnp.zeros((left.shape[0], 128), jnp.float32)
    for j in range(breadth):
        spread = (offset == margin - j).astype(jnp.float32).astype(jnp.bfloat16)
        both = product(left, spread, 0)
        for odd in range(2):
            wide = jnp.concatenate([both[:, odd * 128 : odd * 128 + 128], zeros], 1)
            wide = pltpu.roll(wide, 0, 1, stride=SLOTS, stride_axis=0)
            for part in range(2):
                for pair in range(pairs):
                    base = 2 * pair + odd
                    if base >= bases:
                        continue
                    for block in range(blocks):
                        at = ((part * pairs + pair) * blocks + block) * SLOTS
                        inner = margin if block == 0 else 0
                        outer = 0 if block == 0 else rows - margin
                        for ref, begin, count in (
                            (in_ref, inner, rows - margin), (out_ref, outer, margin),
                        ):
                            lines = pl.ds(base * count * breadth + j, count, stride=breadth)
                            for half in range(2):
                                ref[part, half, block, lines, :] = wide[
                                    at + begin : at + begin + count, half * 128 : half * 128 + 128
                                ]
    for source_ref, ref in ((in_ref, inner_ref), (out_ref, outer_ref)):
        for half in range(2):
            lanes = slice(half * 128, half * 128 + 128)
            both = jnp.concatenate([source_ref[0, half], source_ref[1, half]], 1)
            ref[:, :, lanes] = both.astype(jnp.bfloat16)


def bands(place, stencils, rows, breadth, forward):
    bases, span, _, total = stencils.shape
    margin = span // 2
    inner, outer = bases * (rows - margin) * breadth, bases * margin * breadth
    return call(
        functools.partial(band_kernel, rows=rows, forward=forward),
        [b16(2, 2 * inner, DEPTH), b16(2, 2 * outer, DEPTH)],
        [place, stencils],
        [SMEM, VMEM],
        [
            pltpu.VMEM(((bases + 1) // 2 * 128, -(-total // 128) * 128), jnp.float32),
            pltpu.VMEM((2, DEPTH // 128, 2, inner, 128), jnp.float32),
            pltpu.VMEM((2, DEPTH // 128, 2, outer, 128), jnp.float32),
        ],
        flops=10**9, size=4 << 20,
    )


def pack(place_ref, field_ref, up_ref, down_ref, first_ref, second_ref, breadth):
    height = field_ref.shape[0] // breadth
    margin = up_ref.shape[0] // height
    for row in range(height):
        at = slice(row * margin, (row + 1) * margin)
        up_ref[at, :] = field_ref[(row + 1) * breadth - margin : (row + 1) * breadth, :]
        down_ref[at, :] = field_ref[row * breadth : row * breadth + margin, :]
    low = field_ref[: margin * breadth, :]
    high = field_ref[(height - margin) * breadth :, :]
    odd = place_ref[1] == 1
    first_ref[...] = jnp.where(odd, low, high)
    second_ref[...] = jnp.where(odd, high, low)


def pack_kernel(place_ref, field_ref, up_ref, down_ref, first_ref, second_ref, kept_ref, *, breadth):
    pack(place_ref, field_ref, up_ref, down_ref, first_ref, second_ref, breadth)
    kept_ref[...] = field_ref[...]


def edges(cells, channels, breadth, margin):
    side, row = f32(cells // breadth * margin, channels), f32(margin * breadth, channels)
    return [side, side, row, row]


def corner_kernel(first_ref, second_ref, up_ref, down_ref, *, breadth, margin):
    for part, ref in enumerate((first_ref, second_ref)):
        for row in range(margin):
            at = slice((part * margin + row) * margin, (part * margin + row + 1) * margin)
            up_ref[at, :] = ref[(row + 1) * breadth - margin : (row + 1) * breadth, :]
            down_ref[at, :] = ref[row * breadth : row * breadth + margin, :]


def widen(own, left, right):
    spare = jnp.zeros((SLOTS - own.shape[0] - left.shape[0] - right.shape[0], own.shape[1]), jnp.float32)
    return jnp.concatenate([own, left, right, spare], 0)


def inner_kernel(field_ref, left_ref, right_ref, band_ref, xhigh_ref, xlow_ref, shigh_ref, slow_ref, *, breadth):
    height = field_ref.shape[0] // breadth
    margin = left_ref.shape[0] // height
    bases, cells = shigh_ref.shape[:2]
    count = cells // 2
    zeros = jnp.zeros((margin * SLOTS, field_ref.shape[1]), jnp.bfloat16)
    for ref in (xhigh_ref, xlow_ref):
        ref[: margin * SLOTS, :] = zeros
        ref[(margin + height) * SLOTS :, :] = zeros
    for row in range(height):
        here = slice(row * margin, (row + 1) * margin)
        tile = widen(field_ref[row * breadth : (row + 1) * breadth, :], left_ref[here, :], right_ref[here, :])
        at = slice((margin + row) * SLOTS, (margin + row + 1) * SLOTS)
        xhigh_ref[at, :], xlow_ref[at, :] = split(tile)
    got = []
    for block in range(2):
        window = slice(block * (height // 2) * SLOTS, block * (height // 2) * SLOTS + DEPTH)
        got.append(banded(band_ref[block], xhigh_ref[window, :], xlow_ref[window, :]))
    keep(got, shigh_ref, slow_ref, bases, count)


def banded(band, high, low):
    lines = band.shape[0] // 2
    both = product(band, high, 0)
    return both[:lines] + both[lines:] + product(band[:lines], low, 0)


def keep(got, shigh_ref, slow_ref, bases, count):
    for base in range(bases):
        at = slice(base * count, (base + 1) * count)
        shigh_ref[base], slow_ref[base] = split(jnp.concatenate([part[at] for part in got], 0))


def outer_kernel(place_ref, first_ref, second_ref, left_ref, right_ref, band_ref, xhigh_ref, xlow_ref,
                 shigh_ref, slow_ref, zhigh_ref, zlow_ref, *, breadth):
    margin = first_ref.shape[0] // breadth
    bases, cells = shigh_ref.shape[:2]
    edge = margin * SLOTS
    own = xhigh_ref.shape[0] - 2 * edge
    body = DEPTH - edge
    odd = place_ref[1] == 1
    tiles = []
    for part, ref in enumerate((first_ref, second_ref)):
        rows = []
        for row in range(margin):
            here = slice((part * margin + row) * margin, (part * margin + row + 1) * margin)
            rows.append(widen(ref[row * breadth : (row + 1) * breadth, :], left_ref[here, :], right_ref[here, :]))
        tiles.append(jnp.concatenate(rows, 0))
    low, high = jnp.where(odd, tiles[0], tiles[1]), jnp.where(odd, tiles[1], tiles[0])
    zhigh_ref[0, :edge], zlow_ref[0, :edge] = split(low)
    zhigh_ref[1, body:], zlow_ref[1, body:] = split(high)
    for ref, source_ref in ((zhigh_ref, xhigh_ref), (zlow_ref, xlow_ref)):
        ref[0, edge:] = source_ref[edge : edge + body, :]
        ref[1, :body] = source_ref[edge + own - body : edge + own, :]
    got = [banded(band_ref[block], zhigh_ref[block], zlow_ref[block]) for block in range(2)]
    keep(got, shigh_ref, slow_ref, bases, cells // 2)


def ring(up, down):
    count = lax.axis_size("lon")
    there = [(i, (i + 1) % count) for i in range(count)]
    back = [(b, a) for a, b in there]
    return lax.ppermute(up, "lon", there), lax.ppermute(down, "lon", back)


def swap(first, second):
    count = lax.axis_size("lat")

    def one(piece, lows):
        table = {i: i for i in range(count)}
        for low in lows:
            if low + 1 < count:
                table[low], table[low + 1] = low + 1, low
        return lax.ppermute(piece, "lat", sorted(table.items()))

    return (one(first, range(0, count, 2)), one(second, range(1, count, 2)))


def split_mixing(mixing_ref, high_ref, low_ref):
    for base in range(mixing_ref.shape[0]):
        high_ref[base], low_ref[base] = split(mixing_ref[base])


def contract(taps, mhigh_ref, mlow_ref, lanes, axis):
    inner_high, inner_low, outer_high, outer_low = taps
    total = None
    for base in range(mhigh_ref.shape[0]):
        high = jnp.concatenate([inner_high[base], outer_high[base]], 0)
        low = jnp.concatenate([inner_low[base], outer_low[base]], 0)
        part = product3(high, low, mhigh_ref[base, :, lanes], mlow_ref[base, :, lanes], axis)
        total = part if total is None else total + part
    edge = outer_high.shape[1] // 2
    inner = inner_high.shape[1]
    return jnp.concatenate([total[inner : inner + edge], total[:inner], total[inner + edge :]], 0)


def forward(ihigh_ref, ilow_ref, ohigh_ref, olow_ref, mhigh_ref, mlow_ref, field_ref, predicted_ref, bounded_ref, *, start):
    lanes = slice(start, start + predicted_ref.shape[1])
    total = contract((ihigh_ref, ilow_ref, ohigh_ref, olow_ref), mhigh_ref, mlow_ref, lanes, 0)
    bounded = jnp.tanh(total)
    bounded_ref[...] = bounded
    predicted_ref[...] = field_ref[:, lanes] + bounded


def backward(ihigh_ref, ilow_ref, ohigh_ref, olow_ref, mhigh_ref, mlow_ref, grad_ref, tail_ref, out_ref):
    total = contract((ihigh_ref, ilow_ref, ohigh_ref, olow_ref), mhigh_ref, mlow_ref, slice(None), 1)
    edge = grad_ref.shape[1]
    out_ref[:, :edge] = total[:, :edge] + grad_ref[...]
    out_ref[:, edge:] = total[:, edge:] + tail_ref[...]


def slope(value):
    return value * lax.rsqrt(value * value + SMOOTH)


def soft(value):
    return jnp.sqrt(value * value + SMOOTH)


def loss_first(own_ref, other_ref, bounded_ref, analysis_ref, grad_ref, inner_ref):
    analysis = analysis_ref[:, : own_ref.shape[1]]
    own = own_ref[...] - analysis
    grad = slope(own) - slope(own - (other_ref[...] - analysis))
    grad_ref[...] = grad
    inner_ref[...] = grad * (1.0 - bounded_ref[...] * bounded_ref[...])


def loss_rest(place_ref, own_ref, other_ref, bounded_ref, analysis_ref, before_ref, grad_ref, inner_ref,
              up_ref, down_ref, first_ref, second_ref, *, breadth):
    edge = before_ref.shape[1]
    analysis = analysis_ref[:, edge:]
    own = own_ref[...] - analysis
    grad = slope(own) - slope(own - (other_ref[...] - analysis))
    grad_ref[...] = grad
    inner_ref[:, :edge] = before_ref[...]
    inner_ref[:, edge:] = grad * (1.0 - bounded_ref[...] * bounded_ref[...])
    pack(place_ref, inner_ref, up_ref, down_ref, first_ref, second_ref, breadth)


def whole_analysis(place_ref, mine_ref, theirs_ref, out_ref):
    half = mine_ref.shape[1]
    first = place_ref[2] == 0
    mine, theirs = mine_ref[...], theirs_ref[...]
    out_ref[:, :half] = jnp.where(first, mine, theirs)
    out_ref[:, half:] = jnp.where(first, theirs, mine)


def crps_kernel(place_ref, own1_ref, own2_ref, other1_ref, other2_ref, mine_ref, out_ref):
    half = mine_ref.shape[1]
    edge = own1_ref.shape[1]
    for part in range(2):
        @pl.when(place_ref[2] == part)
        def _():
            low, high = part * half, (part + 1) * half
            pieces = []
            if low < edge:
                pieces.append((own1_ref, other1_ref, slice(low, min(high, edge)), 0))
            if high > edge:
                start = max(low, edge)
                pieces.append((own2_ref, other2_ref, slice(start - edge, high - edge), start - low))
            for own_ref, other_ref, lanes, at in pieces:
                here = slice(at, at + lanes.stop - lanes.start)
                mine = mine_ref[:, here]
                own = own_ref[:, lanes] - mine
                other = other_ref[:, lanes] - mine
                gap = own - other
                pair = 2.0 * (soft(gap) + jnp.sqrt(jnp.full_like(gap, SMOOTH)))
                out_ref[:, here] = 0.5 * (soft(own) + soft(other)) - pair / 4.0


def loss_many(predicted, bounded, analysis):
    grouped = lax.all_to_all(predicted[None], "ens", split_axis=2, concat_axis=0, tiled=True)
    misfit = grouped - analysis[None]
    count = misfit.shape[0]

    def step(other, totals):
        differ = misfit - lax.dynamic_index_in_dim(misfit, other, 0)
        smooth_abs = jnp.sqrt(differ * differ + SMOOTH)
        return totals[0] + smooth_abs.sum(0), totals[1] + differ / smooth_abs

    sums, slopes = lax.fori_loop(
        0, count, step, (jnp.zeros_like(misfit[0]), jnp.zeros_like(misfit))
    )
    own = jnp.sqrt(misfit * misfit + SMOOTH)
    crps = jnp.mean(own, 0) - sums / (2.0 * count * (count - 1))
    grad = misfit / own - slopes / (count - 1.0)
    grad = lax.all_to_all(grad, "ens", split_axis=0, concat_axis=2, tiled=True)[0]
    return grad, grad * (1.0 - bounded * bounded), crps


def local(members, analysis, stencils, mixing):
    _, height, breadth, channels = members.shape
    bases, span = stencils.shape[:2]
    margin = span // 2
    rows = height // 2
    assert height == 2 * rows and rows + 2 * margin <= DEPTH // SLOTS and rows >= 2 * margin
    cells = height * breadth
    pair = lax.axis_size("ens") == 2
    flat = members.reshape(cells, channels)
    mine = analysis.reshape(cells, analysis.shape[2])
    rest = channels - EDGE
    place = jnp.stack([
        lax.axis_index("lat") * height, lax.axis_index("lat") % 2, lax.axis_index("ens")
    ]).astype(jnp.int32)
    packed = edges(cells, channels, breadth, margin)
    mix_flops = 6 * cells * bases * channels * channels
    stencil_flops = 6 * bases * cells * DEPTH * channels
    inner_cells, outer_cells = cells - 2 * margin * breadth, 2 * margin * breadth

    def taps(count):
        return [b16(bases, count, channels)] * 2

    def spread(up, down, first, second, field, band):
        left, right = ring(up, down)
        first, second = swap(first, second)
        corner = f32(2 * margin * margin, channels)
        corners = call(
            functools.partial(corner_kernel, breadth=breadth, margin=margin),
            [corner, corner], [first, second], size=1 << 18, limit=4,
        )
        cleft, cright = ring(*corners)
        window = b16((height + 2 * margin) * SLOTS, channels)
        xhigh, xlow, *inner = call(
            functools.partial(inner_kernel, breadth=breadth),
            [window, window] + taps(inner_cells), [field, left, right, band[0]],
            flops=stencil_flops * 7 // 10,
        )
        depth = pltpu.VMEM((2, DEPTH, channels), jnp.bfloat16)
        outer = call(
            functools.partial(outer_kernel, breadth=breadth), taps(outer_cells),
            [place, first, second, cleft, cright, band[1], xhigh, xlow], [SMEM] + [VMEM] * 7,
            [depth, depth], flops=stencil_flops * 3 // 10,
        )
        return [*inner, *outer]

    *sent, flat = call(
        functools.partial(pack_kernel, breadth=breadth), packed + [f32(cells, channels)],
        [place, flat], [SMEM, VMEM], flops=10**10, size=1 << 20, limit=8,
    )
    band = bands(place, stencils, rows, breadth, True)
    spread0 = spread(*sent, flat, band)
    if pair:
        theirs = lax.ppermute(mine, "ens", SWAP)
    weights = call(split_mixing, [b16(*mixing.shape)] * 2, [mixing], size=mixing.size * 4)
    predicted1, bounded1 = call(
        functools.partial(forward, start=0), [f32(cells, EDGE)] * 2,
        [*spread0, *weights, flat], flops=mix_flops * EDGE // channels,
    )
    if pair:
        other1 = lax.ppermute(predicted1, "ens", SWAP)
    predicted2, bounded2 = call(
        functools.partial(forward, start=EDGE), [f32(cells, rest)] * 2,
        [*spread0, *weights, flat], flops=mix_flops * rest // channels,
    )
    back = bands(place, stencils, rows, breadth, False)
    if pair:
        other2 = lax.ppermute(predicted2, "ens", SWAP)
        (known,) = call(
            whole_analysis, [f32(cells, channels)], [place, mine, theirs],
            [SMEM, VMEM, VMEM], size=1 << 20, limit=8,
        )
        grad1, inner1 = call(
            loss_first, [f32(cells, EDGE)] * 2,
            [predicted1, other1, bounded1, known], size=1 << 20, limit=8,
        )
        grad2, inner, *sent = call(
            functools.partial(loss_rest, breadth=breadth),
            [f32(cells, rest), f32(cells, channels)] + packed,
            [place, predicted2, other2, bounded2, known, inner1], [SMEM] + [VMEM] * 5,
            size=2 << 20, limit=8,
        )
        (crps,) = call(
            crps_kernel, [f32(*mine.shape)],
            [place, predicted1, predicted2, other1, other2, mine], [SMEM] + [VMEM] * 5,
            size=1 << 20, limit=8,
        )
    else:
        predicted = jnp.concatenate([predicted1, predicted2], 1)
        bounded = jnp.concatenate([bounded1, bounded2], 1)
        grad, inner, crps = loss_many(predicted, bounded, mine)
        grad1, grad2 = grad[:, :EDGE], grad[:, EDGE:]
        *sent, inner = call(
            functools.partial(pack_kernel, breadth=breadth), packed + [f32(cells, channels)],
            [place, inner], [SMEM, VMEM], size=1 << 20, limit=8,
        )
    (result,) = call(
        backward, [f32(cells, channels)],
        [*spread(*sent, inner, back), *weights, grad1, grad2], flops=mix_flops,
    )
    return result.reshape(members.shape), crps.reshape(analysis.shape)


def solution(mesh):
    in_specs = (P("ens", "lat", "lon", None), P("lat", "lon", "ens"), P(), P())
    out_specs = (P("ens", "lat", "lon", None), P("lat", "lon", "ens"))
    return jax.shard_map(local, mesh=mesh, in_specs=in_specs, out_specs=out_specs, check_vma=False)
```

time: 69.6 us -> 55.7 us (0.80)
  the two profiles are of different devices: /device:TPU:0 before, /device:TPU:1 now
where the time goes in v2:
time: 55.7 us; the launch traced here: 55.5 us
  Pallas kernels  23.5 us (42%)
  starting transfers between devices  18.3 us (33%)
  waiting for transfers between devices  11.6 us (21%)
  local copies, waits for them, and re-layouts  1.17 us (2%)
  between operations  0.85 us (2%)
    pallas_call x17, Pallas kernels, call(): pl.pallas_call(body, out_shape=out_shape, in_specs=specs or [VMEM] * len(...  23.5 us
    ppermute x8, starting transfers between devices, ring(): return (lax.ppermute(up, 'lon', there), lax.ppermute(down, 'lon', back))  8.63 us
    ppermute x4, starting transfers between devices, one(): return lax.ppermute(piece, 'lat', sorted(table.items()))  6.85 us
    ppermute x1, waiting for transfers between devices, local(): other1 = lax.ppermute(predicted1, 'ens', SWAP)  6.81 us
    ppermute x8, waiting for transfers between devices, ring(): return (lax.ppermute(up, 'lon', there), lax.ppermute(down, 'lon', back))  4.79 us
    ppermute x1, starting transfers between devices, local(): other1 = lax.ppermute(predicted1, 'ens', SWAP)  1.27 us
    ppermute x1, starting transfers between devices, local(): theirs = lax.ppermute(mine, 'ens', SWAP)  1.21 us
    unnamed x12, local copies, waits for them, and re-layouts  1.17 us
  transfers between devices with their start and end apart: 15, of which 3 were waited for; matrix products, arithmetic and copies ran while one was open for 0% of the time, Pallas kernels for 28%

profile of v2, /device:TPU:1, one launch (start us, length us, event | category | flops | bytes accessed | tf_op | source)
XLA Modules:
  0.0 55.5 jit_solution(4662083321427187609)
XLA Ops:
  0.6 0.1 pad_add_fusion.place_ref
  0.7 0.0 slice-start
  0.7 0.0 copy-start.1
  0.7 1.2 %copy-done.1 = f32[1,20,8,640]{3,2,1,0:T(8,128)S(1)} copy-done((f32[1,20,8,640]{3,2,1,0:T(8,128)S(1)}, f32[1,20,8,640]{3,2,1,0:T(8,128)}, u32[]{:S(2)}) %copy-start.1) | copy-done | bytes 409624
  1.9 0.0 copy-start
  1.9 0.0 slice-start.1
  1.9 0.0 slice-start.2
  1.9 0.7 %shard_map.59 = (f32[60,640]{1,0:T(8,128)S(1)}, f32[60,640]{1,0:T(8,128)S(1)}, f32[24,640]{1,0:T(8,128)S(1)}, f32[24,640]{1,0:T(8,128)S(1)}, f32[160,640]{1,0:T(8,128)S(1)}) custom-call(s32[3]{0:T(128)S(1)} %pad_add_fusion.place_ref, f32[160,640]{1,0:T(8,128)S(1)} %bitcast.12), custom_call_target="tpu_custom_call" | custom-call | flops 10000000000 | bytes 1048576 | tf_op jit(solution)/shard_map/pallas_call | solution.py:47
  2.6 2.7 %collective-permute-start = (f32[60,640]{1,0:T(8,128)S(1)}, f32[60,640]{1,0:T(8,128)S(1)}, u32[]{:S(2)}, u32[]{:S(2)}) collective-permute-start(f32[60,640]{1,0:T(8,128)S(1)} %get-tuple-element.42), channel_id=1, source_target_pairs={{0,4},{4,8},{8,12},{12,0},{1,5},{5,9},{9,13},{13,1},{2,6},{6,10},{... | collective-permute-start | bytes 460808 | tf_op jit(solution)/shard_map/ppermute | solution.py:262
  5.2 0.0 collective-permute-start.1
  5.2 0.0 copy-done
  5.2 1.2 %collective-permute-start.7 = (f32[160,320]{1,0:T(8,128)S(1)}, f32[160,320]{1,0:T(8,128)S(1)}, u32[]{:S(2)}, u32[]{:S(2)}) collective-permute-start(f32[160,320]{1,0:T(8,128)S(1)} %bitcast.9), channel_id=1, source_target_pairs={{0,16},{16,0},{1,17},{17,1},{2,18},{18,2},{3,19},{19,3},{4,20},{20... | collective-permute-start | bytes 614408 | tf_op jit(solution)/shard_map/ppermute | solution.py:442
  6.4 1.3 %collective-permute-start.2 = (f32[24,640]{1,0:T(8,128)S(1)}, f32[24,640]{1,0:T(8,128)S(1)}, u32[]{:S(2)}, u32[]{:S(2)}) collective-permute-start(f32[24,640]{1,0:T(8,128)S(1)} %get-tuple-element.47), channel_id=1, source_target_pairs={{0,1},{1,0},{2,3},{3,2},{4,5},{5,4},{6,7},{7,6},{8,9},{9,8},{10,11... | collective-permute-start | bytes 184328 | tf_op jit(solution)/shard_map/ppermute | solution.py:273
  7.7 0.0 copy-start.2
  7.7 0.8 %collective-permute-start.3 = (f32[24,640]{1,0:T(8,128)S(1)}, f32[24,640]{1,0:T(8,128)S(1)}, u32[]{:S(2)}, u32[]{:S(2)}) collective-permute-start(f32[24,640]{1,0:T(8,128)S(1)} %get-tuple-element.48), channel_id=1, source_target_pairs={{0,0},{1,2},{2,1},{3,3},{4,4},{5,6},{6,5},{7,7},{8,8},{9,10},{10,9... | collective-permute-start | bytes 184328 | tf_op jit(solution)/shard_map/ppermute | solution.py:273
  8.5 0.0 slice-done
  8.5 0.0 slice-done.1
  8.6 0.0 slice-done.2
  8.6 1.7 %shard_map.64 = (bf16[7,640,640]{2,1,0:T(8,128)(2,1)S(1)}, bf16[7,640,640]{2,1,0:T(8,128)(2,1)S(1)}) custom-call(f32[7,640,640]{2,1,0:T(8,128)S(1)} %bitcast.8), custom_call_target="tpu_custom_call" | custom-call | bytes 11468800 | tf_op jit(solution)/shard_map/pallas_call | solution.py:47
  10.2 0.0 copy-done.2
  10.2 1.6 %shard_map.60 = (bf16[2,784,256]{2,1,0:T(8,128)(2,1)S(1)}, bf16[2,336,256]{2,1,0:T(8,128)(2,1)S(1)}) custom-call(s32[3]{0:T(128)S(1)} %pad_add_fusion.place_ref, f32[7,7,7,80]{3,2,1,0:T(8,128)S(1)} %copy-done.2), custom_call_target="tpu_custom_call" | custom-call | flops 1000000000 | bytes 4194304 | tf_op jit(solution)/shard_map/pallas_call | solution.py:47
  11.9 0.0 collective-permute-done.2.first_ref
  11.9 0.0 collective-permute-done.3.second_ref
  12.0 2.4 %collective-permute-start.4 = (f32[18,640]{1,0:T(8,128)S(1)}, f32[18,640]{1,0:T(8,128)S(1)}, u32[]{:S(2)}, u32[]{:S(2)}) collective-permute-start(f32[18,640]{1,0:T(8,128)S(1)} %get-tuple-element.49), channel_id=1, source_target_pairs={{0,4},{4,8},{8,12},{12,0},{1,5},{5,9},{9,13},{13,1},{2,6},{6,10},{... | collective-permute-start | bytes 138248 | tf_op jit(solution)/shard_map/ppermute | solution.py:262
  14.3 0.0 collective-permute-start.5
  14.3 0.0 collective-permute-done.left_ref
  14.3 0.0 collective-permute-done.1.right_ref
  14.3 1.2 %shard_map.61 = (bf16[416,640]{1,0:T(8,128)(2,1)S(1)}, bf16[416,640]{1,0:T(8,128)(2,1)S(1)}, bf16[7,112,640]{2,1,0:T(8,128)(2,1)S(1)}, bf16[7,112,640]{2,1,0:T(8,128)(2,1)S(1)}) custom-call(f32[160,640]{1,0:T(8,128)S(1)} %get-tuple-element.41.field_ref, f32[60,640]{1,0:T(8,128)S(1)} %collective-permute-done.left_ref, ...), custom_call_target="tpu_custom_call" | custom-call | flops 770703360 | tf_op jit(solution)/shard_map/pallas_call | solution.py:47
  15.6 0.0 collective-permute-done.4.left_ref
  15.6 2.4 %collective-permute-done.5.right_ref = f32[18,640]{1,0:T(8,128)S(1)} collective-permute-done((f32[18,640]{1,0:T(8,128)S(1)}, f32[18,640]{1,0:T(8,128)S(1)}, u32[]{:S(2)}, u32[]{:S(2)}) %collective-permute-start.5) | collective-permute-done | bytes 46112 | tf_op jit(solution)/shard_map/ppermute | solution.py:262
  18.0 1.2 %shard_map.63 = (bf16[7,48,640]{2,1,0:T(8,128)(2,1)S(1)}, bf16[7,48,640]{2,1,0:T(8,128)(2,1)S(1)}) custom-call(s32[3]{0:T(128)S(1)} %pad_add_fusion.place_ref, f32[24,640]{1,0:T(8,128)S(1)} %collective-permute-done.2.first_ref, f32[24,640]{1,0:T(8,128)S(1)} %collective-permute-done.3.second_ref, f32[18,640]{1,0:T(8,128)S(1)} %collective-permute-done.4.left_ref, ...), custom_call_target="tpu_custom_call" | custom-call | flops 330301440 | tf_op jit(solution)/shard_map/pallas_call | solution.py:47
  19.2 2.7 %shard_map.65 = (f32[160,384]{1,0:T(8,128)S(1)}, f32[160,384]{1,0:T(8,128)S(1)}) custom-call(bf16[7,112,640]{2,1,0:T(8,128)(2,1)S(1)} %get-tuple-element.45.ihigh_ref, bf16[7,112,640]{2,1,0:T(8,128)(2,1)S(1)} %get-tuple-element.46.ilow_ref, bf16[7,48,640]{2,1,0:T(8,128)(2,1)S(1)} %get-tuple-element.54.ohigh_ref, ...), custom_call_target="tpu_custom_call" | custom-call | flops 1651507200 | tf_op jit(solution)/shard_map/pallas_call | solution.py:47
  21.9 0.3 collective-permute-start.6
  22.2 1.5 %shard_map.67 = (f32[160,256]{1,0:T(8,128)S(1)}, f32[160,256]{1,0:T(8,128)S(1)}) custom-call(bf16[7,112,640]{2,1,0:T(8,128)(2,1)S(1)} %get-tuple-element.45.ihigh_ref, bf16[7,112,640]{2,1,0:T(8,128)(2,1)S(1)} %get-tuple-element.46.ilow_ref, bf16[7,48,640]{2,1,0:T(8,128)(2,1)S(1)} %get-tuple-element.54.ohigh_ref, ...), custom_call_target="tpu_custom_call" | custom-call | flops 1101004800 | tf_op jit(solution)/shard_map/pallas_call | solution.py:47
  23.7 1.3 %collective-permute-start.8 = (f32[160,256]{1,0:T(8,128)S(1)}, f32[160,256]{1,0:T(8,128)S(1)}, u32[]{:S(2)}, u32[]{:S(2)}) collective-permute-start(f32[160,256]{1,0:T(8,128)S(1)} %get-tuple-element.60.own_ref.own1_ref), channel_id=1, source_target_pairs={{0,16},{16,0},{1,17},{17,1},{2,18},{18,2},{3,19},{19,3},{4,20},{20... | collective-permute-start | bytes 491528 | tf_op jit(solution)/shard_map/ppermute | solution.py:449
  25.0 0.0 collective-permute-done.7.theirs_ref
  25.0 0.7 %shard_map.66.analysis_ref = f32[160,640]{1,0:T(8,128)S(1)} custom-call(s32[3]{0:T(128)S(1)} %pad_add_fusion.place_ref, f32[160,320]{1,0:T(8,128)S(1)} %bitcast.10, f32[160,320]{1,0:T(8,128)S(1)} %collective-permute-done.7.theirs_ref), custom_call_target="tpu_custom_call" | custom-call | bytes 1048576 | tf_op jit(solution)/shard_map/pallas_call | solution.py:47
  25.7 6.8 %collective-permute-done.8.other_ref.other1_ref = f32[160,256]{1,0:T(8,128)S(1)} collective-permute-done((f32[160,256]{1,0:T(8,128)S(1)}, f32[160,256]{1,0:T(8,128)S(1)}, u32[]{:S(2)}, u32[]{:S(2)}) %collective-permute-start.8) | collective-permute-done | bytes 163872 | tf_op jit(solution)/shard_map/ppermute | solution.py:449
  32.5 0.1 shard_map.68
  32.5 0.0 collective-permute-done.6.other_ref.other2_ref
  32.6 0.9 %shard_map.69 = (f32[160,384]{1,0:T(8,128)S(1)}, f32[160,640]{1,0:T(8,128)S(1)}, f32[60,640]{1,0:T(8,128)S(1)}, f32[60,640]{1,0:T(8,128)S(1)}, f32[24,640]{1,0:T(8,128)S(1)}, /*index=5*/f32[24,640]{1,0:T(8,128)S(1)}) custom-call(s32[3]{0:T(128)S(1)} %pad_add_fusion.place_ref, f32[160,384]{1,0:T(8,128)S(1)} %get-tuple-element.58.own_ref.own2_ref, ...), custom_call_target="tpu_custom_call" | custom-call | bytes 2097152 | tf_op jit(solution)/shard_map/pallas_call | solution.py:47
  33.4 1.5 %collective-permute-start.9 = (f32[60,640]{1,0:T(8,128)S(1)}, f32[60,640]{1,0:T(8,128)S(1)}, u32[]{:S(2)}, u32[]{:S(2)}) collective-permute-start(f32[60,640]{1,0:T(8,128)S(1)} %get-tuple-element.64), channel_id=1, source_target_pairs={{0,4},{4,8},{8,12},{12,0},{1,5},{5,9},{9,13},{13,1},{2,6},{6,10},{... | collective-permute-start | bytes 460808 | tf_op jit(solution)/shard_map/ppermute | solution.py:262
  34.9 0.0 collective-permute-start.10
  34.9 4.1 %collective-permute-start.11 = (f32[24,640]{1,0:T(8,128)S(1)}, f32[24,640]{1,0:T(8,128)S(1)}, u32[]{:S(2)}, u32[]{:S(2)}) collective-permute-start(f32[24,640]{1,0:T(8,128)S(1)} %get-tuple-element.69), channel_id=1, source_target_pairs={{0,1},{1,0},{2,3},{3,2},{4,5},{5,4},{6,7},{7,6},{8,9},{9,8},{10,11... | collective-permute-start | bytes 184328 | tf_op jit(solution)/shard_map/ppermute | solution.py:273
  39.1 0.7 %collective-permute-start.12 = (f32[24,640]{1,0:T(8,128)S(1)}, f32[24,640]{1,0:T(8,128)S(1)}, u32[]{:S(2)}, u32[]{:S(2)}) collective-permute-start(f32[24,640]{1,0:T(8,128)S(1)} %get-tuple-element.70), channel_id=1, source_target_pairs={{0,0},{1,2},{2,1},{3,3},{4,4},{5,6},{6,5},{7,7},{8,8},{9,10},{10,9... | collective-permute-start | bytes 184328 | tf_op jit(solution)/shard_map/ppermute | solution.py:273
  39.7 1.7 %shard_map.70 = (bf16[2,784,256]{2,1,0:T(8,128)(2,1)S(1)}, bf16[2,336,256]{2,1,0:T(8,128)(2,1)S(1)}) custom-call(s32[3]{0:T(128)S(1)} %pad_add_fusion.place_ref, f32[7,7,7,80]{3,2,1,0:T(8,128)S(1)} %copy-done.2), custom_call_target="tpu_custom_call" | custom-call | flops 1000000000 | bytes 4194304 | tf_op jit(solution)/shard_map/pallas_call | solution.py:47
  41.5 1.7 %shard_map.75 = f32[160,320]{1,0:T(8,128)} custom-call(s32[3]{0:T(128)S(1)} %pad_add_fusion.place_ref, f32[160,256]{1,0:T(8,128)S(1)} %get-tuple-element.60.own_ref.own1_ref, f32[160,384]{1,0:T(8,128)S(1)} %get-tuple-element.58.own_ref.own2_ref, f32[160,256]{1,0:T(8,128)S(1)} %collective-permute-done.8.other_ref.other1_ref, ...), custom_call_target="tpu_custom_call" | custom-call | bytes 1048576 | tf_op jit(solution)/shard_map/pallas_call | solution.py:47
  43.2 0.0 collective-permute-done.11.first_ref
  43.2 0.0 collective-permute-done.12.second_ref
  43.2 2.1 %collective-permute-start.13 = (f32[18,640]{1,0:T(8,128)S(1)}, f32[18,640]{1,0:T(8,128)S(1)}, u32[]{:S(2)}, u32[]{:S(2)}) collective-permute-start(f32[18,640]{1,0:T(8,128)S(1)} %get-tuple-element.71), channel_id=1, source_target_pairs={{0,4},{4,8},{8,12},{12,0},{1,5},{5,9},{9,13},{13,1},{2,6},{6,10},{... | collective-permute-start | bytes 138248 | tf_op jit(solution)/shard_map/ppermute | solution.py:262
  45.3 0.0 collective-permute-start.14
  45.3 0.0 collective-permute-done.9.left_ref
  45.3 0.0 collective-permute-done.10.right_ref
  45.3 1.2 %shard_map.71 = (bf16[416,640]{1,0:T(8,128)(2,1)S(1)}, bf16[416,640]{1,0:T(8,128)(2,1)S(1)}, bf16[7,112,640]{2,1,0:T(8,128)(2,1)S(1)}, bf16[7,112,640]{2,1,0:T(8,128)(2,1)S(1)}) custom-call(f32[160,640]{1,0:T(8,128)S(1)} %get-tuple-element.63.field_ref, f32[60,640]{1,0:T(8,128)S(1)} %collective-permute-done.9.left_ref, ...), custom_call_target="tpu_custom_call" | custom-call | flops 770703360 | tf_op jit(solution)/shard_map/pallas_call | solution.py:47
  46.6 0.0 collective-permute-done.13.left_ref
  46.6 2.4 %collective-permute-done.14.right_ref = f32[18,640]{1,0:T(8,128)S(1)} collective-permute-done((f32[18,640]{1,0:T(8,128)S(1)}, f32[18,640]{1,0:T(8,128)S(1)}, u32[]{:S(2)}, u32[]{:S(2)}) %collective-permute-start.14) | collective-permute-done | bytes 46112 | tf_op jit(solution)/shard_map/ppermute | solution.py:262
  48.9 1.2 %shard_map.73 = (bf16[7,48,640]{2,1,0:T(8,128)(2,1)S(1)}, bf16[7,48,640]{2,1,0:T(8,128)(2,1)S(1)}) custom-call(s32[3]{0:T(128)S(1)} %pad_add_fusion.place_ref, f32[24,640]{1,0:T(8,128)S(1)} %collective-permute-done.11.first_ref, f32[24,640]{1,0:T(8,128)S(1)} %collective-permute-done.12.second_ref, f32[18,640]{1,0:T(8,128)S(1)} %collective-permute-done.13.left_ref, ...), custom_call_target="tpu_custom_call" | custom-call | flops 330301440 | tf_op jit(solution)/shard_map/pallas_call | solution.py:47
  50.2 5.3 %shard_map.74 = f32[160,640]{1,0:T(8,128)} custom-call(bf16[7,112,640]{2,1,0:T(8,128)(2,1)S(1)} %get-tuple-element.67.ihigh_ref, bf16[7,112,640]{2,1,0:T(8,128)(2,1)S(1)} %get-tuple-element.68.ilow_ref, bf16[7,48,640]{2,1,0:T(8,128)(2,1)S(1)} %get-tuple-element.76.ohigh_ref, bf16[7,48,640]{2,1,0:T(8,128)(2,1)S(1)} %get-tuple-element.77.olow_ref, ...), custom_call_target="tpu_custom_call" | custom-call | flops 2752512000 | tf_op jit(solution)/shard_map/pallas_call | solution.py:47
  (3 shorter events, 0.1 us)
Async XLA Ops:
  0.7 7.8 %slice-start = ((s8[11468800]{0:T(1024)(128)(4,1)}), s8[4194304]{0:T(1024)(128)(4,1)S(1)}, s32[]{:S(2)}) async-start(s8[11468800]{0:T(1024)(128)(4,1)} %bitcast.7), calls=%async_computation | async-start | bytes 8388608
  0.7 1.2 %copy-start.1 = (f32[1,20,8,640]{3,2,1,0:T(8,128)S(1)}, f32[1,20,8,640]{3,2,1,0:T(8,128)}, u32[]{:S(2)}) copy-start(f32[1,20,8,640]{3,2,1,0:T(8,128)} %param.4) | copy-start | bytes 1228804
  1.9 3.4 %copy-start = (f32[20,8,320]{2,1,0:T(8,128)S(1)}, f32[20,8,320]{2,1,0:T(8,128)}, u32[]{:S(2)}) copy-start(f32[20,8,320]{2,1,0:T(8,128)} %param.5) | copy-start | bytes 614404
  1.9 6.7 %slice-start.1 = ((s8[11468800]{0:T(1024)(128)(4,1)}), s8[4194304]{0:T(1024)(128)(4,1)S(1)}, s32[]{:S(2)}) async-start(s8[11468800]{0:T(1024)(128)(4,1)} %bitcast.7), calls=%async_computation.1 | async-start | bytes 8388608
  1.9 6.7 %slice-start.2 = ((s8[11468800]{0:T(1024)(128)(4,1)}), s8[3080192]{0:T(1024)(128)(4,1)S(1)}, s32[]{:S(2)}) async-start(s8[11468800]{0:T(1024)(128)(4,1)} %bitcast.7), calls=%async_computation.2 | async-start | bytes 6160384
  2.6 11.8 %collective-permute-start = (f32[60,640]{1,0:T(8,128)S(1)}, f32[60,640]{1,0:T(8,128)S(1)}, u32[]{:S(2)}, u32[]{:S(2)}) collective-permute-start(f32[60,640]{1,0:T(8,128)S(1)} %get-tuple-element.42), channel_id=1, source_target_pairs={{0,4},{4,8},{8,12},{12,0},{1,5},{5,9},{9,13},{13,1},{2,6},{6,10},{... | collective-permute-start | bytes 460808 | tf_op jit(solution)/shard_map/ppermute | solution.py:262
  5.2 9.1 %collective-permute-start.1 = (f32[60,640]{1,0:T(8,128)S(1)}, f32[60,640]{1,0:T(8,128)S(1)}, u32[]{:S(2)}, u32[]{:S(2)}) collective-permute-start(f32[60,640]{1,0:T(8,128)S(1)} %get-tuple-element.43), channel_id=1, source_target_pairs={{4,0},{8,4},{12,8},{0,12},{5,1},{9,5},{13,9},{1,13},{6,2},{10,6},{... | collective-permute-start | bytes 460808 | tf_op jit(solution)/shard_map/ppermute | solution.py:262
  5.2 19.7 %collective-permute-start.7 = (f32[160,320]{1,0:T(8,128)S(1)}, f32[160,320]{1,0:T(8,128)S(1)}, u32[]{:S(2)}, u32[]{:S(2)}) collective-permute-start(f32[160,320]{1,0:T(8,128)S(1)} %bitcast.9), channel_id=1, source_target_pairs={{0,16},{16,0},{1,17},{17,1},{2,18},{18,2},{3,19},{19,3},{4,20},{20... | collective-permute-start | bytes 614408 | tf_op jit(solution)/shard_map/ppermute | solution.py:442
  6.4 5.5 %collective-permute-start.2 = (f32[24,640]{1,0:T(8,128)S(1)}, f32[24,640]{1,0:T(8,128)S(1)}, u32[]{:S(2)}, u32[]{:S(2)}) collective-permute-start(f32[24,640]{1,0:T(8,128)S(1)} %get-tuple-element.47), channel_id=1, source_target_pairs={{0,1},{1,0},{2,3},{3,2},{4,5},{5,4},{6,7},{7,6},{8,9},{9,8},{10,11... | collective-permute-start | bytes 184328 | tf_op jit(solution)/shard_map/ppermute | solution.py:273
  7.7 2.5 %copy-start.2 = (f32[7,7,7,80]{3,2,1,0:T(8,128)S(1)}, f32[7,7,7,80]{3,2,1,0:T(8,128)}, u32[]{:S(2)}) copy-start(f32[7,7,7,80]{3,2,1,0:T(8,128)} %stencils_ref.3) | copy-start | bytes 329284
  7.7 4.2 %collective-permute-start.3 = (f32[24,640]{1,0:T(8,128)S(1)}, f32[24,640]{1,0:T(8,128)S(1)}, u32[]{:S(2)}, u32[]{:S(2)}) collective-permute-start(f32[24,640]{1,0:T(8,128)S(1)} %get-tuple-element.48), channel_id=1, source_target_pairs={{0,0},{1,2},{2,1},{3,3},{4,4},{5,6},{6,5},{7,7},{8,8},{9,10},{10,9... | collective-permute-start | bytes 184328 | tf_op jit(solution)/shard_map/ppermute | solution.py:273
  12.0 3.6 %collective-permute-start.4 = (f32[18,640]{1,0:T(8,128)S(1)}, f32[18,640]{1,0:T(8,128)S(1)}, u32[]{:S(2)}, u32[]{:S(2)}) collective-permute-start(f32[18,640]{1,0:T(8,128)S(1)} %get-tuple-element.49), channel_id=1, source_target_pairs={{0,4},{4,8},{8,12},{12,0},{1,5},{5,9},{9,13},{13,1},{2,6},{6,10},{... | collective-permute-start | bytes 138248 | tf_op jit(solution)/shard_map/ppermute | solution.py:262
  14.3 3.6 %collective-permute-start.5 = (f32[18,640]{1,0:T(8,128)S(1)}, f32[18,640]{1,0:T(8,128)S(1)}, u32[]{:S(2)}, u32[]{:S(2)}) collective-permute-start(f32[18,640]{1,0:T(8,128)S(1)} %get-tuple-element.50), channel_id=1, source_target_pairs={{4,0},{8,4},{12,8},{0,12},{5,1},{9,5},{13,9},{1,13},{6,2},{10,6},{... | collective-permute-start | bytes 138248 | tf_op jit(solution)/shard_map/ppermute | solution.py:262
  21.9 10.7 %collective-permute-start.6 = (f32[160,384]{1,0:T(8,128)S(1)}, f32[160,384]{1,0:T(8,128)S(1)}, u32[]{:S(2)}, u32[]{:S(2)}) collective-permute-start(f32[160,384]{1,0:T(8,128)S(1)} %get-tuple-element.58.own_ref.own2_ref), channel_id=1, source_target_pairs={{0,16},{16,0},{1,17},{17,1},{2,18},{18,2},{3,19},{19,3},{4,20},{20... | collective-permute-start | bytes 737288 | tf_op jit(solution)/shard_map/ppermute | solution.py:456
  23.7 8.8 %collective-permute-start.8 = (f32[160,256]{1,0:T(8,128)S(1)}, f32[160,256]{1,0:T(8,128)S(1)}, u32[]{:S(2)}, u32[]{:S(2)}) collective-permute-start(f32[160,256]{1,0:T(8,128)S(1)} %get-tuple-element.60.own_ref.own1_ref), channel_id=1, source_target_pairs={{0,16},{16,0},{1,17},{17,1},{2,18},{18,2},{3,19},{19,3},{4,20},{20... | collective-permute-start | bytes 491528 | tf_op jit(solution)/shard_map/ppermute | solution.py:449
  33.4 11.9 %collective-permute-start.9 = (f32[60,640]{1,0:T(8,128)S(1)}, f32[60,640]{1,0:T(8,128)S(1)}, u32[]{:S(2)}, u32[]{:S(2)}) collective-permute-start(f32[60,640]{1,0:T(8,128)S(1)} %get-tuple-element.64), channel_id=1, source_target_pairs={{0,4},{4,8},{8,12},{12,0},{1,5},{5,9},{9,13},{13,1},{2,6},{6,10},{... | collective-permute-start | bytes 460808 | tf_op jit(solution)/shard_map/ppermute | solution.py:262
  34.9 10.4 %collective-permute-start.10 = (f32[60,640]{1,0:T(8,128)S(1)}, f32[60,640]{1,0:T(8,128)S(1)}, u32[]{:S(2)}, u32[]{:S(2)}) collective-permute-start(f32[60,640]{1,0:T(8,128)S(1)} %get-tuple-element.65), channel_id=1, source_target_pairs={{4,0},{8,4},{12,8},{0,12},{5,1},{9,5},{13,9},{1,13},{6,2},{10,6},{... | collective-permute-start | bytes 460808 | tf_op jit(solution)/shard_map/ppermute | solution.py:262
  34.9 8.2 %collective-permute-start.11 = (f32[24,640]{1,0:T(8,128)S(1)}, f32[24,640]{1,0:T(8,128)S(1)}, u32[]{:S(2)}, u32[]{:S(2)}) collective-permute-start(f32[24,640]{1,0:T(8,128)S(1)} %get-tuple-element.69), channel_id=1, source_target_pairs={{0,1},{1,0},{2,3},{3,2},{4,5},{5,4},{6,7},{7,6},{8,9},{9,8},{10,11... | collective-permute-start | bytes 184328 | tf_op jit(solution)/shard_map/ppermute | solution.py:273
  39.1 4.1 %collective-permute-start.12 = (f32[24,640]{1,0:T(8,128)S(1)}, f32[24,640]{1,0:T(8,128)S(1)}, u32[]{:S(2)}, u32[]{:S(2)}) collective-permute-start(f32[24,640]{1,0:T(8,128)S(1)} %get-tuple-element.70), channel_id=1, source_target_pairs={{0,0},{1,2},{2,1},{3,3},{4,4},{5,6},{6,5},{7,7},{8,8},{9,10},{10,9... | collective-permute-start | bytes 184328 | tf_op jit(solution)/shard_map/ppermute | solution.py:273
  43.2 3.4 %collective-permute-start.13 = (f32[18,640]{1,0:T(8,128)S(1)}, f32[18,640]{1,0:T(8,128)S(1)}, u32[]{:S(2)}, u32[]{:S(2)}) collective-permute-start(f32[18,640]{1,0:T(8,128)S(1)} %get-tuple-element.71), channel_id=1, source_target_pairs={{0,4},{4,8},{8,12},{12,0},{1,5},{5,9},{9,13},{13,1},{2,6},{6,10},{... | collective-permute-start | bytes 138248 | tf_op jit(solution)/shard_map/ppermute | solution.py:262
  45.3 3.6 %collective-permute-start.14 = (f32[18,640]{1,0:T(8,128)S(1)}, f32[18,640]{1,0:T(8,128)S(1)}, u32[]{:S(2)}, u32[]{:S(2)}) collective-permute-start(f32[18,640]{1,0:T(8,128)S(1)} %get-tuple-element.72), channel_id=1, source_target_pairs={{4,0},{8,4},{12,8},{0,12},{5,1},{9,5},{13,9},{1,13},{6,2},{10,6},{... | collective-permute-start | bytes 138248 | tf_op jit(solution)/shard_map/ppermute | solution.py:262

commit v3 on v2

--- a/solution.py
+++ b/solution.py
@@ -14,7 +14,6 @@
 EDGE = 256
 SWAP = [(0, 1), (1, 0)]
 VMEM = pl.BlockSpec(memory_space=pltpu.VMEM)
-SMEM = pl.BlockSpec(memory_space=pltpu.SMEM)
 
 
 def f32(*shape):
@@ -55,12 +54,12 @@
     )(*operands)
 
 
-def band_kernel(place_ref, stencils_ref, inner_ref, outer_ref, table_ref, in_ref, out_ref, *, rows, forward):
+def band_kernel(stencils_ref, inner_ref, outer_ref, table_ref, in_ref, out_ref, *, rows, forward):
     bases, span, _, total = stencils_ref.shape
     blocks = inner_ref.shape[0]
     margin = span // 2
     breadth = outer_ref.shape[1] // (2 * bases * margin)
-    first_row = place_ref[0]
+    first_row = lax.axis_index("lat") * (2 * rows)
     iota = lambda shape, axis: lax.broadcasted_iota(jnp.int32, shape, axis)
 
     table_ref[...] = jnp.zeros_like(table_ref)
@@ -142,16 +141,15 @@
             ref[:, :, lanes] = both.astype(jnp.bfloat16)
 
 
-def bands(place, stencils, rows, breadth, forward):
+def bands(stencils, rows, breadth, forward):
     bases, span, _, total = stencils.shape
     margin = span // 2
     inner, outer = bases * (rows - margin) * breadth, bases * margin * breadth
     return call(
         functools.partial(band_kernel, rows=rows, forward=forward),
         [b16(2, 2 * inner, DEPTH), b16(2, 2 * outer, DEPTH)],
-        [place, stencils],
-        [SMEM, VMEM],
-        [
+        [stencils],
+        scratch=[
             pltpu.VMEM(((bases + 1) // 2 * 128, -(-total // 128) * 128), jnp.float32),
             pltpu.VMEM((2, DEPTH // 128, 2, inner, 128), jnp.float32),
             pltpu.VMEM((2, DEPTH // 128, 2, outer, 128), jnp.float32),
@@ -160,7 +158,7 @@
     )
 
 
-def pack(place_ref, field_ref, up_ref, down_ref, first_ref, second_ref, breadth):
+def pack(field_ref, up_ref, down_ref, first_ref, second_ref, breadth):
     height = field_ref.shape[0] // breadth
     margin = up_ref.shape[0] // height
     for row in range(height):
@@ -169,13 +167,13 @@
         down_ref[at, :] = field_ref[row * breadth : row * breadth + margin, :]
     low = field_ref[: margin * breadth, :]
     high = field_ref[(height - margin) * breadth :, :]
-    odd = place_ref[1] == 1
+    odd = lax.axis_index("lat") % 2 == 1
     first_ref[...] = jnp.where(odd, low, high)
     second_ref[...] = jnp.where(odd, high, low)
 
 
-def pack_kernel(place_ref, field_ref, up_ref, down_ref, first_ref, second_ref, kept_ref, *, breadth):
-    pack(place_ref, field_ref, up_ref, down_ref, first_ref, second_ref, breadth)
+def pack_kernel(field_ref, up_ref, down_ref, first_ref, second_ref, kept_ref, *, breadth):
+    pack(field_ref, up_ref, down_ref, first_ref, second_ref, breadth)
     kept_ref[...] = field_ref[...]
 
 
@@ -230,14 +228,14 @@
         shigh_ref[base], slow_ref[base] = split(jnp.concatenate([part[at] for part in got], 0))
 
 
-def outer_kernel(place_ref, first_ref, second_ref, left_ref, right_ref, band_ref, xhigh_ref, xlow_ref,
+def outer_kernel(first_ref, second_ref, left_ref, right_ref, band_ref, xhigh_ref, xlow_ref,
                  shigh_ref, slow_ref, zhigh_ref, zlow_ref, *, breadth):
     margin = first_ref.shape[0] // breadth
     bases, cells = shigh_ref.shape[:2]
     edge = margin * SLOTS
     own = xhigh_ref.shape[0] - 2 * edge
     body = DEPTH - edge
-    odd = place_ref[1] == 1
+    odd = lax.axis_index("lat") % 2 == 1
     tiles = []
     for part, ref in enumerate((first_ref, second_ref)):
         rows = []
@@ -324,7 +322,7 @@
     inner_ref[...] = grad * (1.0 - bounded_ref[...] * bounded_ref[...])
 
 
-def loss_rest(place_ref, own_ref, other_ref, bounded_ref, analysis_ref, before_ref, grad_ref, inner_ref,
+def loss_rest(own_ref, other_ref, bounded_ref, analysis_ref, before_ref, grad_ref, inner_ref,
               up_ref, down_ref, first_ref, second_ref, *, breadth):
     edge = before_ref.shape[1]
     analysis = analysis_ref[:, edge:]
@@ -333,22 +331,22 @@
     grad_ref[...] = grad
     inner_ref[:, :edge] = before_ref[...]
     inner_ref[:, edge:] = grad * (1.0 - bounded_ref[...] * bounded_ref[...])
-    pack(place_ref, inner_ref, up_ref, down_ref, first_ref, second_ref, breadth)
-
-
-def whole_analysis(place_ref, mine_ref, theirs_ref, out_ref):
+    pack(inner_ref, up_ref, down_ref, first_ref, second_ref, breadth)
+
+
+def whole_analysis(mine_ref, theirs_ref, out_ref):
     half = mine_ref.shape[1]
-    first = place_ref[2] == 0
+    first = lax.axis_index("ens") == 0
     mine, theirs = mine_ref[...], theirs_ref[...]
     out_ref[:, :half] = jnp.where(first, mine, theirs)
     out_ref[:, half:] = jnp.where(first, theirs, mine)
 
 
-def crps_kernel(place_ref, own1_ref, own2_ref, other1_ref, other2_ref, mine_ref, out_ref):
+def crps_kernel(own1_ref, own2_ref, other1_ref, other2_ref, mine_ref, out_ref):
     half = mine_ref.shape[1]
     edge = own1_ref.shape[1]
     for part in range(2):
-        @pl.when(place_ref[2] == part)
+        @pl.when(lax.axis_index("ens") == part)
         def _():
             low, high = part * half, (part + 1) * half
             pieces = []
@@ -398,9 +396,6 @@
     flat = members.reshape(cells, channels)
     mine = analysis.reshape(cells, analysis.shape[2])
     rest = channels - EDGE
-    place = jnp.stack([
-        lax.axis_index("lat") * height, lax.axis_index("lat") % 2, lax.axis_index("ens")
-    ]).astype(jnp.int32)
     packed = edges(cells, channels, breadth, margin)
     mix_flops = 6 * cells * bases * channels * channels
     stencil_flops = 6 * bases * cells * DEPTH * channels
@@ -427,16 +422,16 @@
         depth = pltpu.VMEM((2, DEPTH, channels), jnp.bfloat16)
         outer = call(
             functools.partial(outer_kernel, breadth=breadth), taps(outer_cells),
-            [place, first, second, cleft, cright, band[1], xhigh, xlow], [SMEM] + [VMEM] * 7,
-            [depth, depth], flops=stencil_flops * 3 // 10,
+            [first, second, cleft, cright, band[1], xhigh, xlow],
+            scratch=[depth, depth], flops=stencil_flops * 3 // 10,
         )
         return [*inner, *outer]
 
     *sent, flat = call(
         functools.partial(pack_kernel, breadth=breadth), packed + [f32(cells, channels)],
-        [place, flat], [SMEM, VMEM], flops=10**10, size=1 << 20, limit=8,
-    )
-    band = bands(place, stencils, rows, breadth, True)
+        [flat], flops=10**10, size=1 << 20, limit=8,
+    )
+    band = bands(stencils, rows, breadth, True)
     spread0 = spread(*sent, flat, band)
     if pair:
         theirs = lax.ppermute(mine, "ens", SWAP)
@@ -451,12 +446,12 @@
         functools.partial(forward, start=EDGE), [f32(cells, rest)] * 2,
         [*spread0, *weights, flat], flops=mix_flops * rest // channels,
     )
-    back = bands(place, stencils, rows, breadth, False)
+    back = bands(stencils, rows, breadth, False)
     if pair:
         other2 = lax.ppermute(predicted2, "ens", SWAP)
         (known,) = call(
-            whole_analysis, [f32(cells, channels)], [place, mine, theirs],
-            [SMEM, VMEM, VMEM], size=1 << 20, limit=8,
+            whole_analysis, [f32(cells, channels)], [mine, theirs],
+            size=1 << 20, limit=8,
         )
         grad1, inner1 = call(
             loss_first, [f32(cells, EDGE)] * 2,
@@ -465,12 +460,12 @@
         grad2, inner, *sent = call(
             functools.partial(loss_rest, breadth=breadth),
             [f32(cells, rest), f32(cells, channels)] + packed,
-            [place, predicted2, other2, bounded2, known, inner1], [SMEM] + [VMEM] * 5,
+            [predicted2, other2, bounded2, known, inner1],
             size=2 << 20, limit=8,
         )
         (crps,) = call(
             crps_kernel, [f32(*mine.shape)],
-            [place, predicted1, predicted2, other1, other2, mine], [SMEM] + [VMEM] * 5,
+            [predicted1, predicted2, other1, other2, mine],
             size=1 << 20, limit=8,
         )
     else:
@@ -480,7 +475,7 @@
         grad1, grad2 = grad[:, :EDGE], grad[:, EDGE:]
         *sent, inner = call(
             functools.partial(pack_kernel, breadth=breadth), packed + [f32(cells, channels)],
-            [place, inner], [SMEM, VMEM], size=1 << 20, limit=8,
+            [inner], size=1 << 20, limit=8,
         )
     (result,) = call(
         backward, [f32(cells, channels)],

time: 55.7 us -> 52.4 us (0.941)
  the two profiles are of different devices: /device:TPU:1 before, /device:TPU:9 now
where the time goes in v3:
time: 52.4 us; the launch traced here: 52.3 us
  Pallas kernels  19.2 us (37%)
  starting transfers between devices  18.9 us (36%)
  waiting for transfers between devices  12.1 us (23%)
  local copies, waits for them, and re-layouts  1.16 us (2%)
  between operations  0.85 us (2%)
    pallas_call x17, Pallas kernels, call(): pl.pallas_call(body, out_shape=out_shape, in_specs=specs or [VMEM] * len(...  19.2 us
    ppermute x8, starting transfers between devices, ring(): return (lax.ppermute(up, 'lon', there), lax.ppermute(down, 'lon', back))  8.55 us
    ppermute x4, starting transfers between devices, one(): return lax.ppermute(piece, 'lat', sorted(table.items()))  7.59 us
    ppermute x1, waiting for transfers between devices, local(): other1 = lax.ppermute(predicted1, 'ens', SWAP)  7.34 us
    ppermute x8, waiting for transfers between devices, ring(): return (lax.ppermute(up, 'lon', there), lax.ppermute(down, 'lon', back))  4.76 us
    ppermute x1, starting transfers between devices, local(): other1 = lax.ppermute(predicted1, 'ens', SWAP)  1.28 us
    ppermute x1, starting transfers between devices, local(): theirs = lax.ppermute(mine, 'ens', SWAP)  1.21 us
    unnamed x12, local copies, waits for them, and re-layouts  1.16 us
  transfers between devices with their start and end apart: 15, of which 3 were waited for; matrix products, arithmetic and copies ran while one was open for 0% of the time, Pallas kernels for 24%

profile of v3, /device:TPU:9, one launch (start us, length us, event | category | flops | bytes accessed | tf_op | source)
XLA Modules:
  0.0 52.3 jit_solution(513956134029073396)
XLA Ops:
  0.6 0.0 slice-start
  0.6 0.0 copy-start.1
  0.7 1.1 %copy-done.1 = f32[1,20,8,640]{3,2,1,0:T(8,128)S(1)} copy-done((f32[1,20,8,640]{3,2,1,0:T(8,128)S(1)}, f32[1,20,8,640]{3,2,1,0:T(8,128)}, u32[]{:S(2)}) %copy-start.1) | copy-done | bytes 409624
  1.8 0.0 copy-start
  1.8 0.0 slice-start.1
  1.8 0.0 slice-start.2
  1.8 0.1 shard_map.59
  1.9 1.9 %collective-permute-start = (f32[60,640]{1,0:T(8,128)S(1)}, f32[60,640]{1,0:T(8,128)S(1)}, u32[]{:S(2)}, u32[]{:S(2)}) collective-permute-start(f32[60,640]{1,0:T(8,128)S(1)} %get-tuple-element.42), channel_id=1, source_target_pairs={{0,4},{4,8},{8,12},{12,0},{1,5},{5,9},{9,13},{13,1},{2,6},{6,10},{... | collective-permute-start | bytes 460808 | tf_op jit(solution)/shard_map/ppermute | solution.py:260
  3.8 0.0 collective-permute-start.1
  3.8 0.0 copy-done
  3.8 1.2 %collective-permute-start.7 = (f32[160,320]{1,0:T(8,128)S(1)}, f32[160,320]{1,0:T(8,128)S(1)}, u32[]{:S(2)}, u32[]{:S(2)}) collective-permute-start(f32[160,320]{1,0:T(8,128)S(1)} %bitcast.6), channel_id=1, source_target_pairs={{0,16},{16,0},{1,17},{17,1},{2,18},{18,2},{3,19},{19,3},{4,20},{20... | collective-permute-start | bytes 614408 | tf_op jit(solution)/shard_map/ppermute | solution.py:437
  5.0 0.2 collective-permute-start.2
  5.2 0.0 copy-start.2
  5.2 4.5 %collective-permute-start.3 = (f32[24,640]{1,0:T(8,128)S(1)}, f32[24,640]{1,0:T(8,128)S(1)}, u32[]{:S(2)}, u32[]{:S(2)}) collective-permute-start(f32[24,640]{1,0:T(8,128)S(1)} %get-tuple-element.48), channel_id=1, source_target_pairs={{0,0},{1,2},{2,1},{3,3},{4,4},{5,6},{6,5},{7,7},{8,8},{9,10},{10,9... | collective-permute-start | bytes 184328 | tf_op jit(solution)/shard_map/ppermute | solution.py:271
  9.6 0.0 slice-done
  9.6 0.0 slice-done.1
  9.7 0.0 slice-done.2
  9.7 1.7 %shard_map.64 = (bf16[7,640,640]{2,1,0:T(8,128)(2,1)S(1)}, bf16[7,640,640]{2,1,0:T(8,128)(2,1)S(1)}) custom-call(f32[7,640,640]{2,1,0:T(8,128)S(1)} %bitcast.5), custom_call_target="tpu_custom_call" | custom-call | bytes 11468800 | tf_op jit(solution)/shard_map/pallas_call | solution.py:46
  11.3 0.0 copy-done.2
  11.3 1.1 %shard_map.60 = (bf16[2,784,256]{2,1,0:T(8,128)(2,1)S(1)}, bf16[2,336,256]{2,1,0:T(8,128)(2,1)S(1)}) custom-call(f32[7,7,7,80]{3,2,1,0:T(8,128)S(1)} %copy-done.2), custom_call_target="tpu_custom_call" | custom-call | flops 1000000000 | bytes 4194304 | tf_op jit(solution)/shard_map/pallas_call | solution.py:46
  12.5 0.0 collective-permute-done.2.first_ref
  12.5 0.0 collective-permute-done.3.second_ref
  12.5 2.6 %collective-permute-start.4 = (f32[18,640]{1,0:T(8,128)S(1)}, f32[18,640]{1,0:T(8,128)S(1)}, u32[]{:S(2)}, u32[]{:S(2)}) collective-permute-start(f32[18,640]{1,0:T(8,128)S(1)} %get-tuple-element.49), channel_id=1, source_target_pairs={{0,4},{4,8},{8,12},{12,0},{1,5},{5,9},{9,13},{13,1},{2,6},{6,10},{... | collective-permute-start | bytes 138248 | tf_op jit(solution)/shard_map/ppermute | solution.py:260
  15.2 0.0 collective-permute-start.5
  15.2 0.0 collective-permute-done.left_ref
  15.2 0.0 collective-permute-done.1.right_ref
  15.2 1.3 %shard_map.61 = (bf16[416,640]{1,0:T(8,128)(2,1)S(1)}, bf16[416,640]{1,0:T(8,128)(2,1)S(1)}, bf16[7,112,640]{2,1,0:T(8,128)(2,1)S(1)}, bf16[7,112,640]{2,1,0:T(8,128)(2,1)S(1)}) custom-call(f32[160,640]{1,0:T(8,128)S(1)} %get-tuple-element.41.field_ref, f32[60,640]{1,0:T(8,128)S(1)} %collective-permute-done.left_ref, ...), custom_call_target="tpu_custom_call" | custom-call | flops 770703360 | tf_op jit(solution)/shard_map/pallas_call | solution.py:46
  16.4 0.0 collective-permute-done.4.left_ref
  16.5 2.3 %collective-permute-done.5.right_ref = f32[18,640]{1,0:T(8,128)S(1)} collective-permute-done((f32[18,640]{1,0:T(8,128)S(1)}, f32[18,640]{1,0:T(8,128)S(1)}, u32[]{:S(2)}, u32[]{:S(2)}) %collective-permute-start.5) | collective-permute-done | bytes 46112 | tf_op jit(solution)/shard_map/ppermute | solution.py:260
  18.8 0.7 %shard_map.63 = (bf16[7,48,640]{2,1,0:T(8,128)(2,1)S(1)}, bf16[7,48,640]{2,1,0:T(8,128)(2,1)S(1)}) custom-call(f32[24,640]{1,0:T(8,128)S(1)} %collective-permute-done.2.first_ref, f32[24,640]{1,0:T(8,128)S(1)} %collective-permute-done.3.second_ref, f32[18,640]{1,0:T(8,128)S(1)} %collective-permute-done.4.left_ref, ...), custom_call_target="tpu_custom_call" | custom-call | flops 330301440 | tf_op jit(solution)/shard_map/pallas_call | solution.py:46
  19.5 2.7 %shard_map.65 = (f32[160,384]{1,0:T(8,128)S(1)}, f32[160,384]{1,0:T(8,128)S(1)}) custom-call(bf16[7,112,640]{2,1,0:T(8,128)(2,1)S(1)} %get-tuple-element.45.ihigh_ref, bf16[7,112,640]{2,1,0:T(8,128)(2,1)S(1)} %get-tuple-element.46.ilow_ref, bf16[7,48,640]{2,1,0:T(8,128)(2,1)S(1)} %get-tuple-element.54.ohigh_ref, ...), custom_call_target="tpu_custom_call" | custom-call | flops 1651507200 | tf_op jit(solution)/shard_map/pallas_call | solution.py:46
  22.2 0.3 collective-permute-start.6
  22.5 1.5 %shard_map.67 = (f32[160,256]{1,0:T(8,128)S(1)}, f32[160,256]{1,0:T(8,128)S(1)}) custom-call(bf16[7,112,640]{2,1,0:T(8,128)(2,1)S(1)} %get-tuple-element.45.ihigh_ref, bf16[7,112,640]{2,1,0:T(8,128)(2,1)S(1)} %get-tuple-element.46.ilow_ref, bf16[7,48,640]{2,1,0:T(8,128)(2,1)S(1)} %get-tuple-element.54.ohigh_ref, ...), custom_call_target="tpu_custom_call" | custom-call | flops 1101004800 | tf_op jit(solution)/shard_map/pallas_call | solution.py:46
  24.0 1.3 %collective-permute-start.8 = (f32[160,256]{1,0:T(8,128)S(1)}, f32[160,256]{1,0:T(8,128)S(1)}, u32[]{:S(2)}, u32[]{:S(2)}) collective-permute-start(f32[160,256]{1,0:T(8,128)S(1)} %get-tuple-element.60.own_ref.own1_ref), channel_id=1, source_target_pairs={{0,16},{16,0},{1,17},{17,1},{2,18},{18,2},{3,19},{19,3},{4,20},{20... | collective-permute-start | bytes 491528 | tf_op jit(solution)/shard_map/ppermute | solution.py:444
  25.3 0.0 collective-permute-done.7.theirs_ref
  25.3 0.1 shard_map.66.analysis_ref
  25.4 7.3 %collective-permute-done.8.other_ref.other1_ref = f32[160,256]{1,0:T(8,128)S(1)} collective-permute-done((f32[160,256]{1,0:T(8,128)S(1)}, f32[160,256]{1,0:T(8,128)S(1)}, u32[]{:S(2)}, u32[]{:S(2)}) %collective-permute-start.8) | collective-permute-done | bytes 163872 | tf_op jit(solution)/shard_map/ppermute | solution.py:444
  32.8 0.1 shard_map.68
  32.8 0.0 collective-permute-done.6.other_ref.other2_ref
  32.9 0.3 shard_map.69
  33.2 1.5 %collective-permute-start.9 = (f32[60,640]{1,0:T(8,128)S(1)}, f32[60,640]{1,0:T(8,128)S(1)}, u32[]{:S(2)}, u32[]{:S(2)}) collective-permute-start(f32[60,640]{1,0:T(8,128)S(1)} %get-tuple-element.64), channel_id=1, source_target_pairs={{0,4},{4,8},{8,12},{12,0},{1,5},{5,9},{9,13},{13,1},{2,6},{6,10},{... | collective-permute-start | bytes 460808 | tf_op jit(solution)/shard_map/ppermute | solution.py:260
  34.7 0.0 collective-permute-start.10
  34.7 0.0 collective-permute-start.11
  34.7 3.0 %collective-permute-start.12 = (f32[24,640]{1,0:T(8,128)S(1)}, f32[24,640]{1,0:T(8,128)S(1)}, u32[]{:S(2)}, u32[]{:S(2)}) collective-permute-start(f32[24,640]{1,0:T(8,128)S(1)} %get-tuple-element.70), channel_id=1, source_target_pairs={{0,0},{1,2},{2,1},{3,3},{4,4},{5,6},{6,5},{7,7},{8,8},{9,10},{10,9... | collective-permute-start | bytes 184328 | tf_op jit(solution)/shard_map/ppermute | solution.py:271
  37.7 1.2 %shard_map.70 = (bf16[2,784,256]{2,1,0:T(8,128)(2,1)S(1)}, bf16[2,336,256]{2,1,0:T(8,128)(2,1)S(1)}) custom-call(f32[7,7,7,80]{3,2,1,0:T(8,128)S(1)} %copy-done.2), custom_call_target="tpu_custom_call" | custom-call | flops 1000000000 | bytes 4194304 | tf_op jit(solution)/shard_map/pallas_call | solution.py:46
  38.9 1.2 %shard_map.75 = f32[160,320]{1,0:T(8,128)} custom-call(f32[160,256]{1,0:T(8,128)S(1)} %get-tuple-element.60.own_ref.own1_ref, f32[160,384]{1,0:T(8,128)S(1)} %get-tuple-element.58.own_ref.own2_ref, f32[160,256]{1,0:T(8,128)S(1)} %collective-permute-done.8.other_ref.other1_ref, f32[160,384]{1,0:T(8,128)S(1)} %collective-permute-done.6.other_ref.other2_ref, ...), custom_call_target="tpu_custom_call" | custom-call | bytes 1048576 | tf_op jit(solution)/shard_map/pallas_call | solution.py:46
  40.1 0.0 collective-permute-done.11.first_ref
  40.1 0.0 collective-permute-done.12.second_ref
  40.1 2.5 %collective-permute-start.13 = (f32[18,640]{1,0:T(8,128)S(1)}, f32[18,640]{1,0:T(8,128)S(1)}, u32[]{:S(2)}, u32[]{:S(2)}) collective-permute-start(f32[18,640]{1,0:T(8,128)S(1)} %get-tuple-element.71), channel_id=1, source_target_pairs={{0,4},{4,8},{8,12},{12,0},{1,5},{5,9},{9,13},{13,1},{2,6},{6,10},{... | collective-permute-start | bytes 138248 | tf_op jit(solution)/shard_map/ppermute | solution.py:260
  42.6 0.0 collective-permute-start.14
  42.6 0.0 collective-permute-done.9.left_ref
  42.6 0.0 collective-permute-done.10.right_ref
  42.7 1.2 %shard_map.71 = (bf16[416,640]{1,0:T(8,128)(2,1)S(1)}, bf16[416,640]{1,0:T(8,128)(2,1)S(1)}, bf16[7,112,640]{2,1,0:T(8,128)(2,1)S(1)}, bf16[7,112,640]{2,1,0:T(8,128)(2,1)S(1)}) custom-call(f32[160,640]{1,0:T(8,128)S(1)} %get-tuple-element.63.field_ref, f32[60,640]{1,0:T(8,128)S(1)} %collective-permute-done.9.left_ref, ...), custom_call_target="tpu_custom_call" | custom-call | flops 770703360 | tf_op jit(solution)/shard_map/pallas_call | solution.py:46
  43.9 0.0 collective-permute-done.13.left_ref
  43.9 2.4 %collective-permute-done.14.right_ref = f32[18,640]{1,0:T(8,128)S(1)} collective-permute-done((f32[18,640]{1,0:T(8,128)S(1)}, f32[18,640]{1,0:T(8,128)S(1)}, u32[]{:S(2)}, u32[]{:S(2)}) %collective-permute-start.14) | collective-permute-done | bytes 46112 | tf_op jit(solution)/shard_map/ppermute | solution.py:260
  46.3 0.7 %shard_map.73 = (bf16[7,48,640]{2,1,0:T(8,128)(2,1)S(1)}, bf16[7,48,640]{2,1,0:T(8,128)(2,1)S(1)}) custom-call(f32[24,640]{1,0:T(8,128)S(1)} %collective-permute-done.11.first_ref, f32[24,640]{1,0:T(8,128)S(1)} %collective-permute-done.12.second_ref, f32[18,640]{1,0:T(8,128)S(1)} %collective-permute-done.13.left_ref, ...), custom_call_target="tpu_custom_call" | custom-call | flops 330301440 | tf_op jit(solution)/shard_map/pallas_call | solution.py:46
  47.0 5.3 %shard_map.74 = f32[160,640]{1,0:T(8,128)} custom-call(bf16[7,112,640]{2,1,0:T(8,128)(2,1)S(1)} %get-tuple-element.67.ihigh_ref, bf16[7,112,640]{2,1,0:T(8,128)(2,1)S(1)} %get-tuple-element.68.ilow_ref, bf16[7,48,640]{2,1,0:T(8,128)(2,1)S(1)} %get-tuple-element.76.ohigh_ref, bf16[7,48,640]{2,1,0:T(8,128)(2,1)S(1)} %get-tuple-element.77.olow_ref, ...), custom_call_target="tpu_custom_call" | custom-call | flops 2752512000 | tf_op jit(solution)/shard_map/pallas_call | solution.py:46
  (3 shorter events, 0.1 us)
Async XLA Ops:
  0.6 9.0 %slice-start = ((s8[11468800]{0:T(1024)(128)(4,1)}), s8[4194304]{0:T(1024)(128)(4,1)S(1)}, s32[]{:S(2)}) async-start(s8[11468800]{0:T(1024)(128)(4,1)} %bitcast.4), calls=%async_computation | async-start | bytes 8388608
  0.6 1.2 %copy-start.1 = (f32[1,20,8,640]{3,2,1,0:T(8,128)S(1)}, f32[1,20,8,640]{3,2,1,0:T(8,128)}, u32[]{:S(2)}) copy-start(f32[1,20,8,640]{3,2,1,0:T(8,128)} %param.4) | copy-start | bytes 1228804
  1.8 2.0 %copy-start = (f32[20,8,320]{2,1,0:T(8,128)S(1)}, f32[20,8,320]{2,1,0:T(8,128)}, u32[]{:S(2)}) copy-start(f32[20,8,320]{2,1,0:T(8,128)} %param.5) | copy-start | bytes 614404
  1.8 7.8 %slice-start.1 = ((s8[11468800]{0:T(1024)(128)(4,1)}), s8[4194304]{0:T(1024)(128)(4,1)S(1)}, s32[]{:S(2)}) async-start(s8[11468800]{0:T(1024)(128)(4,1)} %bitcast.4), calls=%async_computation.1 | async-start | bytes 8388608
  1.8 7.9 %slice-start.2 = ((s8[11468800]{0:T(1024)(128)(4,1)}), s8[3080192]{0:T(1024)(128)(4,1)S(1)}, s32[]{:S(2)}) async-start(s8[11468800]{0:T(1024)(128)(4,1)} %bitcast.4), calls=%async_computation.2 | async-start | bytes 6160384
  1.9 13.2 %collective-permute-start = (f32[60,640]{1,0:T(8,128)S(1)}, f32[60,640]{1,0:T(8,128)S(1)}, u32[]{:S(2)}, u32[]{:S(2)}) collective-permute-start(f32[60,640]{1,0:T(8,128)S(1)} %get-tuple-element.42), channel_id=1, source_target_pairs={{0,4},{4,8},{8,12},{12,0},{1,5},{5,9},{9,13},{13,1},{2,6},{6,10},{... | collective-permute-start | bytes 460808 | tf_op jit(solution)/shard_map/ppermute | solution.py:260
  3.8 11.4 %collective-permute-start.1 = (f32[60,640]{1,0:T(8,128)S(1)}, f32[60,640]{1,0:T(8,128)S(1)}, u32[]{:S(2)}, u32[]{:S(2)}) collective-permute-start(f32[60,640]{1,0:T(8,128)S(1)} %get-tuple-element.43), channel_id=1, source_target_pairs={{4,0},{8,4},{12,8},{0,12},{5,1},{9,5},{13,9},{1,13},{6,2},{10,6},{... | collective-permute-start | bytes 460808 | tf_op jit(solution)/shard_map/ppermute | solution.py:260
  3.8 21.5 %collective-permute-start.7 = (f32[160,320]{1,0:T(8,128)S(1)}, f32[160,320]{1,0:T(8,128)S(1)}, u32[]{:S(2)}, u32[]{:S(2)}) collective-permute-start(f32[160,320]{1,0:T(8,128)S(1)} %bitcast.6), channel_id=1, source_target_pairs={{0,16},{16,0},{1,17},{17,1},{2,18},{18,2},{3,19},{19,3},{4,20},{20... | collective-permute-start | bytes 614408 | tf_op jit(solution)/shard_map/ppermute | solution.py:437
  5.0 7.5 %collective-permute-start.2 = (f32[24,640]{1,0:T(8,128)S(1)}, f32[24,640]{1,0:T(8,128)S(1)}, u32[]{:S(2)}, u32[]{:S(2)}) collective-permute-start(f32[24,640]{1,0:T(8,128)S(1)} %get-tuple-element.47), channel_id=1, source_target_pairs={{0,1},{1,0},{2,3},{3,2},{4,5},{5,4},{6,7},{7,6},{8,9},{9,8},{10,11... | collective-permute-start | bytes 184328 | tf_op jit(solution)/shard_map/ppermute | solution.py:271
  5.2 6.2 %copy-start.2 = (f32[7,7,7,80]{3,2,1,0:T(8,128)S(1)}, f32[7,7,7,80]{3,2,1,0:T(8,128)}, u32[]{:S(2)}) copy-start(f32[7,7,7,80]{3,2,1,0:T(8,128)} %stencils_ref.3) | copy-start | bytes 329284
  5.2 7.3 %collective-permute-start.3 = (f32[24,640]{1,0:T(8,128)S(1)}, f32[24,640]{1,0:T(8,128)S(1)}, u32[]{:S(2)}, u32[]{:S(2)}) collective-permute-start(f32[24,640]{1,0:T(8,128)S(1)} %get-tuple-element.48), channel_id=1, source_target_pairs={{0,0},{1,2},{2,1},{3,3},{4,4},{5,6},{6,5},{7,7},{8,8},{9,10},{10,9... | collective-permute-start | bytes 184328 | tf_op jit(solution)/shard_map/ppermute | solution.py:271
  12.5 3.9 %collective-permute-start.4 = (f32[18,640]{1,0:T(8,128)S(1)}, f32[18,640]{1,0:T(8,128)S(1)}, u32[]{:S(2)}, u32[]{:S(2)}) collective-permute-start(f32[18,640]{1,0:T(8,128)S(1)} %get-tuple-element.49), channel_id=1, source_target_pairs={{0,4},{4,8},{8,12},{12,0},{1,5},{5,9},{9,13},{13,1},{2,6},{6,10},{... | collective-permute-start | bytes 138248 | tf_op jit(solution)/shard_map/ppermute | solution.py:260
  15.2 3.6 %collective-permute-start.5 = (f32[18,640]{1,0:T(8,128)S(1)}, f32[18,640]{1,0:T(8,128)S(1)}, u32[]{:S(2)}, u32[]{:S(2)}) collective-permute-start(f32[18,640]{1,0:T(8,128)S(1)} %get-tuple-element.50), channel_id=1, source_target_pairs={{4,0},{8,4},{12,8},{0,12},{5,1},{9,5},{13,9},{1,13},{6,2},{10,6},{... | collective-permute-start | bytes 138248 | tf_op jit(solution)/shard_map/ppermute | solution.py:260
  22.2 10.7 %collective-permute-start.6 = (f32[160,384]{1,0:T(8,128)S(1)}, f32[160,384]{1,0:T(8,128)S(1)}, u32[]{:S(2)}, u32[]{:S(2)}) collective-permute-start(f32[160,384]{1,0:T(8,128)S(1)} %get-tuple-element.58.own_ref.own2_ref), channel_id=1, source_target_pairs={{0,16},{16,0},{1,17},{17,1},{2,18},{18,2},{3,19},{19,3},{4,20},{20... | collective-permute-start | bytes 737288 | tf_op jit(solution)/shard_map/ppermute | solution.py:451
  24.0 8.8 %collective-permute-start.8 = (f32[160,256]{1,0:T(8,128)S(1)}, f32[160,256]{1,0:T(8,128)S(1)}, u32[]{:S(2)}, u32[]{:S(2)}) collective-permute-start(f32[160,256]{1,0:T(8,128)S(1)} %get-tuple-element.60.own_ref.own1_ref), channel_id=1, source_target_pairs={{0,16},{16,0},{1,17},{17,1},{2,18},{18,2},{3,19},{19,3},{4,20},{20... | collective-permute-start | bytes 491528 | tf_op jit(solution)/shard_map/ppermute | solution.py:444
  33.2 9.5 %collective-permute-start.9 = (f32[60,640]{1,0:T(8,128)S(1)}, f32[60,640]{1,0:T(8,128)S(1)}, u32[]{:S(2)}, u32[]{:S(2)}) collective-permute-start(f32[60,640]{1,0:T(8,128)S(1)} %get-tuple-element.64), channel_id=1, source_target_pairs={{0,4},{4,8},{8,12},{12,0},{1,5},{5,9},{9,13},{13,1},{2,6},{6,10},{... | collective-permute-start | bytes 460808 | tf_op jit(solution)/shard_map/ppermute | solution.py:260
  34.7 7.9 %collective-permute-start.10 = (f32[60,640]{1,0:T(8,128)S(1)}, f32[60,640]{1,0:T(8,128)S(1)}, u32[]{:S(2)}, u32[]{:S(2)}) collective-permute-start(f32[60,640]{1,0:T(8,128)S(1)} %get-tuple-element.65), channel_id=1, source_target_pairs={{4,0},{8,4},{12,8},{0,12},{5,1},{9,5},{13,9},{1,13},{6,2},{10,6},{... | collective-permute-start | bytes 460808 | tf_op jit(solution)/shard_map/ppermute | solution.py:260
  34.7 5.4 %collective-permute-start.11 = (f32[24,640]{1,0:T(8,128)S(1)}, f32[24,640]{1,0:T(8,128)S(1)}, u32[]{:S(2)}, u32[]{:S(2)}) collective-permute-start(f32[24,640]{1,0:T(8,128)S(1)} %get-tuple-element.69), channel_id=1, source_target_pairs={{0,1},{1,0},{2,3},{3,2},{4,5},{5,4},{6,7},{7,6},{8,9},{9,8},{10,11... | collective-permute-start | bytes 184328 | tf_op jit(solution)/shard_map/ppermute | solution.py:271
  34.7 5.4 %collective-permute-start.12 = (f32[24,640]{1,0:T(8,128)S(1)}, f32[24,640]{1,0:T(8,128)S(1)}, u32[]{:S(2)}, u32[]{:S(2)}) collective-permute-start(f32[24,640]{1,0:T(8,128)S(1)} %get-tuple-element.70), channel_id=1, source_target_pairs={{0,0},{1,2},{2,1},{3,3},{4,4},{5,6},{6,5},{7,7},{8,8},{9,10},{10,9... | collective-permute-start | bytes 184328 | tf_op jit(solution)/shard_map/ppermute | solution.py:271
  40.1 3.8 %collective-permute-start.13 = (f32[18,640]{1,0:T(8,128)S(1)}, f32[18,640]{1,0:T(8,128)S(1)}, u32[]{:S(2)}, u32[]{:S(2)}) collective-permute-start(f32[18,640]{1,0:T(8,128)S(1)} %get-tuple-element.71), channel_id=1, source_target_pairs={{0,4},{4,8},{8,12},{12,0},{1,5},{5,9},{9,13},{13,1},{2,6},{6,10},{... | collective-permute-start | bytes 138248 | tf_op jit(solution)/shard_map/ppermute | solution.py:260
  42.6 3.6 %collective-permute-start.14 = (f32[18,640]{1,0:T(8,128)S(1)}, f32[18,640]{1,0:T(8,128)S(1)}, u32[]{:S(2)}, u32[]{:S(2)}) collective-permute-start(f32[18,640]{1,0:T(8,128)S(1)} %get-tuple-element.72), channel_id=1, source_target_pairs={{4,0},{8,4},{12,8},{0,12},{5,1},{9,5},{13,9},{1,13},{6,2},{10,6},{... | collective-permute-start | bytes 138248 | tf_op jit(solution)/shard_map/ppermute | solution.py:260

commit v4 on v3

--- a/solution.py
+++ b/solution.py
@@ -158,22 +158,32 @@
     )
 
 
-def pack(field_ref, up_ref, down_ref, first_ref, second_ref, breadth):
+def odd_place(axis):
+    return lax.axis_index(axis) % 2 == 1
+
+
+def facing(tile, margin, odd):
+    low, high = tile[:margin], tile[tile.shape[0] - margin :]
+    return jnp.where(odd, high, low), jnp.where(odd, low, high)
+
+
+def pack(field_ref, cross_ref, chip_ref, first_ref, second_ref, breadth):
     height = field_ref.shape[0] // breadth
-    margin = up_ref.shape[0] // height
+    margin = cross_ref.shape[0] // height
+    odd = odd_place("lon")
     for row in range(height):
         at = slice(row * margin, (row + 1) * margin)
-        up_ref[at, :] = field_ref[(row + 1) * breadth - margin : (row + 1) * breadth, :]
-        down_ref[at, :] = field_ref[row * breadth : row * breadth + margin, :]
+        tile = field_ref[row * breadth : (row + 1) * breadth, :]
+        cross_ref[at, :], chip_ref[at, :] = facing(tile, margin, odd)
     low = field_ref[: margin * breadth, :]
     high = field_ref[(height - margin) * breadth :, :]
-    odd = lax.axis_index("lat") % 2 == 1
+    odd = odd_place("lat")
     first_ref[...] = jnp.where(odd, low, high)
     second_ref[...] = jnp.where(odd, high, low)
 
 
-def pack_kernel(field_ref, up_ref, down_ref, first_ref, second_ref, kept_ref, *, breadth):
-    pack(field_ref, up_ref, down_ref, first_ref, second_ref, breadth)
+def pack_kernel(field_ref, cross_ref, chip_ref, first_ref, second_ref, kept_ref, *, breadth):
+    pack(field_ref, cross_ref, chip_ref, first_ref, second_ref, breadth)
     kept_ref[...] = field_ref[...]
 
 
@@ -182,12 +192,19 @@
     return [side, side, row, row]
 
 
-def corner_kernel(first_ref, second_ref, up_ref, down_ref, *, breadth, margin):
+def corner_kernel(first_ref, second_ref, cross_ref, chip_ref, *, breadth, margin):
+    odd = odd_place("lon")
     for part, ref in enumerate((first_ref, second_ref)):
         for row in range(margin):
             at = slice((part * margin + row) * margin, (part * margin + row + 1) * margin)
-            up_ref[at, :] = ref[(row + 1) * breadth - margin : (row + 1) * breadth, :]
-            down_ref[at, :] = ref[row * breadth : row * breadth + margin, :]
+            tile = ref[row * breadth : (row + 1) * breadth, :]
+            cross_ref[at, :], chip_ref[at, :] = facing(tile, margin, odd)
+
+
+def sides_of(cross_ref, chip_ref):
+    odd = odd_place("lon")
+    cross, chip = cross_ref[...], chip_ref[...]
+    return jnp.where(odd, chip, cross), jnp.where(odd, cross, chip)
 
 
 def widen(own, left, right):
@@ -195,9 +212,10 @@
     return jnp.concatenate([own, left, right, spare], 0)
 
 
-def inner_kernel(field_ref, left_ref, right_ref, band_ref, xhigh_ref, xlow_ref, shigh_ref, slow_ref, *, breadth):
+def inner_kernel(field_ref, cross_ref, chip_ref, band_ref, xhigh_ref, xlow_ref, shigh_ref, slow_ref, *, breadth):
     height = field_ref.shape[0] // breadth
-    margin = left_ref.shape[0] // height
+    margin = cross_ref.shape[0] // height
+    left, right = sides_of(cross_ref, chip_ref)
     bases, cells = shigh_ref.shape[:2]
     count = cells // 2
     zeros = jnp.zeros((margin * SLOTS, field_ref.shape[1]), jnp.bfloat16)
@@ -206,7 +224,7 @@
         ref[(margin + height) * SLOTS :, :] = zeros
     for row in range(height):
         here = slice(row * margin, (row + 1) * margin)
-        tile = widen(field_ref[row * breadth : (row + 1) * breadth, :], left_ref[here, :], right_ref[here, :])
+        tile = widen(field_ref[row * breadth : (row + 1) * breadth, :], left[here], right[here])
         at = slice((margin + row) * SLOTS, (margin + row + 1) * SLOTS)
         xhigh_ref[at, :], xlow_ref[at, :] = split(tile)
     got = []
@@ -228,20 +246,21 @@
         shigh_ref[base], slow_ref[base] = split(jnp.concatenate([part[at] for part in got], 0))
 
 
-def outer_kernel(first_ref, second_ref, left_ref, right_ref, band_ref, xhigh_ref, xlow_ref,
+def outer_kernel(first_ref, second_ref, cross_ref, chip_ref, band_ref, xhigh_ref, xlow_ref,
                  shigh_ref, slow_ref, zhigh_ref, zlow_ref, *, breadth):
     margin = first_ref.shape[0] // breadth
     bases, cells = shigh_ref.shape[:2]
     edge = margin * SLOTS
     own = xhigh_ref.shape[0] - 2 * edge
     body = DEPTH - edge
-    odd = lax.axis_index("lat") % 2 == 1
+    left, right = sides_of(cross_ref, chip_ref)
+    odd = odd_place("lat")
     tiles = []
     for part, ref in enumerate((first_ref, second_ref)):
         rows = []
         for row in range(margin):
             here = slice((part * margin + row) * margin, (part * margin + row + 1) * margin)
-            rows.append(widen(ref[row * breadth : (row + 1) * breadth, :], left_ref[here, :], right_ref[here, :]))
+            rows.append(widen(ref[row * breadth : (row + 1) * breadth, :], left[here], right[here]))
         tiles.append(jnp.concatenate(rows, 0))
     low, high = jnp.where(odd, tiles[0], tiles[1]), jnp.where(odd, tiles[1], tiles[0])
     zhigh_ref[0, :edge], zlow_ref[0, :edge] = split(low)
@@ -253,11 +272,12 @@
     keep(got, shigh_ref, slow_ref, bases, cells // 2)
 
 
-def ring(up, down):
+def swap_lon(cross, chip):
     count = lax.axis_size("lon")
-    there = [(i, (i + 1) % count) for i in range(count)]
-    back = [(b, a) for a, b in there]
-    return lax.ppermute(up, "lon", there), lax.ppermute(down, "lon", back)
+    assert count % 2 == 0
+    near = [(i, i ^ 1) for i in range(count)]
+    far = [(i, (i + 1 if i % 2 else i - 1) % count) for i in range(count)]
+    return lax.ppermute(cross, "lon", far), lax.ppermute(chip, "lon", near)
 
 
 def swap(first, second):
@@ -323,7 +343,7 @@
 
 
 def loss_rest(own_ref, other_ref, bounded_ref, analysis_ref, before_ref, grad_ref, inner_ref,
-              up_ref, down_ref, first_ref, second_ref, *, breadth):
+              cross_ref, chip_ref, first_ref, second_ref, *, breadth):
     edge = before_ref.shape[1]
     analysis = analysis_ref[:, edge:]
     own = own_ref[...] - analysis
@@ -331,7 +351,7 @@
     grad_ref[...] = grad
     inner_ref[:, :edge] = before_ref[...]
     inner_ref[:, edge:] = grad * (1.0 - bounded_ref[...] * bounded_ref[...])
-    pack(inner_ref, up_ref, down_ref, first_ref, second_ref, breadth)
+    pack(inner_ref, cross_ref, chip_ref, first_ref, second_ref, breadth)
 
 
 def whole_analysis(mine_ref, theirs_ref, out_ref):
@@ -404,25 +424,25 @@
     def taps(count):
         return [b16(bases, count, channels)] * 2
 
-    def spread(up, down, first, second, field, band):
-        left, right = ring(up, down)
+    def spread(cross, chip, first, second, field, band):
+        cross, chip = swap_lon(cross, chip)
         first, second = swap(first, second)
         corner = f32(2 * margin * margin, channels)
         corners = call(
             functools.partial(corner_kernel, breadth=breadth, margin=margin),
             [corner, corner], [first, second], size=1 << 18, limit=4,
         )
-        cleft, cright = ring(*corners)
+        corners = swap_lon(*corners)
         window = b16((height + 2 * margin) * SLOTS, channels)
         xhigh, xlow, *inner = call(
             functools.partial(inner_kernel, breadth=breadth),
-            [window, window] + taps(inner_cells), [field, left, right, band[0]],
+            [window, window] + taps(inner_cells), [field, cross, chip, band[0]],
             flops=stencil_flops * 7 // 10,
         )
         depth = pltpu.VMEM((2, DEPTH, channels), jnp.bfloat16)
         outer = call(
             functools.partial(outer_kernel, breadth=breadth), taps(outer_cells),
-            [first, second, cleft, cright, band[1], xhigh, xlow],
+            [first, second, *corners, band[1], xhigh, xlow],
             scratch=[depth, depth], flops=stencil_flops * 3 // 10,
         )
         return [*inner, *outer]

time: 52.4 us -> 50 us (0.954)
  the two profiles are of different devices: /device:TPU:9 before, /device:TPU:0 now
where the time goes in v4:
time: 50 us; the launch traced here: 49.8 us
  Pallas kernels  19.2 us (38%)
  starting transfers between devices  17.2 us (34%)
  waiting for transfers between devices  11.4 us (23%)
  local copies, waits for them, and re-layouts  1.16 us (2%)
  between operations  0.87 us (2%)
    pallas_call x17, Pallas kernels, call(): pl.pallas_call(body, out_shape=out_shape, in_specs=specs or [VMEM] * len(...  19.2 us
    ppermute x4, starting transfers between devices, one(): return lax.ppermute(piece, 'lat', sorted(table.items()))  7.41 us
    ppermute x1, waiting for transfers between devices, local(): other1 = lax.ppermute(predicted1, 'ens', SWAP)  7.36 us
    ppermute x8, starting transfers between devices, swap_lon(): return (lax.ppermute(cross, 'lon', far), lax.ppermute(chip, 'lon', near))  6.12 us
    ppermute x8, waiting for transfers between devices, swap_lon(): return (lax.ppermute(cross, 'lon', far), lax.ppermute(chip, 'lon', near))  4.05 us
    ppermute x1, starting transfers between devices, local(): other1 = lax.ppermute(predicted1, 'ens', SWAP)  1.55 us
    ppermute x1, starting transfers between devices, local(): theirs = lax.ppermute(mine, 'ens', SWAP)  1.49 us
    unnamed x12, local copies, waits for them, and re-layouts  1.16 us
  transfers between devices with their start and end apart: 15, of which 3 were waited for; matrix products, arithmetic and copies ran while one was open for 0% of the time, Pallas kernels for 26%

profile of v4, /device:TPU:0, one launch (start us, length us, event | category | flops | bytes accessed | tf_op | source)
XLA Modules:
  0.0 49.8 jit_solution(18063558520127345013)
XLA Ops:
  0.6 0.0 slice-start
  0.6 0.0 copy-start.1
  0.7 1.1 %copy-done.1 = f32[1,20,8,640]{3,2,1,0:T(8,128)S(1)} copy-done((f32[1,20,8,640]{3,2,1,0:T(8,128)S(1)}, f32[1,20,8,640]{3,2,1,0:T(8,128)}, u32[]{:S(2)}) %copy-start.1) | copy-done | bytes 409624
  1.8 0.0 copy-start
  1.8 0.0 slice-start.1
  1.8 0.0 slice-start.2
  1.8 0.1 shard_map.59
  1.9 2.5 %collective-permute-start = (f32[60,640]{1,0:T(8,128)S(1)}, f32[60,640]{1,0:T(8,128)S(1)}, u32[]{:S(2)}, u32[]{:S(2)}) collective-permute-start(f32[60,640]{1,0:T(8,128)S(1)} %get-tuple-element.42), channel_id=1, source_target_pairs={{0,12},{4,8},{8,4},{12,0},{1,13},{5,9},{9,5},{13,1},{2,14},{6,10},... | collective-permute-start | bytes 460808 | tf_op jit(solution)/shard_map/ppermute | solution.py:280
  4.4 0.7 %collective-permute-start.1 = (f32[60,640]{1,0:T(8,128)S(1)}, f32[60,640]{1,0:T(8,128)S(1)}, u32[]{:S(2)}, u32[]{:S(2)}) collective-permute-start(f32[60,640]{1,0:T(8,128)S(1)} %get-tuple-element.43), channel_id=1, source_target_pairs={{0,4},{4,0},{8,12},{12,8},{1,5},{5,1},{9,13},{13,9},{2,6},{6,2},{1... | collective-permute-start | bytes 460808 | tf_op jit(solution)/shard_map/ppermute | solution.py:280
  5.1 0.0 copy-done
  5.1 1.5 %collective-permute-start.7 = (f32[160,320]{1,0:T(8,128)S(1)}, f32[160,320]{1,0:T(8,128)S(1)}, u32[]{:S(2)}, u32[]{:S(2)}) collective-permute-start(f32[160,320]{1,0:T(8,128)S(1)} %bitcast.6), channel_id=1, source_target_pairs={{0,16},{16,0},{1,17},{17,1},{2,18},{18,2},{3,19},{19,3},{4,20},{20... | collective-permute-start | bytes 614408 | tf_op jit(solution)/shard_map/ppermute | solution.py:457
  6.6 1.6 %collective-permute-start.2 = (f32[24,640]{1,0:T(8,128)S(1)}, f32[24,640]{1,0:T(8,128)S(1)}, u32[]{:S(2)}, u32[]{:S(2)}) collective-permute-start(f32[24,640]{1,0:T(8,128)S(1)} %get-tuple-element.47), channel_id=1, source_target_pairs={{0,1},{1,0},{2,3},{3,2},{4,5},{5,4},{6,7},{7,6},{8,9},{9,8},{10,11... | collective-permute-start | bytes 184328 | tf_op jit(solution)/shard_map/ppermute | solution.py:291
  8.2 0.0 copy-start.2
  8.2 0.8 %collective-permute-start.3 = (f32[24,640]{1,0:T(8,128)S(1)}, f32[24,640]{1,0:T(8,128)S(1)}, u32[]{:S(2)}, u32[]{:S(2)}) collective-permute-start(f32[24,640]{1,0:T(8,128)S(1)} %get-tuple-element.48), channel_id=1, source_target_pairs={{0,0},{1,2},{2,1},{3,3},{4,4},{5,6},{6,5},{7,7},{8,8},{9,10},{10,9... | collective-permute-start | bytes 184328 | tf_op jit(solution)/shard_map/ppermute | solution.py:291
  9.0 0.0 slice-done
  9.0 0.0 slice-done.1
  9.0 0.0 slice-done.2
  9.0 1.7 %shard_map.64 = (bf16[7,640,640]{2,1,0:T(8,128)(2,1)S(1)}, bf16[7,640,640]{2,1,0:T(8,128)(2,1)S(1)}) custom-call(f32[7,640,640]{2,1,0:T(8,128)S(1)} %bitcast.5), custom_call_target="tpu_custom_call" | custom-call | bytes 11468800 | tf_op jit(solution)/shard_map/pallas_call | solution.py:46
  10.7 0.0 copy-done.2
  10.7 1.1 %shard_map.60 = (bf16[2,784,256]{2,1,0:T(8,128)(2,1)S(1)}, bf16[2,336,256]{2,1,0:T(8,128)(2,1)S(1)}) custom-call(f32[7,7,7,80]{3,2,1,0:T(8,128)S(1)} %copy-done.2), custom_call_target="tpu_custom_call" | custom-call | flops 1000000000 | bytes 4194304 | tf_op jit(solution)/shard_map/pallas_call | solution.py:46
  11.8 0.0 collective-permute-done.2.first_ref
  11.8 0.0 collective-permute-done.3.second_ref
  11.9 0.1 collective-permute-start.4
  11.9 1.0 %collective-permute-start.5 = (f32[18,640]{1,0:T(8,128)S(1)}, f32[18,640]{1,0:T(8,128)S(1)}, u32[]{:S(2)}, u32[]{:S(2)}) collective-permute-start(f32[18,640]{1,0:T(8,128)S(1)} %get-tuple-element.50), channel_id=1, source_target_pairs={{0,4},{4,0},{8,12},{12,8},{1,5},{5,1},{9,13},{13,9},{2,6},{6,2},{1... | collective-permute-start | bytes 138248 | tf_op jit(solution)/shard_map/ppermute | solution.py:280
  12.9 0.0 collective-permute-done.cross_ref
  12.9 0.0 collective-permute-done.1.chip_ref
  12.9 1.3 %shard_map.61 = (bf16[416,640]{1,0:T(8,128)(2,1)S(1)}, bf16[416,640]{1,0:T(8,128)(2,1)S(1)}, bf16[7,112,640]{2,1,0:T(8,128)(2,1)S(1)}, bf16[7,112,640]{2,1,0:T(8,128)(2,1)S(1)}) custom-call(f32[160,640]{1,0:T(8,128)S(1)} %get-tuple-element.41.field_ref, f32[60,640]{1,0:T(8,128)S(1)} %collective-permute-done.cross_ref, ...), custom_call_target="tpu_custom_call" | custom-call | flops 770703360 | tf_op jit(solution)/shard_map/pallas_call | solution.py:46
  14.2 1.7 %collective-permute-done.4.cross_ref = f32[18,640]{1,0:T(8,128)S(1)} collective-permute-done((f32[18,640]{1,0:T(8,128)S(1)}, f32[18,640]{1,0:T(8,128)S(1)}, u32[]{:S(2)}, u32[]{:S(2)}) %collective-permute-start.4) | collective-permute-done | bytes 46112 | tf_op jit(solution)/shard_map/ppermute | solution.py:280
  15.9 0.0 collective-permute-done.5.chip_ref
  15.9 0.7 %shard_map.63 = (bf16[7,48,640]{2,1,0:T(8,128)(2,1)S(1)}, bf16[7,48,640]{2,1,0:T(8,128)(2,1)S(1)}) custom-call(f32[24,640]{1,0:T(8,128)S(1)} %collective-permute-done.2.first_ref, f32[24,640]{1,0:T(8,128)S(1)} %collective-permute-done.3.second_ref, f32[18,640]{1,0:T(8,128)S(1)} %collective-permute-done.4.cross_ref, ...), custom_call_target="tpu_custom_call" | custom-call | flops 330301440 | tf_op jit(solution)/shard_map/pallas_call | solution.py:46
  16.5 2.7 %shard_map.65 = (f32[160,384]{1,0:T(8,128)S(1)}, f32[160,384]{1,0:T(8,128)S(1)}) custom-call(bf16[7,112,640]{2,1,0:T(8,128)(2,1)S(1)} %get-tuple-element.45.ihigh_ref, bf16[7,112,640]{2,1,0:T(8,128)(2,1)S(1)} %get-tuple-element.46.ilow_ref, bf16[7,48,640]{2,1,0:T(8,128)(2,1)S(1)} %get-tuple-element.54.ohigh_ref, ...), custom_call_target="tpu_custom_call" | custom-call | flops 1651507200 | tf_op jit(solution)/shard_map/pallas_call | solution.py:46
  19.2 0.6 %collective-permute-start.6 = (f32[160,384]{1,0:T(8,128)S(1)}, f32[160,384]{1,0:T(8,128)S(1)}, u32[]{:S(2)}, u32[]{:S(2)}) collective-permute-start(f32[160,384]{1,0:T(8,128)S(1)} %get-tuple-element.58.own_ref.own2_ref), channel_id=1, source_target_pairs={{0,16},{16,0},{1,17},{17,1},{2,18},{18,2},{3,19},{19,3},{4,20},{20... | collective-permute-start | bytes 737288 | tf_op jit(solution)/shard_map/ppermute | solution.py:471
  19.8 1.5 %shard_map.67 = (f32[160,256]{1,0:T(8,128)S(1)}, f32[160,256]{1,0:T(8,128)S(1)}) custom-call(bf16[7,112,640]{2,1,0:T(8,128)(2,1)S(1)} %get-tuple-element.45.ihigh_ref, bf16[7,112,640]{2,1,0:T(8,128)(2,1)S(1)} %get-tuple-element.46.ilow_ref, bf16[7,48,640]{2,1,0:T(8,128)(2,1)S(1)} %get-tuple-element.54.ohigh_ref, ...), custom_call_target="tpu_custom_call" | custom-call | flops 1101004800 | tf_op jit(solution)/shard_map/pallas_call | solution.py:46
  21.3 1.6 %collective-permute-start.8 = (f32[160,256]{1,0:T(8,128)S(1)}, f32[160,256]{1,0:T(8,128)S(1)}, u32[]{:S(2)}, u32[]{:S(2)}) collective-permute-start(f32[160,256]{1,0:T(8,128)S(1)} %get-tuple-element.60.own_ref.own1_ref), channel_id=1, source_target_pairs={{0,16},{16,0},{1,17},{17,1},{2,18},{18,2},{3,19},{19,3},{4,20},{20... | collective-permute-start | bytes 491528 | tf_op jit(solution)/shard_map/ppermute | solution.py:464
  22.9 0.0 collective-permute-done.7.theirs_ref
  22.9 0.1 shard_map.66.analysis_ref
  23.0 7.4 %collective-permute-done.8.other_ref.other1_ref = f32[160,256]{1,0:T(8,128)S(1)} collective-permute-done((f32[160,256]{1,0:T(8,128)S(1)}, f32[160,256]{1,0:T(8,128)S(1)}, u32[]{:S(2)}, u32[]{:S(2)}) %collective-permute-start.8) | collective-permute-done | bytes 163872 | tf_op jit(solution)/shard_map/ppermute | solution.py:464
  30.4 0.1 shard_map.68
  30.5 0.0 collective-permute-done.6.other_ref.other2_ref
  30.5 0.3 shard_map.69
  30.8 0.1 collective-permute-start.9
  30.9 1.2 %collective-permute-start.10 = (f32[60,640]{1,0:T(8,128)S(1)}, f32[60,640]{1,0:T(8,128)S(1)}, u32[]{:S(2)}, u32[]{:S(2)}) collective-permute-start(f32[60,640]{1,0:T(8,128)S(1)} %get-tuple-element.65), channel_id=1, source_target_pairs={{0,4},{4,0},{8,12},{12,8},{1,5},{5,1},{9,13},{13,9},{2,6},{6,2},{1... | collective-permute-start | bytes 460808 | tf_op jit(solution)/shard_map/ppermute | solution.py:280
  32.1 4.4 %collective-permute-start.11 = (f32[24,640]{1,0:T(8,128)S(1)}, f32[24,640]{1,0:T(8,128)S(1)}, u32[]{:S(2)}, u32[]{:S(2)}) collective-permute-start(f32[24,640]{1,0:T(8,128)S(1)} %get-tuple-element.69), channel_id=1, source_target_pairs={{0,1},{1,0},{2,3},{3,2},{4,5},{5,4},{6,7},{7,6},{8,9},{9,8},{10,11... | collective-permute-start | bytes 184328 | tf_op jit(solution)/shard_map/ppermute | solution.py:291
  36.5 0.7 %collective-permute-start.12 = (f32[24,640]{1,0:T(8,128)S(1)}, f32[24,640]{1,0:T(8,128)S(1)}, u32[]{:S(2)}, u32[]{:S(2)}) collective-permute-start(f32[24,640]{1,0:T(8,128)S(1)} %get-tuple-element.70), channel_id=1, source_target_pairs={{0,0},{1,2},{2,1},{3,3},{4,4},{5,6},{6,5},{7,7},{8,8},{9,10},{10,9... | collective-permute-start | bytes 184328 | tf_op jit(solution)/shard_map/ppermute | solution.py:291
  37.1 1.2 %shard_map.70 = (bf16[2,784,256]{2,1,0:T(8,128)(2,1)S(1)}, bf16[2,336,256]{2,1,0:T(8,128)(2,1)S(1)}) custom-call(f32[7,7,7,80]{3,2,1,0:T(8,128)S(1)} %copy-done.2), custom_call_target="tpu_custom_call" | custom-call | flops 1000000000 | bytes 4194304 | tf_op jit(solution)/shard_map/pallas_call | solution.py:46
  38.3 1.2 %shard_map.75 = f32[160,320]{1,0:T(8,128)} custom-call(f32[160,256]{1,0:T(8,128)S(1)} %get-tuple-element.60.own_ref.own1_ref, f32[160,384]{1,0:T(8,128)S(1)} %get-tuple-element.58.own_ref.own2_ref, f32[160,256]{1,0:T(8,128)S(1)} %collective-permute-done.8.other_ref.other1_ref, f32[160,384]{1,0:T(8,128)S(1)} %collective-permute-done.6.other_ref.other2_ref, ...), custom_call_target="tpu_custom_call" | custom-call | bytes 1048576 | tf_op jit(solution)/shard_map/pallas_call | solution.py:46
  39.5 0.0 collective-permute-done.11.first_ref
  39.5 0.0 collective-permute-done.12.second_ref
  39.6 0.1 collective-permute-start.13
  39.7 0.6 %collective-permute-start.14 = (f32[18,640]{1,0:T(8,128)S(1)}, f32[18,640]{1,0:T(8,128)S(1)}, u32[]{:S(2)}, u32[]{:S(2)}) collective-permute-start(f32[18,640]{1,0:T(8,128)S(1)} %get-tuple-element.72), channel_id=1, source_target_pairs={{0,4},{4,0},{8,12},{12,8},{1,5},{5,1},{9,13},{13,9},{2,6},{6,2},{1... | collective-permute-start | bytes 138248 | tf_op jit(solution)/shard_map/ppermute | solution.py:280
  40.3 0.0 collective-permute-done.9.cross_ref
  40.3 0.0 collective-permute-done.10.chip_ref
  40.3 1.2 %shard_map.71 = (bf16[416,640]{1,0:T(8,128)(2,1)S(1)}, bf16[416,640]{1,0:T(8,128)(2,1)S(1)}, bf16[7,112,640]{2,1,0:T(8,128)(2,1)S(1)}, bf16[7,112,640]{2,1,0:T(8,128)(2,1)S(1)}) custom-call(f32[160,640]{1,0:T(8,128)S(1)} %get-tuple-element.63.field_ref, f32[60,640]{1,0:T(8,128)S(1)} %collective-permute-done.9.cross_ref, ...), custom_call_target="tpu_custom_call" | custom-call | flops 770703360 | tf_op jit(solution)/shard_map/pallas_call | solution.py:46
  41.5 2.3 %collective-permute-done.13.cross_ref = f32[18,640]{1,0:T(8,128)S(1)} collective-permute-done((f32[18,640]{1,0:T(8,128)S(1)}, f32[18,640]{1,0:T(8,128)S(1)}, u32[]{:S(2)}, u32[]{:S(2)}) %collective-permute-start.13) | collective-permute-done | bytes 46112 | tf_op jit(solution)/shard_map/ppermute | solution.py:280
  43.9 0.0 collective-permute-done.14.chip_ref
  43.9 0.7 %shard_map.73 = (bf16[7,48,640]{2,1,0:T(8,128)(2,1)S(1)}, bf16[7,48,640]{2,1,0:T(8,128)(2,1)S(1)}) custom-call(f32[24,640]{1,0:T(8,128)S(1)} %collective-permute-done.11.first_ref, f32[24,640]{1,0:T(8,128)S(1)} %collective-permute-done.12.second_ref, f32[18,640]{1,0:T(8,128)S(1)} %collective-permute-done.13.cross_ref, ...), custom_call_target="tpu_custom_call" | custom-call | flops 330301440 | tf_op jit(solution)/shard_map/pallas_call | solution.py:46
  44.5 5.3 %shard_map.74 = f32[160,640]{1,0:T(8,128)} custom-call(bf16[7,112,640]{2,1,0:T(8,128)(2,1)S(1)} %get-tuple-element.67.ihigh_ref, bf16[7,112,640]{2,1,0:T(8,128)(2,1)S(1)} %get-tuple-element.68.ilow_ref, bf16[7,48,640]{2,1,0:T(8,128)(2,1)S(1)} %get-tuple-element.76.ohigh_ref, bf16[7,48,640]{2,1,0:T(8,128)(2,1)S(1)} %get-tuple-element.77.olow_ref, ...), custom_call_target="tpu_custom_call" | custom-call | flops 2752512000 | tf_op jit(solution)/shard_map/pallas_call | solution.py:46
  (3 shorter events, 0.1 us)
Async XLA Ops:
  0.6 8.3 %slice-start = ((s8[11468800]{0:T(1024)(128)(4,1)}), s8[4194304]{0:T(1024)(128)(4,1)S(1)}, s32[]{:S(2)}) async-start(s8[11468800]{0:T(1024)(128)(4,1)} %bitcast.4), calls=%async_computation | async-start | bytes 8388608
  0.6 1.2 %copy-start.1 = (f32[1,20,8,640]{3,2,1,0:T(8,128)S(1)}, f32[1,20,8,640]{3,2,1,0:T(8,128)}, u32[]{:S(2)}) copy-start(f32[1,20,8,640]{3,2,1,0:T(8,128)} %param.4) | copy-start | bytes 1228804
  1.8 3.3 %copy-start = (f32[20,8,320]{2,1,0:T(8,128)S(1)}, f32[20,8,320]{2,1,0:T(8,128)}, u32[]{:S(2)}) copy-start(f32[20,8,320]{2,1,0:T(8,128)} %param.5) | copy-start | bytes 614404
  1.8 7.2 %slice-start.1 = ((s8[11468800]{0:T(1024)(128)(4,1)}), s8[4194304]{0:T(1024)(128)(4,1)S(1)}, s32[]{:S(2)}) async-start(s8[11468800]{0:T(1024)(128)(4,1)} %bitcast.4), calls=%async_computation.1 | async-start | bytes 8388608
  1.8 7.2 %slice-start.2 = ((s8[11468800]{0:T(1024)(128)(4,1)}), s8[3080192]{0:T(1024)(128)(4,1)S(1)}, s32[]{:S(2)}) async-start(s8[11468800]{0:T(1024)(128)(4,1)} %bitcast.4), calls=%async_computation.2 | async-start | bytes 6160384
  1.9 11.0 %collective-permute-start = (f32[60,640]{1,0:T(8,128)S(1)}, f32[60,640]{1,0:T(8,128)S(1)}, u32[]{:S(2)}, u32[]{:S(2)}) collective-permute-start(f32[60,640]{1,0:T(8,128)S(1)} %get-tuple-element.42), channel_id=1, source_target_pairs={{0,12},{4,8},{8,4},{12,0},{1,13},{5,9},{9,5},{13,1},{2,14},{6,10},... | collective-permute-start | bytes 460808 | tf_op jit(solution)/shard_map/ppermute | solution.py:280
  4.4 8.5 %collective-permute-start.1 = (f32[60,640]{1,0:T(8,128)S(1)}, f32[60,640]{1,0:T(8,128)S(1)}, u32[]{:S(2)}, u32[]{:S(2)}) collective-permute-start(f32[60,640]{1,0:T(8,128)S(1)} %get-tuple-element.43), channel_id=1, source_target_pairs={{0,4},{4,0},{8,12},{12,8},{1,5},{5,1},{9,13},{13,9},{2,6},{6,2},{1... | collective-permute-start | bytes 460808 | tf_op jit(solution)/shard_map/ppermute | solution.py:280
  5.1 17.8 %collective-permute-start.7 = (f32[160,320]{1,0:T(8,128)S(1)}, f32[160,320]{1,0:T(8,128)S(1)}, u32[]{:S(2)}, u32[]{:S(2)}) collective-permute-start(f32[160,320]{1,0:T(8,128)S(1)} %bitcast.6), channel_id=1, source_target_pairs={{0,16},{16,0},{1,17},{17,1},{2,18},{18,2},{3,19},{19,3},{4,20},{20... | collective-permute-start | bytes 614408 | tf_op jit(solution)/shard_map/ppermute | solution.py:457
  6.6 5.2 %collective-permute-start.2 = (f32[24,640]{1,0:T(8,128)S(1)}, f32[24,640]{1,0:T(8,128)S(1)}, u32[]{:S(2)}, u32[]{:S(2)}) collective-permute-start(f32[24,640]{1,0:T(8,128)S(1)} %get-tuple-element.47), channel_id=1, source_target_pairs={{0,1},{1,0},{2,3},{3,2},{4,5},{5,4},{6,7},{7,6},{8,9},{9,8},{10,11... | collective-permute-start | bytes 184328 | tf_op jit(solution)/shard_map/ppermute | solution.py:291
  8.2 2.5 %copy-start.2 = (f32[7,7,7,80]{3,2,1,0:T(8,128)S(1)}, f32[7,7,7,80]{3,2,1,0:T(8,128)}, u32[]{:S(2)}) copy-start(f32[7,7,7,80]{3,2,1,0:T(8,128)} %stencils_ref.3) | copy-start | bytes 329284
  8.2 3.6 %collective-permute-start.3 = (f32[24,640]{1,0:T(8,128)S(1)}, f32[24,640]{1,0:T(8,128)S(1)}, u32[]{:S(2)}, u32[]{:S(2)}) collective-permute-start(f32[24,640]{1,0:T(8,128)S(1)} %get-tuple-element.48), channel_id=1, source_target_pairs={{0,0},{1,2},{2,1},{3,3},{4,4},{5,6},{6,5},{7,7},{8,8},{9,10},{10,9... | collective-permute-start | bytes 184328 | tf_op jit(solution)/shard_map/ppermute | solution.py:291
  11.9 4.0 %collective-permute-start.4 = (f32[18,640]{1,0:T(8,128)S(1)}, f32[18,640]{1,0:T(8,128)S(1)}, u32[]{:S(2)}, u32[]{:S(2)}) collective-permute-start(f32[18,640]{1,0:T(8,128)S(1)} %get-tuple-element.49), channel_id=1, source_target_pairs={{0,12},{4,8},{8,4},{12,0},{1,13},{5,9},{9,5},{13,1},{2,14},{6,10},... | collective-permute-start | bytes 138248 | tf_op jit(solution)/shard_map/ppermute | solution.py:280
  11.9 3.9 %collective-permute-start.5 = (f32[18,640]{1,0:T(8,128)S(1)}, f32[18,640]{1,0:T(8,128)S(1)}, u32[]{:S(2)}, u32[]{:S(2)}) collective-permute-start(f32[18,640]{1,0:T(8,128)S(1)} %get-tuple-element.50), channel_id=1, source_target_pairs={{0,4},{4,0},{8,12},{12,8},{1,5},{5,1},{9,13},{13,9},{2,6},{6,2},{1... | collective-permute-start | bytes 138248 | tf_op jit(solution)/shard_map/ppermute | solution.py:280
  19.2 11.3 %collective-permute-start.6 = (f32[160,384]{1,0:T(8,128)S(1)}, f32[160,384]{1,0:T(8,128)S(1)}, u32[]{:S(2)}, u32[]{:S(2)}) collective-permute-start(f32[160,384]{1,0:T(8,128)S(1)} %get-tuple-element.58.own_ref.own2_ref), channel_id=1, source_target_pairs={{0,16},{16,0},{1,17},{17,1},{2,18},{18,2},{3,19},{19,3},{4,20},{20... | collective-permute-start | bytes 737288 | tf_op jit(solution)/shard_map/ppermute | solution.py:471
  21.3 9.1 %collective-permute-start.8 = (f32[160,256]{1,0:T(8,128)S(1)}, f32[160,256]{1,0:T(8,128)S(1)}, u32[]{:S(2)}, u32[]{:S(2)}) collective-permute-start(f32[160,256]{1,0:T(8,128)S(1)} %get-tuple-element.60.own_ref.own1_ref), channel_id=1, source_target_pairs={{0,16},{16,0},{1,17},{17,1},{2,18},{18,2},{3,19},{19,3},{4,20},{20... | collective-permute-start | bytes 491528 | tf_op jit(solution)/shard_map/ppermute | solution.py:464
  30.8 9.4 %collective-permute-start.9 = (f32[60,640]{1,0:T(8,128)S(1)}, f32[60,640]{1,0:T(8,128)S(1)}, u32[]{:S(2)}, u32[]{:S(2)}) collective-permute-start(f32[60,640]{1,0:T(8,128)S(1)} %get-tuple-element.64), channel_id=1, source_target_pairs={{0,12},{4,8},{8,4},{12,0},{1,13},{5,9},{9,5},{13,1},{2,14},{6,10},... | collective-permute-start | bytes 460808 | tf_op jit(solution)/shard_map/ppermute | solution.py:280
  30.9 9.4 %collective-permute-start.10 = (f32[60,640]{1,0:T(8,128)S(1)}, f32[60,640]{1,0:T(8,128)S(1)}, u32[]{:S(2)}, u32[]{:S(2)}) collective-permute-start(f32[60,640]{1,0:T(8,128)S(1)} %get-tuple-element.65), channel_id=1, source_target_pairs={{0,4},{4,0},{8,12},{12,8},{1,5},{5,1},{9,13},{13,9},{2,6},{6,2},{1... | collective-permute-start | bytes 460808 | tf_op jit(solution)/shard_map/ppermute | solution.py:280
  32.1 7.4 %collective-permute-start.11 = (f32[24,640]{1,0:T(8,128)S(1)}, f32[24,640]{1,0:T(8,128)S(1)}, u32[]{:S(2)}, u32[]{:S(2)}) collective-permute-start(f32[24,640]{1,0:T(8,128)S(1)} %get-tuple-element.69), channel_id=1, source_target_pairs={{0,1},{1,0},{2,3},{3,2},{4,5},{5,4},{6,7},{7,6},{8,9},{9,8},{10,11... | collective-permute-start | bytes 184328 | tf_op jit(solution)/shard_map/ppermute | solution.py:291
  36.5 3.0 %collective-permute-start.12 = (f32[24,640]{1,0:T(8,128)S(1)}, f32[24,640]{1,0:T(8,128)S(1)}, u32[]{:S(2)}, u32[]{:S(2)}) collective-permute-start(f32[24,640]{1,0:T(8,128)S(1)} %get-tuple-element.70), channel_id=1, source_target_pairs={{0,0},{1,2},{2,1},{3,3},{4,4},{5,6},{6,5},{7,7},{8,8},{9,10},{10,9... | collective-permute-start | bytes 184328 | tf_op jit(solution)/shard_map/ppermute | solution.py:291
  39.6 4.3 %collective-permute-start.13 = (f32[18,640]{1,0:T(8,128)S(1)}, f32[18,640]{1,0:T(8,128)S(1)}, u32[]{:S(2)}, u32[]{:S(2)}) collective-permute-start(f32[18,640]{1,0:T(8,128)S(1)} %get-tuple-element.71), channel_id=1, source_target_pairs={{0,12},{4,8},{8,4},{12,0},{1,13},{5,9},{9,5},{13,1},{2,14},{6,10},... | collective-permute-start | bytes 138248 | tf_op jit(solution)/shard_map/ppermute | solution.py:280
  39.7 4.2 %collective-permute-start.14 = (f32[18,640]{1,0:T(8,128)S(1)}, f32[18,640]{1,0:T(8,128)S(1)}, u32[]{:S(2)}, u32[]{:S(2)}) collective-permute-start(f32[18,640]{1,0:T(8,128)S(1)} %get-tuple-element.72), channel_id=1, source_target_pairs={{0,4},{4,0},{8,12},{12,8},{1,5},{5,1},{9,13},{13,9},{2,6},{6,2},{1... | collective-permute-start | bytes 138248 | tf_op jit(solution)/shard_map/ppermute | solution.py:280

commit v5 on v4

--- a/solution.py
+++ b/solution.py
@@ -11,7 +11,7 @@
 SMOOTH = 0.01
 SLOTS = 16
 DEPTH = 256
-EDGE = 256
+CHUNKS = (2, 2)
 SWAP = [(0, 1), (1, 0)]
 VMEM = pl.BlockSpec(memory_space=pltpu.VMEM)
 
@@ -293,19 +293,21 @@
     return (one(first, range(0, count, 2)), one(second, range(1, count, 2)))
 
 
-def split_mixing(mixing_ref, high_ref, low_ref):
+def split_mixing(mixing_ref, high_ref, low_ref, *, start):
+    lanes = slice(start, start + high_ref.shape[2])
     for base in range(mixing_ref.shape[0]):
-        high_ref[base], low_ref[base] = split(mixing_ref[base])
-
-
-def contract(taps, mhigh_ref, mlow_ref, lanes, axis):
+        high_ref[base], low_ref[base] = split(mixing_ref[base, :, lanes])
+
+
+def contract(taps, parts, axis):
     inner_high, inner_low, outer_high, outer_low = taps
     total = None
-    for base in range(mhigh_ref.shape[0]):
-        high = jnp.concatenate([inner_high[base], outer_high[base]], 0)
-        low = jnp.concatenate([inner_low[base], outer_low[base]], 0)
-        part = product3(high, low, mhigh_ref[base, :, lanes], mlow_ref[base, :, lanes], axis)
-        total = part if total is None else total + part
+    for high_ref, low_ref, lanes in parts:
+        for base in range(high_ref.shape[0]):
+            high = jnp.concatenate([inner_high[base, :, lanes], outer_high[base, :, lanes]], 0)
+            low = jnp.concatenate([inner_low[base, :, lanes], outer_low[base, :, lanes]], 0)
+            part = product3(high, low, high_ref[base], low_ref[base], axis)
+            total = part if total is None else total + part
     edge = outer_high.shape[1] // 2
     inner = inner_high.shape[1]
     return jnp.concatenate([total[inner : inner + edge], total[:inner], total[inner + edge :]], 0)
@@ -313,17 +315,23 @@
 
 def forward(ihigh_ref, ilow_ref, ohigh_ref, olow_ref, mhigh_ref, mlow_ref, field_ref, predicted_ref, bounded_ref, *, start):
     lanes = slice(start, start + predicted_ref.shape[1])
-    total = contract((ihigh_ref, ilow_ref, ohigh_ref, olow_ref), mhigh_ref, mlow_ref, lanes, 0)
+    taps = (ihigh_ref, ilow_ref, ohigh_ref, olow_ref)
+    total = contract(taps, [(mhigh_ref, mlow_ref, slice(None))], 0)
     bounded = jnp.tanh(total)
     bounded_ref[...] = bounded
     predicted_ref[...] = field_ref[:, lanes] + bounded
 
 
-def backward(ihigh_ref, ilow_ref, ohigh_ref, olow_ref, mhigh_ref, mlow_ref, grad_ref, tail_ref, out_ref):
-    total = contract((ihigh_ref, ilow_ref, ohigh_ref, olow_ref), mhigh_ref, mlow_ref, slice(None), 1)
-    edge = grad_ref.shape[1]
-    out_ref[:, :edge] = total[:, :edge] + grad_ref[...]
-    out_ref[:, edge:] = total[:, edge:] + tail_ref[...]
+def backward(*refs):
+    taps, rest, out_ref = refs[:4], refs[4:-1], refs[-1]
+    grads, weights = rest[: len(rest) // 3], rest[len(rest) // 3 :]
+    parts, start = [], 0
+    for high_ref, low_ref in zip(weights[::2], weights[1::2]):
+        parts.append((high_ref, low_ref, slice(start, start + high_ref.shape[2])))
+        start += high_ref.shape[2]
+    total = contract(taps, parts, 1)
+    for grad_ref, (_, _, lanes) in zip(grads, parts):
+        out_ref[:, lanes] = total[:, lanes] + grad_ref[...]
 
 
 def slope(value):
@@ -334,23 +342,24 @@
     return jnp.sqrt(value * value + SMOOTH)
 
 
-def loss_first(own_ref, other_ref, bounded_ref, analysis_ref, grad_ref, inner_ref):
-    analysis = analysis_ref[:, : own_ref.shape[1]]
+def loss(own_ref, other_ref, bounded_ref, analysis_ref, start):
+    analysis = analysis_ref[:, start : start + own_ref.shape[1]]
     own = own_ref[...] - analysis
     grad = slope(own) - slope(own - (other_ref[...] - analysis))
-    grad_ref[...] = grad
-    inner_ref[...] = grad * (1.0 - bounded_ref[...] * bounded_ref[...])
-
-
-def loss_rest(own_ref, other_ref, bounded_ref, analysis_ref, before_ref, grad_ref, inner_ref,
-              cross_ref, chip_ref, first_ref, second_ref, *, breadth):
-    edge = before_ref.shape[1]
-    analysis = analysis_ref[:, edge:]
-    own = own_ref[...] - analysis
-    grad = slope(own) - slope(own - (other_ref[...] - analysis))
-    grad_ref[...] = grad
-    inner_ref[:, :edge] = before_ref[...]
-    inner_ref[:, edge:] = grad * (1.0 - bounded_ref[...] * bounded_ref[...])
+    return grad, grad * (1.0 - bounded_ref[...] * bounded_ref[...])
+
+
+def loss_part(own_ref, other_ref, bounded_ref, analysis_ref, grad_ref, inner_ref, *, start):
+    grad_ref[...], inner_ref[...] = loss(own_ref, other_ref, bounded_ref, analysis_ref, start)
+
+
+def loss_last(own_ref, other_ref, bounded_ref, analysis_ref, *rest, breadth):
+    before, (grad_ref, inner_ref, cross_ref, chip_ref, first_ref, second_ref) = rest[:-6], rest[-6:]
+    start = 0
+    for ref in before:
+        inner_ref[:, start : start + ref.shape[1]] = ref[...]
+        start += ref.shape[1]
+    grad_ref[...], inner_ref[:, start:] = loss(own_ref, other_ref, bounded_ref, analysis_ref, start)
     pack(inner_ref, cross_ref, chip_ref, first_ref, second_ref, breadth)
 
 
@@ -362,27 +371,28 @@
     out_ref[:, half:] = jnp.where(first, theirs, mine)
 
 
-def crps_kernel(own1_ref, own2_ref, other1_ref, other2_ref, mine_ref, out_ref):
+def crps_kernel(*refs):
+    mine_ref, out_ref = refs[-2:]
+    owns, others = refs[: len(refs) // 2 - 1], refs[len(refs) // 2 - 1 : -2]
     half = mine_ref.shape[1]
-    edge = own1_ref.shape[1]
     for part in range(2):
         @pl.when(lax.axis_index("ens") == part)
         def _():
             low, high = part * half, (part + 1) * half
-            pieces = []
-            if low < edge:
-                pieces.append((own1_ref, other1_ref, slice(low, min(high, edge)), 0))
-            if high > edge:
-                start = max(low, edge)
-                pieces.append((own2_ref, other2_ref, slice(start - edge, high - edge), start - low))
-            for own_ref, other_ref, lanes, at in pieces:
-                here = slice(at, at + lanes.stop - lanes.start)
-                mine = mine_ref[:, here]
-                own = own_ref[:, lanes] - mine
-                other = other_ref[:, lanes] - mine
-                gap = own - other
-                pair = 2.0 * (soft(gap) + jnp.sqrt(jnp.full_like(gap, SMOOTH)))
-                out_ref[:, here] = 0.5 * (soft(own) + soft(other)) - pair / 4.0
+            start = 0
+            for own_ref, other_ref in zip(owns, others):
+                stop = start + own_ref.shape[1]
+                begin, end = max(low, start), min(high, stop)
+                if begin < end:
+                    here = slice(begin - low, end - low)
+                    lanes = slice(begin - start, end - start)
+                    mine = mine_ref[:, here]
+                    own = own_ref[:, lanes] - mine
+                    other = other_ref[:, lanes] - mine
+                    gap = own - other
+                    pair = 2.0 * (soft(gap) + jnp.sqrt(jnp.full_like(gap, SMOOTH)))
+                    out_ref[:, here] = 0.5 * (soft(own) + soft(other)) - pair / 4.0
+                start = stop
 
 
 def loss_many(predicted, bounded, analysis):
@@ -415,7 +425,10 @@
     pair = lax.axis_size("ens") == 2
     flat = members.reshape(cells, channels)
     mine = analysis.reshape(cells, analysis.shape[2])
-    rest = channels - EDGE
+    widths = [128 * n for n in CHUNKS]
+    widths.append(channels - sum(widths))
+    starts = [sum(widths[:n]) for n in range(len(widths))]
+    assert widths[-1] > 0
     packed = edges(cells, channels, breadth, margin)
     mix_flops = 6 * cells * bases * channels * channels
     stencil_flops = 6 * bases * cells * DEPTH * channels
@@ -455,51 +468,58 @@
     spread0 = spread(*sent, flat, band)
     if pair:
         theirs = lax.ppermute(mine, "ens", SWAP)
-    weights = call(split_mixing, [b16(*mixing.shape)] * 2, [mixing], size=mixing.size * 4)
-    predicted1, bounded1 = call(
-        functools.partial(forward, start=0), [f32(cells, EDGE)] * 2,
-        [*spread0, *weights, flat], flops=mix_flops * EDGE // channels,
-    )
-    if pair:
-        other1 = lax.ppermute(predicted1, "ens", SWAP)
-    predicted2, bounded2 = call(
-        functools.partial(forward, start=EDGE), [f32(cells, rest)] * 2,
-        [*spread0, *weights, flat], flops=mix_flops * rest // channels,
-    )
+    weights, predicted, bounded, others = [], [], [], []
+    for start, width in zip(starts, widths):
+        weights += call(
+            functools.partial(split_mixing, start=start),
+            [b16(bases, channels, width)] * 2, [mixing], size=bases * channels * width * 4,
+        )
+        ahead, tanh = call(
+            functools.partial(forward, start=start), [f32(cells, width)] * 2,
+            [*spread0, *weights[-2:], flat], flops=mix_flops * width // channels,
+        )
+        predicted.append(ahead)
+        bounded.append(tanh)
+        if pair:
+            others.append(lax.ppermute(ahead, "ens", SWAP))
     back = bands(stencils, rows, breadth, False)
     if pair:
-        other2 = lax.ppermute(predicted2, "ens", SWAP)
         (known,) = call(
             whole_analysis, [f32(cells, channels)], [mine, theirs],
             size=1 << 20, limit=8,
         )
-        grad1, inner1 = call(
-            loss_first, [f32(cells, EDGE)] * 2,
-            [predicted1, other1, bounded1, known], size=1 << 20, limit=8,
-        )
-        grad2, inner, *sent = call(
-            functools.partial(loss_rest, breadth=breadth),
-            [f32(cells, rest), f32(cells, channels)] + packed,
-            [predicted2, other2, bounded2, known, inner1],
-            size=2 << 20, limit=8,
-        )
+        grads, inners = [], []
+        for n, (start, width) in enumerate(zip(starts, widths)):
+            pieces = [predicted[n], others[n], bounded[n], known]
+            if n < len(widths) - 1:
+                grad, inner = call(
+                    functools.partial(loss_part, start=start),
+                    [f32(cells, width)] * 2, pieces, size=1 << 20, limit=8,
+                )
+                inners.append(inner)
+            else:
+                grad, inner, *sent = call(
+                    functools.partial(loss_last, breadth=breadth),
+                    [f32(cells, width), f32(cells, channels)] + packed, pieces + inners,
+                    size=2 << 20, limit=8,
+                )
+            grads.append(grad)
         (crps,) = call(
-            crps_kernel, [f32(*mine.shape)],
-            [predicted1, predicted2, other1, other2, mine],
+            crps_kernel, [f32(*mine.shape)], [*predicted, *others, mine],
             size=1 << 20, limit=8,
         )
     else:
-        predicted = jnp.concatenate([predicted1, predicted2], 1)
-        bounded = jnp.concatenate([bounded1, bounded2], 1)
-        grad, inner, crps = loss_many(predicted, bounded, mine)
-        grad1, grad2 = grad[:, :EDGE], grad[:, EDGE:]
+        grad, inner, crps = loss_many(
+            jnp.concatenate(predicted, 1), jnp.concatenate(bounded, 1), mine
+        )
+        grads = [grad[:, start : start + width] for start, width in zip(starts, widths)]
         *sent, inner = call(
             functools.partial(pack_kernel, breadth=breadth), packed + [f32(cells, channels)],
             [inner], size=1 << 20, limit=8,
         )
     (result,) = call(
         backward, [f32(cells, channels)],
-        [*spread(*sent, inner, back), *weights, grad1, grad2], flops=mix_flops,
+        [*spread(*sent, inner, back), *grads, *weights], flops=mix_flops,
     )
     return result.reshape(members.shape), crps.reshape(analysis.shape)
 

time: 50 us -> 48.6 us (0.972)
  waiting for transfers between devices: 11.4 us -> 9.64 us
    ppermute x2 -> x3, waiting for transfers between devices: 7.36 us -> 4.86 us  [local(): others.append(lax.ppermute(ahead, 'ens', SWAP))]
    ppermute x8, waiting for transfers between devices: 4.05 us -> 4.76 us  [swap_lon(): return (lax.ppermute(cross, 'lon', far), lax.ppermute(chip, 'lon', near))]
    ppermute x2 -> x3, starting transfers between devices: 2.16 us -> 2.76 us  [local(): others.append(lax.ppermute(ahead, 'ens', SWAP))]
    pallas_call x17 -> x21, Pallas kernels: 19.2 us -> 19.4 us  [call(): pl.pallas_call(body, out_shape=out_shape, in_specs=specs or [VMEM] * len(...]
  transfers between devices with their start and end apart: 15 -> 16, of which waited for: 3 -> 5; matrix products, arithmetic and copies ran while one was open for 0% -> 0% of each run, Pallas kernels for 26% -> 28%
where the time goes in v5:
time: 48.6 us; the launch traced here: 48.4 us
  Pallas kernels  19.4 us (40%)
  starting transfers between devices  17.3 us (36%)
  waiting for transfers between devices  9.64 us (20%)
  local copies, waits for them, and re-layouts  1.23 us (3%)
  between operations  0.86 us (2%)
    pallas_call x21, Pallas kernels, call(): pl.pallas_call(body, out_shape=out_shape, in_specs=specs or [VMEM] * len(...  19.4 us
    ppermute x4, starting transfers between devices, one(): return lax.ppermute(piece, 'lat', sorted(table.items()))  7.28 us
    ppermute x8, starting transfers between devices, swap_lon(): return (lax.ppermute(cross, 'lon', far), lax.ppermute(chip, 'lon', near))  5.66 us
    ppermute x3, waiting for transfers between devices, local(): others.append(lax.ppermute(ahead, 'ens', SWAP))  4.86 us
    ppermute x8, waiting for transfers between devices, swap_lon(): return (lax.ppermute(cross, 'lon', far), lax.ppermute(chip, 'lon', near))  4.76 us
    ppermute x3, starting transfers between devices, local(): others.append(lax.ppermute(ahead, 'ens', SWAP))  2.76 us
    ppermute x1, starting transfers between devices, local(): theirs = lax.ppermute(mine, 'ens', SWAP)  1.56 us
    unnamed x12, local copies, waits for them, and re-layouts  1.23 us
  transfers between devices with their start and end apart: 16, of which 5 were waited for; matrix products, arithmetic and copies ran while one was open for 0% of the time, Pallas kernels for 28%

profile of v5, /device:TPU:0, one launch (start us, length us, event | category | flops | bytes accessed | tf_op | source)
XLA Modules:
  0.0 48.4 jit_solution(2588386608343117864)
XLA Ops:
  0.6 0.0 slice-start
  0.6 0.0 copy-start.1
  0.7 1.1 %copy-done.1 = f32[1,20,8,640]{3,2,1,0:T(8,128)S(1)} copy-done((f32[1,20,8,640]{3,2,1,0:T(8,128)S(1)}, f32[1,20,8,640]{3,2,1,0:T(8,128)}, u32[]{:S(2)}) %copy-start.1) | copy-done | bytes 409624
  1.8 0.0 copy-start
  1.8 0.0 slice-start.1
  1.8 0.0 slice-start.2
  1.8 0.1 shard_map.59
  1.9 2.5 %collective-permute-start = (f32[60,640]{1,0:T(8,128)S(1)}, f32[60,640]{1,0:T(8,128)S(1)}, u32[]{:S(2)}, u32[]{:S(2)}) collective-permute-start(f32[60,640]{1,0:T(8,128)S(1)} %get-tuple-element.50), channel_id=1, source_target_pairs={{0,12},{4,8},{8,4},{12,0},{1,13},{5,9},{9,5},{13,1},{2,14},{6,10},... | collective-permute-start | bytes 460808 | tf_op jit(solution)/shard_map/ppermute | solution.py:280
  4.4 0.7 %collective-permute-start.1 = (f32[60,640]{1,0:T(8,128)S(1)}, f32[60,640]{1,0:T(8,128)S(1)}, u32[]{:S(2)}, u32[]{:S(2)}) collective-permute-start(f32[60,640]{1,0:T(8,128)S(1)} %get-tuple-element.51), channel_id=1, source_target_pairs={{0,4},{4,0},{8,12},{12,8},{1,5},{5,1},{9,13},{13,9},{2,6},{6,2},{1... | collective-permute-start | bytes 460808 | tf_op jit(solution)/shard_map/ppermute | solution.py:280
  5.1 1.6 %collective-permute-start.2 = (f32[24,640]{1,0:T(8,128)S(1)}, f32[24,640]{1,0:T(8,128)S(1)}, u32[]{:S(2)}, u32[]{:S(2)}) collective-permute-start(f32[24,640]{1,0:T(8,128)S(1)} %get-tuple-element.55), channel_id=1, source_target_pairs={{0,1},{1,0},{2,3},{3,2},{4,5},{5,4},{6,7},{7,6},{8,9},{9,8},{10,11... | collective-permute-start | bytes 184328 | tf_op jit(solution)/shard_map/ppermute | solution.py:291
  6.7 0.7 %collective-permute-start.3 = (f32[24,640]{1,0:T(8,128)S(1)}, f32[24,640]{1,0:T(8,128)S(1)}, u32[]{:S(2)}, u32[]{:S(2)}) collective-permute-start(f32[24,640]{1,0:T(8,128)S(1)} %get-tuple-element.56), channel_id=1, source_target_pairs={{0,0},{1,2},{2,1},{3,3},{4,4},{5,6},{6,5},{7,7},{8,8},{9,10},{10,9... | collective-permute-start | bytes 184328 | tf_op jit(solution)/shard_map/ppermute | solution.py:291
  7.3 0.0 copy-done
  7.4 1.6 %collective-permute-start.7 = (f32[160,320]{1,0:T(8,128)S(1)}, f32[160,320]{1,0:T(8,128)S(1)}, u32[]{:S(2)}, u32[]{:S(2)}) collective-permute-start(f32[160,320]{1,0:T(8,128)S(1)} %bitcast.6), channel_id=1, source_target_pairs={{0,16},{16,0},{1,17},{17,1},{2,18},{18,2},{3,19},{19,3},{4,20},{20... | collective-permute-start | bytes 614408 | tf_op jit(solution)/shard_map/ppermute | solution.py:470
  8.9 0.0 slice-done
  8.9 0.0 slice-done.1
  8.9 0.0 slice-done.2
  8.9 0.8 %shard_map.70 = (bf16[7,640,256]{2,1,0:T(8,128)(2,1)S(1)}, bf16[7,640,256]{2,1,0:T(8,128)(2,1)S(1)}) custom-call(f32[7,640,640]{2,1,0:T(8,128)S(1)} %bitcast.5), custom_call_target="tpu_custom_call" | custom-call | bytes 4587520 | tf_op jit(solution)/shard_map/pallas_call | solution.py:46
  9.8 0.0 copy-start.2
  9.8 0.8 %shard_map.67 = (bf16[7,640,256]{2,1,0:T(8,128)(2,1)S(1)}, bf16[7,640,256]{2,1,0:T(8,128)(2,1)S(1)}) custom-call(f32[7,640,640]{2,1,0:T(8,128)S(1)} %bitcast.5), custom_call_target="tpu_custom_call" | custom-call | bytes 4587520 | tf_op jit(solution)/shard_map/pallas_call | solution.py:46
  10.6 0.1 copy-done.2
  10.7 1.1 %shard_map.60 = (bf16[2,784,256]{2,1,0:T(8,128)(2,1)S(1)}, bf16[2,336,256]{2,1,0:T(8,128)(2,1)S(1)}) custom-call(f32[7,7,7,80]{3,2,1,0:T(8,128)S(1)} %copy-done.2), custom_call_target="tpu_custom_call" | custom-call | flops 1000000000 | bytes 4194304 | tf_op jit(solution)/shard_map/pallas_call | solution.py:46
  11.8 0.0 collective-permute-done.2.first_ref
  11.8 0.0 collective-permute-done.3.second_ref
  11.9 0.1 collective-permute-start.4
  12.0 0.7 %collective-permute-start.5 = (f32[18,640]{1,0:T(8,128)S(1)}, f32[18,640]{1,0:T(8,128)S(1)}, u32[]{:S(2)}, u32[]{:S(2)}) collective-permute-start(f32[18,640]{1,0:T(8,128)S(1)} %get-tuple-element.58), channel_id=1, source_target_pairs={{0,4},{4,0},{8,12},{12,8},{1,5},{5,1},{9,13},{13,9},{2,6},{6,2},{1... | collective-permute-start | bytes 138248 | tf_op jit(solution)/shard_map/ppermute | solution.py:280
  12.7 0.0 collective-permute-done.cross_ref
  12.7 0.0 collective-permute-done.1.chip_ref
  12.7 1.2 %shard_map.61 = (bf16[416,640]{1,0:T(8,128)(2,1)S(1)}, bf16[416,640]{1,0:T(8,128)(2,1)S(1)}, bf16[7,112,640]{2,1,0:T(8,128)(2,1)S(1)}, bf16[7,112,640]{2,1,0:T(8,128)(2,1)S(1)}) custom-call(f32[160,640]{1,0:T(8,128)S(1)} %get-tuple-element.49.field_ref, f32[60,640]{1,0:T(8,128)S(1)} %collective-permute-done.cross_ref, ...), custom_call_target="tpu_custom_call" | custom-call | flops 770703360 | tf_op jit(solution)/shard_map/pallas_call | solution.py:46
  13.9 1.9 %collective-permute-done.4.cross_ref = f32[18,640]{1,0:T(8,128)S(1)} collective-permute-done((f32[18,640]{1,0:T(8,128)S(1)}, f32[18,640]{1,0:T(8,128)S(1)}, u32[]{:S(2)}, u32[]{:S(2)}) %collective-permute-start.4) | collective-permute-done | bytes 46112 | tf_op jit(solution)/shard_map/ppermute | solution.py:280
  15.9 0.0 collective-permute-done.5.chip_ref
  15.9 0.7 %shard_map.63 = (bf16[7,48,640]{2,1,0:T(8,128)(2,1)S(1)}, bf16[7,48,640]{2,1,0:T(8,128)(2,1)S(1)}) custom-call(f32[24,640]{1,0:T(8,128)S(1)} %collective-permute-done.2.first_ref, f32[24,640]{1,0:T(8,128)S(1)} %collective-permute-done.3.second_ref, f32[18,640]{1,0:T(8,128)S(1)} %collective-permute-done.4.cross_ref, ...), custom_call_target="tpu_custom_call" | custom-call | flops 330301440 | tf_op jit(solution)/shard_map/pallas_call | solution.py:46
  16.6 1.5 %shard_map.71 = (f32[160,256]{1,0:T(8,128)S(1)}, f32[160,256]{1,0:T(8,128)S(1)}) custom-call(bf16[7,112,640]{2,1,0:T(8,128)(2,1)S(1)} %get-tuple-element.53.ihigh_ref, bf16[7,112,640]{2,1,0:T(8,128)(2,1)S(1)} %get-tuple-element.54.ilow_ref, bf16[7,48,640]{2,1,0:T(8,128)(2,1)S(1)} %get-tuple-element.62.ohigh_ref, ...), custom_call_target="tpu_custom_call" | custom-call | flops 1101004800 | tf_op jit(solution)/shard_map/pallas_call | solution.py:46
  18.1 0.6 %collective-permute-start.9 = (f32[160,256]{1,0:T(8,128)S(1)}, f32[160,256]{1,0:T(8,128)S(1)}, u32[]{:S(2)}, u32[]{:S(2)}) collective-permute-start(f32[160,256]{1,0:T(8,128)S(1)} %get-tuple-element.75.own_ref.refs_1_), channel_id=1, source_target_pairs={{0,16},{16,0},{1,17},{17,1},{2,18},{18,2},{3,19},{19,3},{4,20},{20... | collective-permute-start | bytes 491528 | tf_op jit(solution)/shard_map/ppermute | solution.py:484
  18.7 1.5 %shard_map.68 = (f32[160,256]{1,0:T(8,128)S(1)}, f32[160,256]{1,0:T(8,128)S(1)}) custom-call(bf16[7,112,640]{2,1,0:T(8,128)(2,1)S(1)} %get-tuple-element.53.ihigh_ref, bf16[7,112,640]{2,1,0:T(8,128)(2,1)S(1)} %get-tuple-element.54.ilow_ref, bf16[7,48,640]{2,1,0:T(8,128)(2,1)S(1)} %get-tuple-element.62.ohigh_ref, ...), custom_call_target="tpu_custom_call" | custom-call | flops 1101004800 | tf_op jit(solution)/shard_map/pallas_call | solution.py:46
  20.2 1.6 %collective-permute-start.8 = (f32[160,256]{1,0:T(8,128)S(1)}, f32[160,256]{1,0:T(8,128)S(1)}, u32[]{:S(2)}, u32[]{:S(2)}) collective-permute-start(f32[160,256]{1,0:T(8,128)S(1)} %get-tuple-element.70.own_ref.refs_0_), channel_id=1, source_target_pairs={{0,16},{16,0},{1,17},{17,1},{2,18},{18,2},{3,19},{19,3},{4,20},{20... | collective-permute-start | bytes 491528 | tf_op jit(solution)/shard_map/ppermute | solution.py:484
  21.8 0.3 shard_map.64
  22.1 1.3 %shard_map.65 = (f32[160,128]{1,0:T(8,128)S(1)}, f32[160,128]{1,0:T(8,128)S(1)}) custom-call(bf16[7,112,640]{2,1,0:T(8,128)(2,1)S(1)} %get-tuple-element.53.ihigh_ref, bf16[7,112,640]{2,1,0:T(8,128)(2,1)S(1)} %get-tuple-element.54.ilow_ref, bf16[7,48,640]{2,1,0:T(8,128)(2,1)S(1)} %get-tuple-element.62.ohigh_ref, ...), custom_call_target="tpu_custom_call" | custom-call | flops 550502400 | tf_op jit(solution)/shard_map/pallas_call | solution.py:46
  23.4 0.6 %collective-permute-start.6 = (f32[160,128]{1,0:T(8,128)S(1)}, f32[160,128]{1,0:T(8,128)S(1)}, u32[]{:S(2)}, u32[]{:S(2)}) collective-permute-start(f32[160,128]{1,0:T(8,128)S(1)} %get-tuple-element.66.own_ref.refs_2_), channel_id=1, source_target_pairs={{0,16},{16,0},{1,17},{17,1},{2,18},{18,2},{3,19},{19,3},{4,20},{20... | collective-permute-start | bytes 245768 | tf_op jit(solution)/shard_map/ppermute | solution.py:484
  24.0 0.0 collective-permute-done.7.theirs_ref
  24.0 0.1 shard_map.66.analysis_ref
  24.2 1.0 %collective-permute-done.9.other_ref.refs_4_ = f32[160,256]{1,0:T(8,128)S(1)} collective-permute-done((f32[160,256]{1,0:T(8,128)S(1)}, f32[160,256]{1,0:T(8,128)S(1)}, u32[]{:S(2)}, u32[]{:S(2)}) %collective-permute-start.9) | collective-permute-done | bytes 163872 | tf_op jit(solution)/shard_map/ppermute | solution.py:484
  25.2 0.1 shard_map.72
  25.3 3.0 %collective-permute-done.8.other_ref.refs_3_ = f32[160,256]{1,0:T(8,128)S(1)} collective-permute-done((f32[160,256]{1,0:T(8,128)S(1)}, f32[160,256]{1,0:T(8,128)S(1)}, u32[]{:S(2)}, u32[]{:S(2)}) %collective-permute-start.8) | collective-permute-done | bytes 163872 | tf_op jit(solution)/shard_map/ppermute | solution.py:484
  28.4 0.1 shard_map.69
  28.5 0.8 %collective-permute-done.6.other_ref.refs_5_ = f32[160,128]{1,0:T(8,128)S(1)} collective-permute-done((f32[160,128]{1,0:T(8,128)S(1)}, f32[160,128]{1,0:T(8,128)S(1)}, u32[]{:S(2)}, u32[]{:S(2)}) %collective-permute-start.6) | collective-permute-done | bytes 81952 | tf_op jit(solution)/shard_map/ppermute | solution.py:484
  29.3 0.2 shard_map.73
  29.4 0.2 collective-permute-start.10
  29.6 1.3 %collective-permute-start.11 = (f32[60,640]{1,0:T(8,128)S(1)}, f32[60,640]{1,0:T(8,128)S(1)}, u32[]{:S(2)}, u32[]{:S(2)}) collective-permute-start(f32[60,640]{1,0:T(8,128)S(1)} %get-tuple-element.80), channel_id=1, source_target_pairs={{0,4},{4,0},{8,12},{12,8},{1,5},{5,1},{9,13},{13,9},{2,6},{6,2},{1... | collective-permute-start | bytes 460808 | tf_op jit(solution)/shard_map/ppermute | solution.py:280
  30.9 4.4 %collective-permute-start.12 = (f32[24,640]{1,0:T(8,128)S(1)}, f32[24,640]{1,0:T(8,128)S(1)}, u32[]{:S(2)}, u32[]{:S(2)}) collective-permute-start(f32[24,640]{1,0:T(8,128)S(1)} %get-tuple-element.84), channel_id=1, source_target_pairs={{0,1},{1,0},{2,3},{3,2},{4,5},{5,4},{6,7},{7,6},{8,9},{9,8},{10,11... | collective-permute-start | bytes 184328 | tf_op jit(solution)/shard_map/ppermute | solution.py:291
  35.3 0.7 %collective-permute-start.13 = (f32[24,640]{1,0:T(8,128)S(1)}, f32[24,640]{1,0:T(8,128)S(1)}, u32[]{:S(2)}, u32[]{:S(2)}) collective-permute-start(f32[24,640]{1,0:T(8,128)S(1)} %get-tuple-element.85), channel_id=1, source_target_pairs={{0,0},{1,2},{2,1},{3,3},{4,4},{5,6},{6,5},{7,7},{8,8},{9,10},{10,9... | collective-permute-start | bytes 184328 | tf_op jit(solution)/shard_map/ppermute | solution.py:291
  35.9 1.2 %shard_map.74 = (bf16[2,784,256]{2,1,0:T(8,128)(2,1)S(1)}, bf16[2,336,256]{2,1,0:T(8,128)(2,1)S(1)}) custom-call(f32[7,7,7,80]{3,2,1,0:T(8,128)S(1)} %copy-done.2), custom_call_target="tpu_custom_call" | custom-call | flops 1000000000 | bytes 4194304 | tf_op jit(solution)/shard_map/pallas_call | solution.py:46
  37.1 1.2 %shard_map.79 = f32[160,320]{1,0:T(8,128)} custom-call(f32[160,256]{1,0:T(8,128)S(1)} %get-tuple-element.70.own_ref.refs_0_, f32[160,256]{1,0:T(8,128)S(1)} %get-tuple-element.75.own_ref.refs_1_, f32[160,128]{1,0:T(8,128)S(1)} %get-tuple-element.66.own_ref.refs_2_, f32[160,256]{1,0:T(8,128)S(1)} %collective-permute-done.8.other_ref.refs_3_, ...), custom_call_target="tpu_custom_call" | custom-call | bytes 1048576 | tf_op jit(solution)/shard_map/pallas_call | solution.py:46
  38.3 0.0 collective-permute-done.12.first_ref
  38.3 0.0 collective-permute-done.13.second_ref
  38.4 0.1 collective-permute-start.14
  38.5 0.1 collective-permute-start.15
  38.6 0.0 collective-permute-done.10.cross_ref
  38.6 0.0 collective-permute-done.11.chip_ref
  38.6 1.2 %shard_map.75 = (bf16[416,640]{1,0:T(8,128)(2,1)S(1)}, bf16[416,640]{1,0:T(8,128)(2,1)S(1)}, bf16[7,112,640]{2,1,0:T(8,128)(2,1)S(1)}, bf16[7,112,640]{2,1,0:T(8,128)(2,1)S(1)}) custom-call(f32[160,640]{1,0:T(8,128)S(1)} %get-tuple-element.78.field_ref, f32[60,640]{1,0:T(8,128)S(1)} %collective-permute-done.10.cross_ref, ...), custom_call_target="tpu_custom_call" | custom-call | flops 770703360 | tf_op jit(solution)/shard_map/pallas_call | solution.py:46
  39.9 2.8 %collective-permute-done.14.cross_ref = f32[18,640]{1,0:T(8,128)S(1)} collective-permute-done((f32[18,640]{1,0:T(8,128)S(1)}, f32[18,640]{1,0:T(8,128)S(1)}, u32[]{:S(2)}, u32[]{:S(2)}) %collective-permute-start.14) | collective-permute-done | bytes 46112 | tf_op jit(solution)/shard_map/ppermute | solution.py:280
  42.7 0.0 collective-permute-done.15.chip_ref
  42.7 0.7 %shard_map.77 = (bf16[7,48,640]{2,1,0:T(8,128)(2,1)S(1)}, bf16[7,48,640]{2,1,0:T(8,128)(2,1)S(1)}) custom-call(f32[24,640]{1,0:T(8,128)S(1)} %collective-permute-done.12.first_ref, f32[24,640]{1,0:T(8,128)S(1)} %collective-permute-done.13.second_ref, f32[18,640]{1,0:T(8,128)S(1)} %collective-permute-done.14.cross_ref, ...), custom_call_target="tpu_custom_call" | custom-call | flops 330301440 | tf_op jit(solution)/shard_map/pallas_call | solution.py:46
  43.3 5.1 %shard_map.78 = f32[160,640]{1,0:T(8,128)} custom-call(bf16[7,112,640]{2,1,0:T(8,128)(2,1)S(1)} %get-tuple-element.82.refs_0_, bf16[7,112,640]{2,1,0:T(8,128)(2,1)S(1)} %get-tuple-element.83.refs_1_, bf16[7,48,640]{2,1,0:T(8,128)(2,1)S(1)} %get-tuple-element.91.refs_2_, bf16[7,48,640]{2,1,0:T(8,128)(2,1)S(1)} %get-tuple-element.92.refs_3_, ...), custom_call_target="tpu_custom_call" | custom-call | flops 2752512000 | tf_op jit(solution)/shard_map/pallas_call | solution.py:46
  (3 shorter events, 0.1 us)
Async XLA Ops:
  0.6 8.3 %slice-start = ((s8[11468800]{0:T(1024)(128)(4,1)}), s8[4194304]{0:T(1024)(128)(4,1)S(1)}, s32[]{:S(2)}) async-start(s8[11468800]{0:T(1024)(128)(4,1)} %bitcast.4), calls=%async_computation | async-start | bytes 8388608
  0.6 1.2 %copy-start.1 = (f32[1,20,8,640]{3,2,1,0:T(8,128)S(1)}, f32[1,20,8,640]{3,2,1,0:T(8,128)}, u32[]{:S(2)}) copy-start(f32[1,20,8,640]{3,2,1,0:T(8,128)} %param.4) | copy-start | bytes 1228804
  1.8 5.6 %copy-start = (f32[20,8,320]{2,1,0:T(8,128)S(1)}, f32[20,8,320]{2,1,0:T(8,128)}, u32[]{:S(2)}) copy-start(f32[20,8,320]{2,1,0:T(8,128)} %param.5) | copy-start | bytes 614404
  1.8 7.1 %slice-start.1 = ((s8[11468800]{0:T(1024)(128)(4,1)}), s8[4194304]{0:T(1024)(128)(4,1)S(1)}, s32[]{:S(2)}) async-start(s8[11468800]{0:T(1024)(128)(4,1)} %bitcast.4), calls=%async_computation.1 | async-start | bytes 8388608
  1.8 7.1 %slice-start.2 = ((s8[11468800]{0:T(1024)(128)(4,1)}), s8[3080192]{0:T(1024)(128)(4,1)S(1)}, s32[]{:S(2)}) async-start(s8[11468800]{0:T(1024)(128)(4,1)} %bitcast.4), calls=%async_computation.2 | async-start | bytes 6160384
  1.9 10.8 %collective-permute-start = (f32[60,640]{1,0:T(8,128)S(1)}, f32[60,640]{1,0:T(8,128)S(1)}, u32[]{:S(2)}, u32[]{:S(2)}) collective-permute-start(f32[60,640]{1,0:T(8,128)S(1)} %get-tuple-element.50), channel_id=1, source_target_pairs={{0,12},{4,8},{8,4},{12,0},{1,13},{5,9},{9,5},{13,1},{2,14},{6,10},... | collective-permute-start | bytes 460808 | tf_op jit(solution)/shard_map/ppermute | solution.py:280
  4.4 8.3 %collective-permute-start.1 = (f32[60,640]{1,0:T(8,128)S(1)}, f32[60,640]{1,0:T(8,128)S(1)}, u32[]{:S(2)}, u32[]{:S(2)}) collective-permute-start(f32[60,640]{1,0:T(8,128)S(1)} %get-tuple-element.51), channel_id=1, source_target_pairs={{0,4},{4,0},{8,12},{12,8},{1,5},{5,1},{9,13},{13,9},{2,6},{6,2},{1... | collective-permute-start | bytes 460808 | tf_op jit(solution)/shard_map/ppermute | solution.py:280
  5.1 6.7 %collective-permute-start.2 = (f32[24,640]{1,0:T(8,128)S(1)}, f32[24,640]{1,0:T(8,128)S(1)}, u32[]{:S(2)}, u32[]{:S(2)}) collective-permute-start(f32[24,640]{1,0:T(8,128)S(1)} %get-tuple-element.55), channel_id=1, source_target_pairs={{0,1},{1,0},{2,3},{3,2},{4,5},{5,4},{6,7},{7,6},{8,9},{9,8},{10,11... | collective-permute-start | bytes 184328 | tf_op jit(solution)/shard_map/ppermute | solution.py:291
  6.7 5.1 %collective-permute-start.3 = (f32[24,640]{1,0:T(8,128)S(1)}, f32[24,640]{1,0:T(8,128)S(1)}, u32[]{:S(2)}, u32[]{:S(2)}) collective-permute-start(f32[24,640]{1,0:T(8,128)S(1)} %get-tuple-element.56), channel_id=1, source_target_pairs={{0,0},{1,2},{2,1},{3,3},{4,4},{5,6},{6,5},{7,7},{8,8},{9,10},{10,9... | collective-permute-start | bytes 184328 | tf_op jit(solution)/shard_map/ppermute | solution.py:291
  7.4 16.7 %collective-permute-start.7 = (f32[160,320]{1,0:T(8,128)S(1)}, f32[160,320]{1,0:T(8,128)S(1)}, u32[]{:S(2)}, u32[]{:S(2)}) collective-permute-start(f32[160,320]{1,0:T(8,128)S(1)} %bitcast.6), channel_id=1, source_target_pairs={{0,16},{16,0},{1,17},{17,1},{2,18},{18,2},{3,19},{19,3},{4,20},{20... | collective-permute-start | bytes 614408 | tf_op jit(solution)/shard_map/ppermute | solution.py:470
  9.8 0.9 %copy-start.2 = (f32[7,7,7,80]{3,2,1,0:T(8,128)S(1)}, f32[7,7,7,80]{3,2,1,0:T(8,128)}, u32[]{:S(2)}) copy-start(f32[7,7,7,80]{3,2,1,0:T(8,128)} %stencils_ref.3) | copy-start | bytes 329284
  11.9 4.0 %collective-permute-start.4 = (f32[18,640]{1,0:T(8,128)S(1)}, f32[18,640]{1,0:T(8,128)S(1)}, u32[]{:S(2)}, u32[]{:S(2)}) collective-permute-start(f32[18,640]{1,0:T(8,128)S(1)} %get-tuple-element.57), channel_id=1, source_target_pairs={{0,12},{4,8},{8,4},{12,0},{1,13},{5,9},{9,5},{13,1},{2,14},{6,10},... | collective-permute-start | bytes 138248 | tf_op jit(solution)/shard_map/ppermute | solution.py:280
  12.0 3.9 %collective-permute-start.5 = (f32[18,640]{1,0:T(8,128)S(1)}, f32[18,640]{1,0:T(8,128)S(1)}, u32[]{:S(2)}, u32[]{:S(2)}) collective-permute-start(f32[18,640]{1,0:T(8,128)S(1)} %get-tuple-element.58), channel_id=1, source_target_pairs={{0,4},{4,0},{8,12},{12,8},{1,5},{5,1},{9,13},{13,9},{2,6},{6,2},{1... | collective-permute-start | bytes 138248 | tf_op jit(solution)/shard_map/ppermute | solution.py:280
  18.1 7.1 %collective-permute-start.9 = (f32[160,256]{1,0:T(8,128)S(1)}, f32[160,256]{1,0:T(8,128)S(1)}, u32[]{:S(2)}, u32[]{:S(2)}) collective-permute-start(f32[160,256]{1,0:T(8,128)S(1)} %get-tuple-element.75.own_ref.refs_1_), channel_id=1, source_target_pairs={{0,16},{16,0},{1,17},{17,1},{2,18},{18,2},{3,19},{19,3},{4,20},{20... | collective-permute-start | bytes 491528 | tf_op jit(solution)/shard_map/ppermute | solution.py:484
  20.2 8.2 %collective-permute-start.8 = (f32[160,256]{1,0:T(8,128)S(1)}, f32[160,256]{1,0:T(8,128)S(1)}, u32[]{:S(2)}, u32[]{:S(2)}) collective-permute-start(f32[160,256]{1,0:T(8,128)S(1)} %get-tuple-element.70.own_ref.refs_0_), channel_id=1, source_target_pairs={{0,16},{16,0},{1,17},{17,1},{2,18},{18,2},{3,19},{19,3},{4,20},{20... | collective-permute-start | bytes 491528 | tf_op jit(solution)/shard_map/ppermute | solution.py:484
  23.4 5.8 %collective-permute-start.6 = (f32[160,128]{1,0:T(8,128)S(1)}, f32[160,128]{1,0:T(8,128)S(1)}, u32[]{:S(2)}, u32[]{:S(2)}) collective-permute-start(f32[160,128]{1,0:T(8,128)S(1)} %get-tuple-element.66.own_ref.refs_2_), channel_id=1, source_target_pairs={{0,16},{16,0},{1,17},{17,1},{2,18},{18,2},{3,19},{19,3},{4,20},{20... | collective-permute-start | bytes 245768 | tf_op jit(solution)/shard_map/ppermute | solution.py:484
  29.4 9.2 %collective-permute-start.10 = (f32[60,640]{1,0:T(8,128)S(1)}, f32[60,640]{1,0:T(8,128)S(1)}, u32[]{:S(2)}, u32[]{:S(2)}) collective-permute-start(f32[60,640]{1,0:T(8,128)S(1)} %get-tuple-element.79), channel_id=1, source_target_pairs={{0,12},{4,8},{8,4},{12,0},{1,13},{5,9},{9,5},{13,1},{2,14},{6,10},... | collective-permute-start | bytes 460808 | tf_op jit(solution)/shard_map/ppermute | solution.py:280
  29.6 9.0 %collective-permute-start.11 = (f32[60,640]{1,0:T(8,128)S(1)}, f32[60,640]{1,0:T(8,128)S(1)}, u32[]{:S(2)}, u32[]{:S(2)}) collective-permute-start(f32[60,640]{1,0:T(8,128)S(1)} %get-tuple-element.80), channel_id=1, source_target_pairs={{0,4},{4,0},{8,12},{12,8},{1,5},{5,1},{9,13},{13,9},{2,6},{6,2},{1... | collective-permute-start | bytes 460808 | tf_op jit(solution)/shard_map/ppermute | solution.py:280
  30.9 7.4 %collective-permute-start.12 = (f32[24,640]{1,0:T(8,128)S(1)}, f32[24,640]{1,0:T(8,128)S(1)}, u32[]{:S(2)}, u32[]{:S(2)}) collective-permute-start(f32[24,640]{1,0:T(8,128)S(1)} %get-tuple-element.84), channel_id=1, source_target_pairs={{0,1},{1,0},{2,3},{3,2},{4,5},{5,4},{6,7},{7,6},{8,9},{9,8},{10,11... | collective-permute-start | bytes 184328 | tf_op jit(solution)/shard_map/ppermute | solution.py:291
  35.3 3.0 %collective-permute-start.13 = (f32[24,640]{1,0:T(8,128)S(1)}, f32[24,640]{1,0:T(8,128)S(1)}, u32[]{:S(2)}, u32[]{:S(2)}) collective-permute-start(f32[24,640]{1,0:T(8,128)S(1)} %get-tuple-element.85), channel_id=1, source_target_pairs={{0,0},{1,2},{2,1},{3,3},{4,4},{5,6},{6,5},{7,7},{8,8},{9,10},{10,9... | collective-permute-start | bytes 184328 | tf_op jit(solution)/shard_map/ppermute | solution.py:291
  38.4 4.3 %collective-permute-start.14 = (f32[18,640]{1,0:T(8,128)S(1)}, f32[18,640]{1,0:T(8,128)S(1)}, u32[]{:S(2)}, u32[]{:S(2)}) collective-permute-start(f32[18,640]{1,0:T(8,128)S(1)} %get-tuple-element.86), channel_id=1, source_target_pairs={{0,12},{4,8},{8,4},{12,0},{1,13},{5,9},{9,5},{13,1},{2,14},{6,10},... | collective-permute-start | bytes 138248 | tf_op jit(solution)/shard_map/ppermute | solution.py:280
  38.5 4.2 %collective-permute-start.15 = (f32[18,640]{1,0:T(8,128)S(1)}, f32[18,640]{1,0:T(8,128)S(1)}, u32[]{:S(2)}, u32[]{:S(2)}) collective-permute-start(f32[18,640]{1,0:T(8,128)S(1)} %get-tuple-element.87), channel_id=1, source_target_pairs={{0,4},{4,0},{8,12},{12,8},{1,5},{5,1},{9,13},{13,9},{2,6},{6,2},{1... | collective-permute-start | bytes 138248 | tf_op jit(solution)/shard_map/ppermute | solution.py:280

commit v6 on v5

--- a/solution.py
+++ b/solution.py
@@ -43,7 +43,7 @@
 
 
 def call(body, out_shape, operands, specs=None, scratch=(), flops=0, size=0, limit=12):
-    return pl.pallas_call(
+    run = pl.pallas_call(
         body,
         out_shape=out_shape,
         in_specs=specs or [VMEM] * len(operands),
@@ -51,7 +51,8 @@
         scratch_shapes=scratch,
         cost_estimate=pl.CostEstimate(flops=flops, bytes_accessed=size, transcendentals=0),
         compiler_params=pltpu.CompilerParams(vmem_limit_bytes=limit << 20),
-    )(*operands)
+    )
+    return run(*operands)
 
 
 def band_kernel(stencils_ref, inner_ref, outer_ref, table_ref, in_ref, out_ref, *, rows, forward):
@@ -194,16 +195,24 @@
 
 def corner_kernel(first_ref, second_ref, cross_ref, chip_ref, *, breadth, margin):
     odd = odd_place("lon")
+    count = 2 * margin * margin
     for part, ref in enumerate((first_ref, second_ref)):
         for row in range(margin):
             at = slice((part * margin + row) * margin, (part * margin + row + 1) * margin)
             tile = ref[row * breadth : (row + 1) * breadth, :]
-            cross_ref[at, :], chip_ref[at, :] = facing(tile, margin, odd)
-
-
-def sides_of(cross_ref, chip_ref):
+            for target_ref, value in zip((cross_ref, chip_ref), facing(tile, margin, odd)):
+                for lane in range(value.shape[1] // 128):
+                    here = slice(lane * count + at.start, lane * count + at.stop)
+                    target_ref[here, :] = value[:, lane * 128 : lane * 128 + 128]
+
+
+def unstacked(ref, lanes):
+    count = ref.shape[0] // lanes
+    return jnp.concatenate([ref[n * count : (n + 1) * count, :] for n in range(lanes)], 1)
+
+
+def sides_of(cross, chip):
     odd = odd_place("lon")
-    cross, chip = cross_ref[...], chip_ref[...]
     return jnp.where(odd, chip, cross), jnp.where(odd, cross, chip)
 
 
@@ -215,7 +224,7 @@
 def inner_kernel(field_ref, cross_ref, chip_ref, band_ref, xhigh_ref, xlow_ref, shigh_ref, slow_ref, *, breadth):
     height = field_ref.shape[0] // breadth
     margin = cross_ref.shape[0] // height
-    left, right = sides_of(cross_ref, chip_ref)
+    left, right = sides_of(cross_ref[...], chip_ref[...])
     bases, cells = shigh_ref.shape[:2]
     count = cells // 2
     zeros = jnp.zeros((margin * SLOTS, field_ref.shape[1]), jnp.bfloat16)
@@ -253,7 +262,8 @@
     edge = margin * SLOTS
     own = xhigh_ref.shape[0] - 2 * edge
     body = DEPTH - edge
-    left, right = sides_of(cross_ref, chip_ref)
+    lanes = first_ref.shape[1] // 128
+    left, right = sides_of(unstacked(cross_ref, lanes), unstacked(chip_ref, lanes))
     odd = odd_place("lat")
     tiles = []
     for part, ref in enumerate((first_ref, second_ref)):
@@ -440,7 +450,7 @@
     def spread(cross, chip, first, second, field, band):
         cross, chip = swap_lon(cross, chip)
         first, second = swap(first, second)
-        corner = f32(2 * margin * margin, channels)
+        corner = f32(channels // 128 * 2 * margin * margin, 128)
         corners = call(
             functools.partial(corner_kernel, breadth=breadth, margin=margin),
             [corner, corner], [first, second], size=1 << 18, limit=4,

time: 48.6 us -> 48.1 us (0.990)
  waiting for transfers between devices: 9.64 us -> 8.84 us
    ppermute x8, waiting for transfers between devices: 4.76 us -> 3.98 us  [swap_lon(): return (lax.ppermute(cross, 'lon', far), lax.ppermute(chip, 'lon', near))]
where the time goes in v6:
time: 48.1 us; the launch traced here: 47.9 us
  Pallas kernels  19.5 us (41%)
  starting transfers between devices  17.4 us (36%)
  waiting for transfers between devices  8.84 us (18%)
  local copies, waits for them, and re-layouts  1.23 us (3%)
  between operations  0.86 us (2%)
    pallas_call x21, Pallas kernels, call(): return run(*operands)  19.5 us
    ppermute x4, starting transfers between devices, one(): return lax.ppermute(piece, 'lat', sorted(table.items()))  7.28 us
    ppermute x8, starting transfers between devices, swap_lon(): return (lax.ppermute(cross, 'lon', far), lax.ppermute(chip, 'lon', near))  5.85 us
    ppermute x3, waiting for transfers between devices, local(): others.append(lax.ppermute(ahead, 'ens', SWAP))  4.85 us
    ppermute x8, waiting for transfers between devices, swap_lon(): return (lax.ppermute(cross, 'lon', far), lax.ppermute(chip, 'lon', near))  3.98 us
    ppermute x3, starting transfers between devices, local(): others.append(lax.ppermute(ahead, 'ens', SWAP))  2.75 us
    ppermute x1, starting transfers between devices, local(): theirs = lax.ppermute(mine, 'ens', SWAP)  1.56 us
    unnamed x12, local copies, waits for them, and re-layouts  1.23 us
  transfers between devices with their start and end apart: 16, of which 5 were waited for; matrix products, arithmetic and copies ran while one was open for 0% of the time, Pallas kernels for 28%

profile of v6, /device:TPU:0, one launch (start us, length us, event | category | flops | bytes accessed | tf_op | source)
XLA Modules:
  0.0 47.9 jit_solution(3532532913466238670)
XLA Ops:
  0.6 0.0 slice-start
  0.6 0.0 copy-start.1
  0.7 1.1 %copy-done.1 = f32[1,20,8,640]{3,2,1,0:T(8,128)S(1)} copy-done((f32[1,20,8,640]{3,2,1,0:T(8,128)S(1)}, f32[1,20,8,640]{3,2,1,0:T(8,128)}, u32[]{:S(2)}) %copy-start.1) | copy-done | bytes 409624
  1.8 0.0 copy-start
  1.8 0.0 slice-start.1
  1.8 0.0 slice-start.2
  1.8 0.1 shard_map.59
  1.9 2.5 %collective-permute-start = (f32[60,640]{1,0:T(8,128)S(1)}, f32[60,640]{1,0:T(8,128)S(1)}, u32[]{:S(2)}, u32[]{:S(2)}) collective-permute-start(f32[60,640]{1,0:T(8,128)S(1)} %get-tuple-element.50), channel_id=1, source_target_pairs={{0,12},{4,8},{8,4},{12,0},{1,13},{5,9},{9,5},{13,1},{2,14},{6,10},... | collective-permute-start | bytes 460808 | tf_op jit(solution)/shard_map/ppermute | solution.py:290
  4.4 0.7 %collective-permute-start.1 = (f32[60,640]{1,0:T(8,128)S(1)}, f32[60,640]{1,0:T(8,128)S(1)}, u32[]{:S(2)}, u32[]{:S(2)}) collective-permute-start(f32[60,640]{1,0:T(8,128)S(1)} %get-tuple-element.51), channel_id=1, source_target_pairs={{0,4},{4,0},{8,12},{12,8},{1,5},{5,1},{9,13},{13,9},{2,6},{6,2},{1... | collective-permute-start | bytes 460808 | tf_op jit(solution)/shard_map/ppermute | solution.py:290
  5.1 1.6 %collective-permute-start.2 = (f32[24,640]{1,0:T(8,128)S(1)}, f32[24,640]{1,0:T(8,128)S(1)}, u32[]{:S(2)}, u32[]{:S(2)}) collective-permute-start(f32[24,640]{1,0:T(8,128)S(1)} %get-tuple-element.55), channel_id=1, source_target_pairs={{0,1},{1,0},{2,3},{3,2},{4,5},{5,4},{6,7},{7,6},{8,9},{9,8},{10,11... | collective-permute-start | bytes 184328 | tf_op jit(solution)/shard_map/ppermute | solution.py:301
  6.7 0.7 %collective-permute-start.3 = (f32[24,640]{1,0:T(8,128)S(1)}, f32[24,640]{1,0:T(8,128)S(1)}, u32[]{:S(2)}, u32[]{:S(2)}) collective-permute-start(f32[24,640]{1,0:T(8,128)S(1)} %get-tuple-element.56), channel_id=1, source_target_pairs={{0,0},{1,2},{2,1},{3,3},{4,4},{5,6},{6,5},{7,7},{8,8},{9,10},{10,9... | collective-permute-start | bytes 184328 | tf_op jit(solution)/shard_map/ppermute | solution.py:301
  7.3 0.0 copy-done
  7.4 1.6 %collective-permute-start.7 = (f32[160,320]{1,0:T(8,128)S(1)}, f32[160,320]{1,0:T(8,128)S(1)}, u32[]{:S(2)}, u32[]{:S(2)}) collective-permute-start(f32[160,320]{1,0:T(8,128)S(1)} %bitcast.6), channel_id=1, source_target_pairs={{0,16},{16,0},{1,17},{17,1},{2,18},{18,2},{3,19},{19,3},{4,20},{20... | collective-permute-start | bytes 614408 | tf_op jit(solution)/shard_map/ppermute | solution.py:480
  8.9 0.0 slice-done
  8.9 0.0 slice-done.1
  8.9 0.0 slice-done.2
  8.9 0.8 %shard_map.70 = (bf16[7,640,256]{2,1,0:T(8,128)(2,1)S(1)}, bf16[7,640,256]{2,1,0:T(8,128)(2,1)S(1)}) custom-call(f32[7,640,640]{2,1,0:T(8,128)S(1)} %bitcast.5), custom_call_target="tpu_custom_call" | custom-call | bytes 4587520 | tf_op jit(solution)/shard_map/pallas_call | solution.py:55
  9.8 0.0 copy-start.2
  9.8 0.8 %shard_map.67 = (bf16[7,640,256]{2,1,0:T(8,128)(2,1)S(1)}, bf16[7,640,256]{2,1,0:T(8,128)(2,1)S(1)}) custom-call(f32[7,640,640]{2,1,0:T(8,128)S(1)} %bitcast.5), custom_call_target="tpu_custom_call" | custom-call | bytes 4587520 | tf_op jit(solution)/shard_map/pallas_call | solution.py:55
  10.6 0.1 copy-done.2
  10.7 1.1 %shard_map.60 = (bf16[2,784,256]{2,1,0:T(8,128)(2,1)S(1)}, bf16[2,336,256]{2,1,0:T(8,128)(2,1)S(1)}) custom-call(f32[7,7,7,80]{3,2,1,0:T(8,128)S(1)} %copy-done.2), custom_call_target="tpu_custom_call" | custom-call | flops 1000000000 | bytes 4194304 | tf_op jit(solution)/shard_map/pallas_call | solution.py:55
  11.8 0.0 collective-permute-done.2.first_ref
  11.8 0.0 collective-permute-done.3.second_ref
  11.9 0.1 collective-permute-start.4
  12.0 0.7 %collective-permute-start.5 = (f32[90,128]{1,0:T(8,128)S(1)}, f32[90,128]{1,0:T(8,128)S(1)}, u32[]{:S(2)}, u32[]{:S(2)}) collective-permute-start(f32[90,128]{1,0:T(8,128)S(1)} %get-tuple-element.58), channel_id=1, source_target_pairs={{0,4},{4,0},{8,12},{12,8},{1,5},{5,1},{9,13},{13,9},{2,6},{6,2},{1... | collective-permute-start | bytes 138248 | tf_op jit(solution)/shard_map/ppermute | solution.py:290
  12.7 0.0 collective-permute-done.cross_ref
  12.7 0.0 collective-permute-done.1.chip_ref
  12.7 1.2 %shard_map.61 = (bf16[416,640]{1,0:T(8,128)(2,1)S(1)}, bf16[416,640]{1,0:T(8,128)(2,1)S(1)}, bf16[7,112,640]{2,1,0:T(8,128)(2,1)S(1)}, bf16[7,112,640]{2,1,0:T(8,128)(2,1)S(1)}) custom-call(f32[160,640]{1,0:T(8,128)S(1)} %get-tuple-element.49.field_ref, f32[60,640]{1,0:T(8,128)S(1)} %collective-permute-done.cross_ref, ...), custom_call_target="tpu_custom_call" | custom-call | flops 770703360 | tf_op jit(solution)/shard_map/pallas_call | solution.py:55
  13.9 1.7 %collective-permute-done.4.cross_ref = f32[90,128]{1,0:T(8,128)S(1)} collective-permute-done((f32[90,128]{1,0:T(8,128)S(1)}, f32[90,128]{1,0:T(8,128)S(1)}, u32[]{:S(2)}, u32[]{:S(2)}) %collective-permute-start.4) | collective-permute-done | bytes 46112 | tf_op jit(solution)/shard_map/ppermute | solution.py:290
  15.6 0.0 collective-permute-done.5.chip_ref
  15.6 0.7 %shard_map.63 = (bf16[7,48,640]{2,1,0:T(8,128)(2,1)S(1)}, bf16[7,48,640]{2,1,0:T(8,128)(2,1)S(1)}) custom-call(f32[24,640]{1,0:T(8,128)S(1)} %collective-permute-done.2.first_ref, f32[24,640]{1,0:T(8,128)S(1)} %collective-permute-done.3.second_ref, f32[90,128]{1,0:T(8,128)S(1)} %collective-permute-done.4.cross_ref, ...), custom_call_target="tpu_custom_call" | custom-call | flops 330301440 | tf_op jit(solution)/shard_map/pallas_call | solution.py:55
  16.3 1.5 %shard_map.71 = (f32[160,256]{1,0:T(8,128)S(1)}, f32[160,256]{1,0:T(8,128)S(1)}) custom-call(bf16[7,112,640]{2,1,0:T(8,128)(2,1)S(1)} %get-tuple-element.53.ihigh_ref, bf16[7,112,640]{2,1,0:T(8,128)(2,1)S(1)} %get-tuple-element.54.ilow_ref, bf16[7,48,640]{2,1,0:T(8,128)(2,1)S(1)} %get-tuple-element.62.ohigh_ref, ...), custom_call_target="tpu_custom_call" | custom-call | flops 1101004800 | tf_op jit(solution)/shard_map/pallas_call | solution.py:55
  17.8 0.6 %collective-permute-start.9 = (f32[160,256]{1,0:T(8,128)S(1)}, f32[160,256]{1,0:T(8,128)S(1)}, u32[]{:S(2)}, u32[]{:S(2)}) collective-permute-start(f32[160,256]{1,0:T(8,128)S(1)} %get-tuple-element.75.own_ref.refs_1_), channel_id=1, source_target_pairs={{0,16},{16,0},{1,17},{17,1},{2,18},{18,2},{3,19},{19,3},{4,20},{20... | collective-permute-start | bytes 491528 | tf_op jit(solution)/shard_map/ppermute | solution.py:494
  18.4 1.5 %shard_map.68 = (f32[160,256]{1,0:T(8,128)S(1)}, f32[160,256]{1,0:T(8,128)S(1)}) custom-call(bf16[7,112,640]{2,1,0:T(8,128)(2,1)S(1)} %get-tuple-element.53.ihigh_ref, bf16[7,112,640]{2,1,0:T(8,128)(2,1)S(1)} %get-tuple-element.54.ilow_ref, bf16[7,48,640]{2,1,0:T(8,128)(2,1)S(1)} %get-tuple-element.62.ohigh_ref, ...), custom_call_target="tpu_custom_call" | custom-call | flops 1101004800 | tf_op jit(solution)/shard_map/pallas_call | solution.py:55
  19.9 1.6 %collective-permute-start.8 = (f32[160,256]{1,0:T(8,128)S(1)}, f32[160,256]{1,0:T(8,128)S(1)}, u32[]{:S(2)}, u32[]{:S(2)}) collective-permute-start(f32[160,256]{1,0:T(8,128)S(1)} %get-tuple-element.70.own_ref.refs_0_), channel_id=1, source_target_pairs={{0,16},{16,0},{1,17},{17,1},{2,18},{18,2},{3,19},{19,3},{4,20},{20... | collective-permute-start | bytes 491528 | tf_op jit(solution)/shard_map/ppermute | solution.py:494
  21.5 0.3 shard_map.64
  21.9 1.3 %shard_map.65 = (f32[160,128]{1,0:T(8,128)S(1)}, f32[160,128]{1,0:T(8,128)S(1)}) custom-call(bf16[7,112,640]{2,1,0:T(8,128)(2,1)S(1)} %get-tuple-element.53.ihigh_ref, bf16[7,112,640]{2,1,0:T(8,128)(2,1)S(1)} %get-tuple-element.54.ilow_ref, bf16[7,48,640]{2,1,0:T(8,128)(2,1)S(1)} %get-tuple-element.62.ohigh_ref, ...), custom_call_target="tpu_custom_call" | custom-call | flops 550502400 | tf_op jit(solution)/shard_map/pallas_call | solution.py:55
  23.2 0.6 %collective-permute-start.6 = (f32[160,128]{1,0:T(8,128)S(1)}, f32[160,128]{1,0:T(8,128)S(1)}, u32[]{:S(2)}, u32[]{:S(2)}) collective-permute-start(f32[160,128]{1,0:T(8,128)S(1)} %get-tuple-element.66.own_ref.refs_2_), channel_id=1, source_target_pairs={{0,16},{16,0},{1,17},{17,1},{2,18},{18,2},{3,19},{19,3},{4,20},{20... | collective-permute-start | bytes 245768 | tf_op jit(solution)/shard_map/ppermute | solution.py:494
  23.8 0.0 collective-permute-done.7.theirs_ref
  23.8 0.1 shard_map.66.analysis_ref
  24.0 1.0 %collective-permute-done.9.other_ref.refs_4_ = f32[160,256]{1,0:T(8,128)S(1)} collective-permute-done((f32[160,256]{1,0:T(8,128)S(1)}, f32[160,256]{1,0:T(8,128)S(1)}, u32[]{:S(2)}, u32[]{:S(2)}) %collective-permute-start.9) | collective-permute-done | bytes 163872 | tf_op jit(solution)/shard_map/ppermute | solution.py:494
  25.0 0.1 shard_map.72
  25.1 3.1 %collective-permute-done.8.other_ref.refs_3_ = f32[160,256]{1,0:T(8,128)S(1)} collective-permute-done((f32[160,256]{1,0:T(8,128)S(1)}, f32[160,256]{1,0:T(8,128)S(1)}, u32[]{:S(2)}, u32[]{:S(2)}) %collective-permute-start.8) | collective-permute-done | bytes 163872 | tf_op jit(solution)/shard_map/ppermute | solution.py:494
  28.1 0.1 shard_map.69
  28.2 0.8 %collective-permute-done.6.other_ref.refs_5_ = f32[160,128]{1,0:T(8,128)S(1)} collective-permute-done((f32[160,128]{1,0:T(8,128)S(1)}, f32[160,128]{1,0:T(8,128)S(1)}, u32[]{:S(2)}, u32[]{:S(2)}) %collective-permute-start.6) | collective-permute-done | bytes 81952 | tf_op jit(solution)/shard_map/ppermute | solution.py:494
  29.0 0.2 shard_map.73
  29.2 0.2 collective-permute-start.10
  29.3 1.3 %collective-permute-start.11 = (f32[60,640]{1,0:T(8,128)S(1)}, f32[60,640]{1,0:T(8,128)S(1)}, u32[]{:S(2)}, u32[]{:S(2)}) collective-permute-start(f32[60,640]{1,0:T(8,128)S(1)} %get-tuple-element.80), channel_id=1, source_target_pairs={{0,4},{4,0},{8,12},{12,8},{1,5},{5,1},{9,13},{13,9},{2,6},{6,2},{1... | collective-permute-start | bytes 460808 | tf_op jit(solution)/shard_map/ppermute | solution.py:290
  30.6 4.4 %collective-permute-start.12 = (f32[24,640]{1,0:T(8,128)S(1)}, f32[24,640]{1,0:T(8,128)S(1)}, u32[]{:S(2)}, u32[]{:S(2)}) collective-permute-start(f32[24,640]{1,0:T(8,128)S(1)} %get-tuple-element.84), channel_id=1, source_target_pairs={{0,1},{1,0},{2,3},{3,2},{4,5},{5,4},{6,7},{7,6},{8,9},{9,8},{10,11... | collective-permute-start | bytes 184328 | tf_op jit(solution)/shard_map/ppermute | solution.py:301
  35.0 0.7 %collective-permute-start.13 = (f32[24,640]{1,0:T(8,128)S(1)}, f32[24,640]{1,0:T(8,128)S(1)}, u32[]{:S(2)}, u32[]{:S(2)}) collective-permute-start(f32[24,640]{1,0:T(8,128)S(1)} %get-tuple-element.85), channel_id=1, source_target_pairs={{0,0},{1,2},{2,1},{3,3},{4,4},{5,6},{6,5},{7,7},{8,8},{9,10},{10,9... | collective-permute-start | bytes 184328 | tf_op jit(solution)/shard_map/ppermute | solution.py:301
  35.7 1.2 %shard_map.74 = (bf16[2,784,256]{2,1,0:T(8,128)(2,1)S(1)}, bf16[2,336,256]{2,1,0:T(8,128)(2,1)S(1)}) custom-call(f32[7,7,7,80]{3,2,1,0:T(8,128)S(1)} %copy-done.2), custom_call_target="tpu_custom_call" | custom-call | flops 1000000000 | bytes 4194304 | tf_op jit(solution)/shard_map/pallas_call | solution.py:55
  36.9 1.2 %shard_map.79 = f32[160,320]{1,0:T(8,128)} custom-call(f32[160,256]{1,0:T(8,128)S(1)} %get-tuple-element.70.own_ref.refs_0_, f32[160,256]{1,0:T(8,128)S(1)} %get-tuple-element.75.own_ref.refs_1_, f32[160,128]{1,0:T(8,128)S(1)} %get-tuple-element.66.own_ref.refs_2_, f32[160,256]{1,0:T(8,128)S(1)} %collective-permute-done.8.other_ref.refs_3_, ...), custom_call_target="tpu_custom_call" | custom-call | bytes 1048576 | tf_op jit(solution)/shard_map/pallas_call | solution.py:55
  38.1 0.0 collective-permute-done.12.first_ref
  38.1 0.0 collective-permute-done.13.second_ref
  38.1 0.1 collective-permute-start.14
  38.2 0.3 collective-permute-start.15
  38.5 0.0 collective-permute-done.10.cross_ref
  38.5 0.0 collective-permute-done.11.chip_ref
  38.5 1.3 %shard_map.75 = (bf16[416,640]{1,0:T(8,128)(2,1)S(1)}, bf16[416,640]{1,0:T(8,128)(2,1)S(1)}, bf16[7,112,640]{2,1,0:T(8,128)(2,1)S(1)}, bf16[7,112,640]{2,1,0:T(8,128)(2,1)S(1)}) custom-call(f32[160,640]{1,0:T(8,128)S(1)} %get-tuple-element.78.field_ref, f32[60,640]{1,0:T(8,128)S(1)} %collective-permute-done.10.cross_ref, ...), custom_call_target="tpu_custom_call" | custom-call | flops 770703360 | tf_op jit(solution)/shard_map/pallas_call | solution.py:55
  39.8 2.3 %collective-permute-done.14.cross_ref = f32[90,128]{1,0:T(8,128)S(1)} collective-permute-done((f32[90,128]{1,0:T(8,128)S(1)}, f32[90,128]{1,0:T(8,128)S(1)}, u32[]{:S(2)}, u32[]{:S(2)}) %collective-permute-start.14) | collective-permute-done | bytes 46112 | tf_op jit(solution)/shard_map/ppermute | solution.py:290
  42.1 0.0 collective-permute-done.15.chip_ref
  42.1 0.7 %shard_map.77 = (bf16[7,48,640]{2,1,0:T(8,128)(2,1)S(1)}, bf16[7,48,640]{2,1,0:T(8,128)(2,1)S(1)}) custom-call(f32[24,640]{1,0:T(8,128)S(1)} %collective-permute-done.12.first_ref, f32[24,640]{1,0:T(8,128)S(1)} %collective-permute-done.13.second_ref, f32[90,128]{1,0:T(8,128)S(1)} %collective-permute-done.14.cross_ref, ...), custom_call_target="tpu_custom_call" | custom-call | flops 330301440 | tf_op jit(solution)/shard_map/pallas_call | solution.py:55
  42.8 5.1 %shard_map.78 = f32[160,640]{1,0:T(8,128)} custom-call(bf16[7,112,640]{2,1,0:T(8,128)(2,1)S(1)} %get-tuple-element.82.refs_0_, bf16[7,112,640]{2,1,0:T(8,128)(2,1)S(1)} %get-tuple-element.83.refs_1_, bf16[7,48,640]{2,1,0:T(8,128)(2,1)S(1)} %get-tuple-element.91.refs_2_, bf16[7,48,640]{2,1,0:T(8,128)(2,1)S(1)} %get-tuple-element.92.refs_3_, ...), custom_call_target="tpu_custom_call" | custom-call | flops 2752512000 | tf_op jit(solution)/shard_map/pallas_call | solution.py:55
  (3 shorter events, 0.1 us)
Async XLA Ops:
  0.6 8.3 %slice-start = ((s8[11468800]{0:T(1024)(128)(4,1)}), s8[4194304]{0:T(1024)(128)(4,1)S(1)}, s32[]{:S(2)}) async-start(s8[11468800]{0:T(1024)(128)(4,1)} %bitcast.4), calls=%async_computation | async-start | bytes 8388608
  0.6 1.2 %copy-start.1 = (f32[1,20,8,640]{3,2,1,0:T(8,128)S(1)}, f32[1,20,8,640]{3,2,1,0:T(8,128)}, u32[]{:S(2)}) copy-start(f32[1,20,8,640]{3,2,1,0:T(8,128)} %param.4) | copy-start | bytes 1228804
  1.8 5.6 %copy-start = (f32[20,8,320]{2,1,0:T(8,128)S(1)}, f32[20,8,320]{2,1,0:T(8,128)}, u32[]{:S(2)}) copy-start(f32[20,8,320]{2,1,0:T(8,128)} %param.5) | copy-start | bytes 614404
  1.8 7.1 %slice-start.1 = ((s8[11468800]{0:T(1024)(128)(4,1)}), s8[4194304]{0:T(1024)(128)(4,1)S(1)}, s32[]{:S(2)}) async-start(s8[11468800]{0:T(1024)(128)(4,1)} %bitcast.4), calls=%async_computation.1 | async-start | bytes 8388608
  1.8 7.1 %slice-start.2 = ((s8[11468800]{0:T(1024)(128)(4,1)}), s8[3080192]{0:T(1024)(128)(4,1)S(1)}, s32[]{:S(2)}) async-start(s8[11468800]{0:T(1024)(128)(4,1)} %bitcast.4), calls=%async_computation.2 | async-start | bytes 6160384
  1.9 10.8 %collective-permute-start = (f32[60,640]{1,0:T(8,128)S(1)}, f32[60,640]{1,0:T(8,128)S(1)}, u32[]{:S(2)}, u32[]{:S(2)}) collective-permute-start(f32[60,640]{1,0:T(8,128)S(1)} %get-tuple-element.50), channel_id=1, source_target_pairs={{0,12},{4,8},{8,4},{12,0},{1,13},{5,9},{9,5},{13,1},{2,14},{6,10},... | collective-permute-start | bytes 460808 | tf_op jit(solution)/shard_map/ppermute | solution.py:290
  4.4 8.3 %collective-permute-start.1 = (f32[60,640]{1,0:T(8,128)S(1)}, f32[60,640]{1,0:T(8,128)S(1)}, u32[]{:S(2)}, u32[]{:S(2)}) collective-permute-start(f32[60,640]{1,0:T(8,128)S(1)} %get-tuple-element.51), channel_id=1, source_target_pairs={{0,4},{4,0},{8,12},{12,8},{1,5},{5,1},{9,13},{13,9},{2,6},{6,2},{1... | collective-permute-start | bytes 460808 | tf_op jit(solution)/shard_map/ppermute | solution.py:290
  5.1 6.7 %collective-permute-start.2 = (f32[24,640]{1,0:T(8,128)S(1)}, f32[24,640]{1,0:T(8,128)S(1)}, u32[]{:S(2)}, u32[]{:S(2)}) collective-permute-start(f32[24,640]{1,0:T(8,128)S(1)} %get-tuple-element.55), channel_id=1, source_target_pairs={{0,1},{1,0},{2,3},{3,2},{4,5},{5,4},{6,7},{7,6},{8,9},{9,8},{10,11... | collective-permute-start | bytes 184328 | tf_op jit(solution)/shard_map/ppermute | solution.py:301
  6.7 5.1 %collective-permute-start.3 = (f32[24,640]{1,0:T(8,128)S(1)}, f32[24,640]{1,0:T(8,128)S(1)}, u32[]{:S(2)}, u32[]{:S(2)}) collective-permute-start(f32[24,640]{1,0:T(8,128)S(1)} %get-tuple-element.56), channel_id=1, source_target_pairs={{0,0},{1,2},{2,1},{3,3},{4,4},{5,6},{6,5},{7,7},{8,8},{9,10},{10,9... | collective-permute-start | bytes 184328 | tf_op jit(solution)/shard_map/ppermute | solution.py:301
  7.4 16.4 %collective-permute-start.7 = (f32[160,320]{1,0:T(8,128)S(1)}, f32[160,320]{1,0:T(8,128)S(1)}, u32[]{:S(2)}, u32[]{:S(2)}) collective-permute-start(f32[160,320]{1,0:T(8,128)S(1)} %bitcast.6), channel_id=1, source_target_pairs={{0,16},{16,0},{1,17},{17,1},{2,18},{18,2},{3,19},{19,3},{4,20},{20... | collective-permute-start | bytes 614408 | tf_op jit(solution)/shard_map/ppermute | solution.py:480
  9.8 0.9 %copy-start.2 = (f32[7,7,7,80]{3,2,1,0:T(8,128)S(1)}, f32[7,7,7,80]{3,2,1,0:T(8,128)}, u32[]{:S(2)}) copy-start(f32[7,7,7,80]{3,2,1,0:T(8,128)} %stencils_ref.3) | copy-start | bytes 329284
  11.9 3.7 %collective-permute-start.4 = (f32[90,128]{1,0:T(8,128)S(1)}, f32[90,128]{1,0:T(8,128)S(1)}, u32[]{:S(2)}, u32[]{:S(2)}) collective-permute-start(f32[90,128]{1,0:T(8,128)S(1)} %get-tuple-element.57), channel_id=1, source_target_pairs={{0,12},{4,8},{8,4},{12,0},{1,13},{5,9},{9,5},{13,1},{2,14},{6,10},... | collective-permute-start | bytes 138248 | tf_op jit(solution)/shard_map/ppermute | solution.py:290
  12.0 3.7 %collective-permute-start.5 = (f32[90,128]{1,0:T(8,128)S(1)}, f32[90,128]{1,0:T(8,128)S(1)}, u32[]{:S(2)}, u32[]{:S(2)}) collective-permute-start(f32[90,128]{1,0:T(8,128)S(1)} %get-tuple-element.58), channel_id=1, source_target_pairs={{0,4},{4,0},{8,12},{12,8},{1,5},{5,1},{9,13},{13,9},{2,6},{6,2},{1... | collective-permute-start | bytes 138248 | tf_op jit(solution)/shard_map/ppermute | solution.py:290
  17.8 7.1 %collective-permute-start.9 = (f32[160,256]{1,0:T(8,128)S(1)}, f32[160,256]{1,0:T(8,128)S(1)}, u32[]{:S(2)}, u32[]{:S(2)}) collective-permute-start(f32[160,256]{1,0:T(8,128)S(1)} %get-tuple-element.75.own_ref.refs_1_), channel_id=1, source_target_pairs={{0,16},{16,0},{1,17},{17,1},{2,18},{18,2},{3,19},{19,3},{4,20},{20... | collective-permute-start | bytes 491528 | tf_op jit(solution)/shard_map/ppermute | solution.py:494
  19.9 8.2 %collective-permute-start.8 = (f32[160,256]{1,0:T(8,128)S(1)}, f32[160,256]{1,0:T(8,128)S(1)}, u32[]{:S(2)}, u32[]{:S(2)}) collective-permute-start(f32[160,256]{1,0:T(8,128)S(1)} %get-tuple-element.70.own_ref.refs_0_), channel_id=1, source_target_pairs={{0,16},{16,0},{1,17},{17,1},{2,18},{18,2},{3,19},{19,3},{4,20},{20... | collective-permute-start | bytes 491528 | tf_op jit(solution)/shard_map/ppermute | solution.py:494
  23.2 5.8 %collective-permute-start.6 = (f32[160,128]{1,0:T(8,128)S(1)}, f32[160,128]{1,0:T(8,128)S(1)}, u32[]{:S(2)}, u32[]{:S(2)}) collective-permute-start(f32[160,128]{1,0:T(8,128)S(1)} %get-tuple-element.66.own_ref.refs_2_), channel_id=1, source_target_pairs={{0,16},{16,0},{1,17},{17,1},{2,18},{18,2},{3,19},{19,3},{4,20},{20... | collective-permute-start | bytes 245768 | tf_op jit(solution)/shard_map/ppermute | solution.py:494
  29.2 9.4 %collective-permute-start.10 = (f32[60,640]{1,0:T(8,128)S(1)}, f32[60,640]{1,0:T(8,128)S(1)}, u32[]{:S(2)}, u32[]{:S(2)}) collective-permute-start(f32[60,640]{1,0:T(8,128)S(1)} %get-tuple-element.79), channel_id=1, source_target_pairs={{0,12},{4,8},{8,4},{12,0},{1,13},{5,9},{9,5},{13,1},{2,14},{6,10},... | collective-permute-start | bytes 460808 | tf_op jit(solution)/shard_map/ppermute | solution.py:290
  29.3 9.2 %collective-permute-start.11 = (f32[60,640]{1,0:T(8,128)S(1)}, f32[60,640]{1,0:T(8,128)S(1)}, u32[]{:S(2)}, u32[]{:S(2)}) collective-permute-start(f32[60,640]{1,0:T(8,128)S(1)} %get-tuple-element.80), channel_id=1, source_target_pairs={{0,4},{4,0},{8,12},{12,8},{1,5},{5,1},{9,13},{13,9},{2,6},{6,2},{1... | collective-permute-start | bytes 460808 | tf_op jit(solution)/shard_map/ppermute | solution.py:290
  30.6 7.5 %collective-permute-start.12 = (f32[24,640]{1,0:T(8,128)S(1)}, f32[24,640]{1,0:T(8,128)S(1)}, u32[]{:S(2)}, u32[]{:S(2)}) collective-permute-start(f32[24,640]{1,0:T(8,128)S(1)} %get-tuple-element.84), channel_id=1, source_target_pairs={{0,1},{1,0},{2,3},{3,2},{4,5},{5,4},{6,7},{7,6},{8,9},{9,8},{10,11... | collective-permute-start | bytes 184328 | tf_op jit(solution)/shard_map/ppermute | solution.py:301
  35.0 3.1 %collective-permute-start.13 = (f32[24,640]{1,0:T(8,128)S(1)}, f32[24,640]{1,0:T(8,128)S(1)}, u32[]{:S(2)}, u32[]{:S(2)}) collective-permute-start(f32[24,640]{1,0:T(8,128)S(1)} %get-tuple-element.85), channel_id=1, source_target_pairs={{0,0},{1,2},{2,1},{3,3},{4,4},{5,6},{6,5},{7,7},{8,8},{9,10},{10,9... | collective-permute-start | bytes 184328 | tf_op jit(solution)/shard_map/ppermute | solution.py:301
  38.1 4.0 %collective-permute-start.14 = (f32[90,128]{1,0:T(8,128)S(1)}, f32[90,128]{1,0:T(8,128)S(1)}, u32[]{:S(2)}, u32[]{:S(2)}) collective-permute-start(f32[90,128]{1,0:T(8,128)S(1)} %get-tuple-element.86), channel_id=1, source_target_pairs={{0,12},{4,8},{8,4},{12,0},{1,13},{5,9},{9,5},{13,1},{2,14},{6,10},... | collective-permute-start | bytes 138248 | tf_op jit(solution)/shard_map/ppermute | solution.py:290
  38.2 3.9 %collective-permute-start.15 = (f32[90,128]{1,0:T(8,128)S(1)}, f32[90,128]{1,0:T(8,128)S(1)}, u32[]{:S(2)}, u32[]{:S(2)}) collective-permute-start(f32[90,128]{1,0:T(8,128)S(1)} %get-tuple-element.87), channel_id=1, source_target_pairs={{0,4},{4,0},{8,12},{12,8},{1,5},{5,1},{9,13},{13,9},{2,6},{6,2},{1... | collective-permute-start | bytes 138248 | tf_op jit(solution)/shard_map/ppermute | solution.py:290

commit v7 on v6

--- a/solution.py
+++ b/solution.py
@@ -12,6 +12,7 @@
 SLOTS = 16
 DEPTH = 256
 CHUNKS = (2, 2)
+EARLY = 2
 SWAP = [(0, 1), (1, 0)]
 VMEM = pl.BlockSpec(memory_space=pltpu.VMEM)
 
@@ -309,37 +310,66 @@
         high_ref[base], low_ref[base] = split(mixing_ref[base, :, lanes])
 
 
-def contract(taps, parts, axis):
-    inner_high, inner_low, outer_high, outer_low = taps
-    total = None
+def joined(inner_ref, outer_ref, base, lanes):
+    return jnp.concatenate([inner_ref[base, :, lanes], outer_ref[base, :, lanes]], 0)
+
+
+def contract(pairs, parts, axis, bases, total=None):
+    high, low = pairs
     for high_ref, low_ref, lanes in parts:
-        for base in range(high_ref.shape[0]):
-            high = jnp.concatenate([inner_high[base, :, lanes], outer_high[base, :, lanes]], 0)
-            low = jnp.concatenate([inner_low[base, :, lanes], outer_low[base, :, lanes]], 0)
-            part = product3(high, low, high_ref[base], low_ref[base], axis)
+        for base in bases:
+            part = product3(high(base, lanes), low(base, lanes), high_ref[base], low_ref[base], axis)
             total = part if total is None else total + part
-    edge = outer_high.shape[1] // 2
-    inner = inner_high.shape[1]
+    return total
+
+
+def only(ref):
+    return lambda base, lanes: ref[base, :, lanes]
+
+
+def both(inner_ref, outer_ref):
+    return functools.partial(joined, inner_ref, outer_ref)
+
+
+def ordered(total, outer):
+    edge = outer // 2
+    inner = total.shape[0] - outer
     return jnp.concatenate([total[inner : inner + edge], total[:inner], total[inner + edge :]], 0)
 
 
 def forward(ihigh_ref, ilow_ref, ohigh_ref, olow_ref, mhigh_ref, mlow_ref, field_ref, predicted_ref, bounded_ref, *, start):
     lanes = slice(start, start + predicted_ref.shape[1])
-    taps = (ihigh_ref, ilow_ref, ohigh_ref, olow_ref)
-    total = contract(taps, [(mhigh_ref, mlow_ref, slice(None))], 0)
+    pairs = both(ihigh_ref, ohigh_ref), both(ilow_ref, olow_ref)
+    bases = range(mhigh_ref.shape[0])
+    total = contract(pairs, [(mhigh_ref, mlow_ref, slice(None))], 0, bases)
+    total = ordered(total, ohigh_ref.shape[1])
     bounded = jnp.tanh(total)
     bounded_ref[...] = bounded
     predicted_ref[...] = field_ref[:, lanes] + bounded
 
 
-def backward(*refs):
-    taps, rest, out_ref = refs[:4], refs[4:-1], refs[-1]
-    grads, weights = rest[: len(rest) // 3], rest[len(rest) // 3 :]
+def spans(weights):
     parts, start = [], 0
     for high_ref, low_ref in zip(weights[::2], weights[1::2]):
         parts.append((high_ref, low_ref, slice(start, start + high_ref.shape[2])))
         start += high_ref.shape[2]
-    total = contract(taps, parts, 1)
+    return parts
+
+
+def adjoint_early(ihigh_ref, ilow_ref, *refs):
+    weights, out_ref = refs[:-1], refs[-1]
+    out_ref[...] = contract((only(ihigh_ref), only(ilow_ref)), spans(weights), 1, range(EARLY))
+
+
+def backward(early_ref, ihigh_ref, ilow_ref, ohigh_ref, olow_ref, *refs):
+    rest, out_ref = refs[:-1], refs[-1]
+    grads, weights = rest[: len(rest) // 3], rest[len(rest) // 3 :]
+    parts = spans(weights)
+    outer = contract((only(ohigh_ref), only(olow_ref)), parts, 1, range(EARLY))
+    pairs = both(ihigh_ref, ohigh_ref), both(ilow_ref, olow_ref)
+    total = contract(pairs, parts, 1, range(EARLY, ihigh_ref.shape[0]))
+    total = total + jnp.concatenate([early_ref[...], outer], 0)
+    total = ordered(total, ohigh_ref.shape[1])
     for grad_ref, (_, _, lanes) in zip(grads, parts):
         out_ref[:, lanes] = total[:, lanes] + grad_ref[...]
 
@@ -468,14 +498,14 @@
             [first, second, *corners, band[1], xhigh, xlow],
             scratch=[depth, depth], flops=stencil_flops * 3 // 10,
         )
-        return [*inner, *outer]
+        return inner, outer
 
     *sent, flat = call(
         functools.partial(pack_kernel, breadth=breadth), packed + [f32(cells, channels)],
         [flat], flops=10**10, size=1 << 20, limit=8,
     )
     band = bands(stencils, rows, breadth, True)
-    spread0 = spread(*sent, flat, band)
+    inner0, outer0 = spread(*sent, flat, band)
     if pair:
         theirs = lax.ppermute(mine, "ens", SWAP)
     weights, predicted, bounded, others = [], [], [], []
@@ -486,7 +516,7 @@
         )
         ahead, tanh = call(
             functools.partial(forward, start=start), [f32(cells, width)] * 2,
-            [*spread0, *weights[-2:], flat], flops=mix_flops * width // channels,
+            [*inner0, *outer0, *weights[-2:], flat], flops=mix_flops * width // channels,
         )
         predicted.append(ahead)
         bounded.append(tanh)
@@ -527,9 +557,14 @@
             functools.partial(pack_kernel, breadth=breadth), packed + [f32(cells, channels)],
             [inner], size=1 << 20, limit=8,
         )
+    inner1, outer1 = spread(*sent, inner, back)
+    (early,) = call(
+        adjoint_early, [f32(inner_cells, channels)], [*inner1, *weights],
+        flops=mix_flops * EARLY // bases,
+    )
     (result,) = call(
         backward, [f32(cells, channels)],
-        [*spread(*sent, inner, back), *grads, *weights], flops=mix_flops,
+        [early, *inner1, *outer1, *grads, *weights], flops=mix_flops,
     )
     return result.reshape(members.shape), crps.reshape(analysis.shape)
 

time: 48.1 us -> 47.9 us (level)
  waiting for transfers between devices: 8.84 us -> 7.74 us
  Pallas kernels: 19.5 us -> 20.4 us
    ppermute x8, waiting for transfers between devices: 3.98 us -> 2.87 us  [swap_lon(): return (lax.ppermute(cross, 'lon', far), lax.ppermute(chip, 'lon', near))]
    pallas_call x21 -> x22, Pallas kernels: 19.5 us -> 20.4 us  [call(): return run(*operands)]
  transfers between devices with their start and end apart: 16 -> 16, of which waited for: 5 -> 5; matrix products, arithmetic and copies ran while one was open for 0% -> 0% of each run, Pallas kernels for 28% -> 31%
where the time goes in v7:
time: 47.9 us; the launch traced here: 47.7 us
  Pallas kernels  20.4 us (43%)
  starting transfers between devices  17.4 us (36%)
  waiting for transfers between devices  7.74 us (16%)
  local copies, waits for them, and re-layouts  1.23 us (3%)
  between operations  0.86 us (2%)
    pallas_call x22, Pallas kernels, call(): return run(*operands)  20.4 us
    ppermute x4, starting transfers between devices, one(): return lax.ppermute(piece, 'lat', sorted(table.items()))  7.28 us
    ppermute x8, starting transfers between devices, swap_lon(): return (lax.ppermute(cross, 'lon', far), lax.ppermute(chip, 'lon', near))  5.85 us
    ppermute x3, waiting for transfers between devices, local(): others.append(lax.ppermute(ahead, 'ens', SWAP))  4.86 us
    ppermute x8, waiting for transfers between devices, swap_lon(): return (lax.ppermute(cross, 'lon', far), lax.ppermute(chip, 'lon', near))  2.87 us
    ppermute x3, starting transfers between devices, local(): others.append(lax.ppermute(ahead, 'ens', SWAP))  2.76 us
    ppermute x1, starting transfers between devices, local(): theirs = lax.ppermute(mine, 'ens', SWAP)  1.56 us
    unnamed x12, local copies, waits for them, and re-layouts  1.23 us
  transfers between devices with their start and end apart: 16, of which 5 were waited for; matrix products, arithmetic and copies ran while one was open for 0% of the time, Pallas kernels for 31%

profile of v7, /device:TPU:0, one launch (start us, length us, event | category | flops | bytes accessed | tf_op | source)
XLA Modules:
  0.0 47.7 jit_solution(4745842300056314609)
XLA Ops:
  0.6 0.0 slice-start
  0.6 0.0 copy-start.1
  0.7 1.1 %copy-done.1 = f32[1,20,8,640]{3,2,1,0:T(8,128)S(1)} copy-done((f32[1,20,8,640]{3,2,1,0:T(8,128)S(1)}, f32[1,20,8,640]{3,2,1,0:T(8,128)}, u32[]{:S(2)}) %copy-start.1) | copy-done | bytes 409624
  1.8 0.0 copy-start
  1.8 0.0 slice-start.1
  1.8 0.0 slice-start.2
  1.8 0.1 shard_map.59
  1.9 2.5 %collective-permute-start = (f32[60,640]{1,0:T(8,128)S(1)}, f32[60,640]{1,0:T(8,128)S(1)}, u32[]{:S(2)}, u32[]{:S(2)}) collective-permute-start(f32[60,640]{1,0:T(8,128)S(1)} %get-tuple-element.50), channel_id=1, source_target_pairs={{0,12},{4,8},{8,4},{12,0},{1,13},{5,9},{9,5},{13,1},{2,14},{6,10},... | collective-permute-start | bytes 460808 | tf_op jit(solution)/shard_map/ppermute | solution.py:291
  4.4 0.7 %collective-permute-start.1 = (f32[60,640]{1,0:T(8,128)S(1)}, f32[60,640]{1,0:T(8,128)S(1)}, u32[]{:S(2)}, u32[]{:S(2)}) collective-permute-start(f32[60,640]{1,0:T(8,128)S(1)} %get-tuple-element.51), channel_id=1, source_target_pairs={{0,4},{4,0},{8,12},{12,8},{1,5},{5,1},{9,13},{13,9},{2,6},{6,2},{1... | collective-permute-start | bytes 460808 | tf_op jit(solution)/shard_map/ppermute | solution.py:291
  5.1 1.6 %collective-permute-start.2 = (f32[24,640]{1,0:T(8,128)S(1)}, f32[24,640]{1,0:T(8,128)S(1)}, u32[]{:S(2)}, u32[]{:S(2)}) collective-permute-start(f32[24,640]{1,0:T(8,128)S(1)} %get-tuple-element.55), channel_id=1, source_target_pairs={{0,1},{1,0},{2,3},{3,2},{4,5},{5,4},{6,7},{7,6},{8,9},{9,8},{10,11... | collective-permute-start | bytes 184328 | tf_op jit(solution)/shard_map/ppermute | solution.py:302
  6.7 0.7 %collective-permute-start.3 = (f32[24,640]{1,0:T(8,128)S(1)}, f32[24,640]{1,0:T(8,128)S(1)}, u32[]{:S(2)}, u32[]{:S(2)}) collective-permute-start(f32[24,640]{1,0:T(8,128)S(1)} %get-tuple-element.56), channel_id=1, source_target_pairs={{0,0},{1,2},{2,1},{3,3},{4,4},{5,6},{6,5},{7,7},{8,8},{9,10},{10,9... | collective-permute-start | bytes 184328 | tf_op jit(solution)/shard_map/ppermute | solution.py:302
  7.3 0.0 copy-done
  7.4 1.6 %collective-permute-start.7 = (f32[160,320]{1,0:T(8,128)S(1)}, f32[160,320]{1,0:T(8,128)S(1)}, u32[]{:S(2)}, u32[]{:S(2)}) collective-permute-start(f32[160,320]{1,0:T(8,128)S(1)} %bitcast.6), channel_id=1, source_target_pairs={{0,16},{16,0},{1,17},{17,1},{2,18},{18,2},{3,19},{19,3},{4,20},{20... | collective-permute-start | bytes 614408 | tf_op jit(solution)/shard_map/ppermute | solution.py:510
  8.9 0.0 slice-done
  8.9 0.0 slice-done.1
  8.9 0.0 slice-done.2
  8.9 0.8 %shard_map.70 = (bf16[7,640,256]{2,1,0:T(8,128)(2,1)S(1)}, bf16[7,640,256]{2,1,0:T(8,128)(2,1)S(1)}) custom-call(f32[7,640,640]{2,1,0:T(8,128)S(1)} %bitcast.5), custom_call_target="tpu_custom_call" | custom-call | bytes 4587520 | tf_op jit(solution)/shard_map/pallas_call | solution.py:56
  9.8 0.0 copy-start.2
  9.8 0.8 %shard_map.67 = (bf16[7,640,256]{2,1,0:T(8,128)(2,1)S(1)}, bf16[7,640,256]{2,1,0:T(8,128)(2,1)S(1)}) custom-call(f32[7,640,640]{2,1,0:T(8,128)S(1)} %bitcast.5), custom_call_target="tpu_custom_call" | custom-call | bytes 4587520 | tf_op jit(solution)/shard_map/pallas_call | solution.py:56
  10.6 0.1 copy-done.2
  10.7 1.1 %shard_map.60 = (bf16[2,784,256]{2,1,0:T(8,128)(2,1)S(1)}, bf16[2,336,256]{2,1,0:T(8,128)(2,1)S(1)}) custom-call(f32[7,7,7,80]{3,2,1,0:T(8,128)S(1)} %copy-done.2), custom_call_target="tpu_custom_call" | custom-call | flops 1000000000 | bytes 4194304 | tf_op jit(solution)/shard_map/pallas_call | solution.py:56
  11.8 0.0 collective-permute-done.2.first_ref
  11.8 0.0 collective-permute-done.3.second_ref
  11.9 0.1 collective-permute-start.4
  12.0 0.7 %collective-permute-start.5 = (f32[90,128]{1,0:T(8,128)S(1)}, f32[90,128]{1,0:T(8,128)S(1)}, u32[]{:S(2)}, u32[]{:S(2)}) collective-permute-start(f32[90,128]{1,0:T(8,128)S(1)} %get-tuple-element.58), channel_id=1, source_target_pairs={{0,4},{4,0},{8,12},{12,8},{1,5},{5,1},{9,13},{13,9},{2,6},{6,2},{1... | collective-permute-start | bytes 138248 | tf_op jit(solution)/shard_map/ppermute | solution.py:291
  12.7 0.0 collective-permute-done.cross_ref
  12.7 0.0 collective-permute-done.1.chip_ref
  12.7 1.2 %shard_map.61 = (bf16[416,640]{1,0:T(8,128)(2,1)S(1)}, bf16[416,640]{1,0:T(8,128)(2,1)S(1)}, bf16[7,112,640]{2,1,0:T(8,128)(2,1)S(1)}, bf16[7,112,640]{2,1,0:T(8,128)(2,1)S(1)}) custom-call(f32[160,640]{1,0:T(8,128)S(1)} %get-tuple-element.49.field_ref, f32[60,640]{1,0:T(8,128)S(1)} %collective-permute-done.cross_ref, ...), custom_call_target="tpu_custom_call" | custom-call | flops 770703360 | tf_op jit(solution)/shard_map/pallas_call | solution.py:56
  13.9 1.7 %collective-permute-done.4.cross_ref = f32[90,128]{1,0:T(8,128)S(1)} collective-permute-done((f32[90,128]{1,0:T(8,128)S(1)}, f32[90,128]{1,0:T(8,128)S(1)}, u32[]{:S(2)}, u32[]{:S(2)}) %collective-permute-start.4) | collective-permute-done | bytes 46112 | tf_op jit(solution)/shard_map/ppermute | solution.py:291
  15.6 0.0 collective-permute-done.5.chip_ref
  15.6 0.7 %shard_map.63 = (bf16[7,48,640]{2,1,0:T(8,128)(2,1)S(1)}, bf16[7,48,640]{2,1,0:T(8,128)(2,1)S(1)}) custom-call(f32[24,640]{1,0:T(8,128)S(1)} %collective-permute-done.2.first_ref, f32[24,640]{1,0:T(8,128)S(1)} %collective-permute-done.3.second_ref, f32[90,128]{1,0:T(8,128)S(1)} %collective-permute-done.4.cross_ref, ...), custom_call_target="tpu_custom_call" | custom-call | flops 330301440 | tf_op jit(solution)/shard_map/pallas_call | solution.py:56
  16.3 1.5 %shard_map.71 = (f32[160,256]{1,0:T(8,128)S(1)}, f32[160,256]{1,0:T(8,128)S(1)}) custom-call(bf16[7,112,640]{2,1,0:T(8,128)(2,1)S(1)} %get-tuple-element.53.ihigh_ref, bf16[7,112,640]{2,1,0:T(8,128)(2,1)S(1)} %get-tuple-element.54.ilow_ref, bf16[7,48,640]{2,1,0:T(8,128)(2,1)S(1)} %get-tuple-element.62.ohigh_ref, ...), custom_call_target="tpu_custom_call" | custom-call | flops 1101004800 | tf_op jit(solution)/shard_map/pallas_call | solution.py:56
  17.8 0.6 %collective-permute-start.9 = (f32[160,256]{1,0:T(8,128)S(1)}, f32[160,256]{1,0:T(8,128)S(1)}, u32[]{:S(2)}, u32[]{:S(2)}) collective-permute-start(f32[160,256]{1,0:T(8,128)S(1)} %get-tuple-element.75.own_ref.refs_1_), channel_id=1, source_target_pairs={{0,16},{16,0},{1,17},{17,1},{2,18},{18,2},{3,19},{19,3},{4,20},{20... | collective-permute-start | bytes 491528 | tf_op jit(solution)/shard_map/ppermute | solution.py:524
  18.4 1.5 %shard_map.68 = (f32[160,256]{1,0:T(8,128)S(1)}, f32[160,256]{1,0:T(8,128)S(1)}) custom-call(bf16[7,112,640]{2,1,0:T(8,128)(2,1)S(1)} %get-tuple-element.53.ihigh_ref, bf16[7,112,640]{2,1,0:T(8,128)(2,1)S(1)} %get-tuple-element.54.ilow_ref, bf16[7,48,640]{2,1,0:T(8,128)(2,1)S(1)} %get-tuple-element.62.ohigh_ref, ...), custom_call_target="tpu_custom_call" | custom-call | flops 1101004800 | tf_op jit(solution)/shard_map/pallas_call | solution.py:56
  19.9 1.6 %collective-permute-start.8 = (f32[160,256]{1,0:T(8,128)S(1)}, f32[160,256]{1,0:T(8,128)S(1)}, u32[]{:S(2)}, u32[]{:S(2)}) collective-permute-start(f32[160,256]{1,0:T(8,128)S(1)} %get-tuple-element.70.own_ref.refs_0_), channel_id=1, source_target_pairs={{0,16},{16,0},{1,17},{17,1},{2,18},{18,2},{3,19},{19,3},{4,20},{20... | collective-permute-start | bytes 491528 | tf_op jit(solution)/shard_map/ppermute | solution.py:524
  21.5 0.3 shard_map.64
  21.8 1.3 %shard_map.65 = (f32[160,128]{1,0:T(8,128)S(1)}, f32[160,128]{1,0:T(8,128)S(1)}) custom-call(bf16[7,112,640]{2,1,0:T(8,128)(2,1)S(1)} %get-tuple-element.53.ihigh_ref, bf16[7,112,640]{2,1,0:T(8,128)(2,1)S(1)} %get-tuple-element.54.ilow_ref, bf16[7,48,640]{2,1,0:T(8,128)(2,1)S(1)} %get-tuple-element.62.ohigh_ref, ...), custom_call_target="tpu_custom_call" | custom-call | flops 550502400 | tf_op jit(solution)/shard_map/pallas_call | solution.py:56
  23.2 0.6 %collective-permute-start.6 = (f32[160,128]{1,0:T(8,128)S(1)}, f32[160,128]{1,0:T(8,128)S(1)}, u32[]{:S(2)}, u32[]{:S(2)}) collective-permute-start(f32[160,128]{1,0:T(8,128)S(1)} %get-tuple-element.66.own_ref.refs_2_), channel_id=1, source_target_pairs={{0,16},{16,0},{1,17},{17,1},{2,18},{18,2},{3,19},{19,3},{4,20},{20... | collective-permute-start | bytes 245768 | tf_op jit(solution)/shard_map/ppermute | solution.py:524
  23.8 0.0 collective-permute-done.7.theirs_ref
  23.8 0.1 shard_map.66.analysis_ref
  23.9 1.0 %collective-permute-done.9.other_ref.refs_4_ = f32[160,256]{1,0:T(8,128)S(1)} collective-permute-done((f32[160,256]{1,0:T(8,128)S(1)}, f32[160,256]{1,0:T(8,128)S(1)}, u32[]{:S(2)}, u32[]{:S(2)}) %collective-permute-start.9) | collective-permute-done | bytes 163872 | tf_op jit(solution)/shard_map/ppermute | solution.py:524
  24.9 0.1 shard_map.72
  25.0 3.1 %collective-permute-done.8.other_ref.refs_3_ = f32[160,256]{1,0:T(8,128)S(1)} collective-permute-done((f32[160,256]{1,0:T(8,128)S(1)}, f32[160,256]{1,0:T(8,128)S(1)}, u32[]{:S(2)}, u32[]{:S(2)}) %collective-permute-start.8) | collective-permute-done | bytes 163872 | tf_op jit(solution)/shard_map/ppermute | solution.py:524
  28.1 0.1 shard_map.69
  28.2 0.8 %collective-permute-done.6.other_ref.refs_5_ = f32[160,128]{1,0:T(8,128)S(1)} collective-permute-done((f32[160,128]{1,0:T(8,128)S(1)}, f32[160,128]{1,0:T(8,128)S(1)}, u32[]{:S(2)}, u32[]{:S(2)}) %collective-permute-start.6) | collective-permute-done | bytes 81952 | tf_op jit(solution)/shard_map/ppermute | solution.py:524
  29.0 0.2 shard_map.73
  29.2 0.1 collective-permute-start.10
  29.3 1.3 %collective-permute-start.11 = (f32[60,640]{1,0:T(8,128)S(1)}, f32[60,640]{1,0:T(8,128)S(1)}, u32[]{:S(2)}, u32[]{:S(2)}) collective-permute-start(f32[60,640]{1,0:T(8,128)S(1)} %get-tuple-element.80), channel_id=1, source_target_pairs={{0,4},{4,0},{8,12},{12,8},{1,5},{5,1},{9,13},{13,9},{2,6},{6,2},{1... | collective-permute-start | bytes 460808 | tf_op jit(solution)/shard_map/ppermute | solution.py:291
  30.6 4.4 %collective-permute-start.12 = (f32[24,640]{1,0:T(8,128)S(1)}, f32[24,640]{1,0:T(8,128)S(1)}, u32[]{:S(2)}, u32[]{:S(2)}) collective-permute-start(f32[24,640]{1,0:T(8,128)S(1)} %get-tuple-element.84), channel_id=1, source_target_pairs={{0,1},{1,0},{2,3},{3,2},{4,5},{5,4},{6,7},{7,6},{8,9},{9,8},{10,11... | collective-permute-start | bytes 184328 | tf_op jit(solution)/shard_map/ppermute | solution.py:302
  35.0 0.7 %collective-permute-start.13 = (f32[24,640]{1,0:T(8,128)S(1)}, f32[24,640]{1,0:T(8,128)S(1)}, u32[]{:S(2)}, u32[]{:S(2)}) collective-permute-start(f32[24,640]{1,0:T(8,128)S(1)} %get-tuple-element.85), channel_id=1, source_target_pairs={{0,0},{1,2},{2,1},{3,3},{4,4},{5,6},{6,5},{7,7},{8,8},{9,10},{10,9... | collective-permute-start | bytes 184328 | tf_op jit(solution)/shard_map/ppermute | solution.py:302
  35.7 1.2 %shard_map.74 = (bf16[2,784,256]{2,1,0:T(8,128)(2,1)S(1)}, bf16[2,336,256]{2,1,0:T(8,128)(2,1)S(1)}) custom-call(f32[7,7,7,80]{3,2,1,0:T(8,128)S(1)} %copy-done.2), custom_call_target="tpu_custom_call" | custom-call | flops 1000000000 | bytes 4194304 | tf_op jit(solution)/shard_map/pallas_call | solution.py:56
  36.9 1.2 %shard_map.80 = f32[160,320]{1,0:T(8,128)} custom-call(f32[160,256]{1,0:T(8,128)S(1)} %get-tuple-element.70.own_ref.refs_0_, f32[160,256]{1,0:T(8,128)S(1)} %get-tuple-element.75.own_ref.refs_1_, f32[160,128]{1,0:T(8,128)S(1)} %get-tuple-element.66.own_ref.refs_2_, f32[160,256]{1,0:T(8,128)S(1)} %collective-permute-done.8.other_ref.refs_3_, ...), custom_call_target="tpu_custom_call" | custom-call | bytes 1048576 | tf_op jit(solution)/shard_map/pallas_call | solution.py:56
  38.1 0.0 collective-permute-done.12.first_ref
  38.1 0.0 collective-permute-done.13.second_ref
  38.1 0.1 collective-permute-start.14
  38.2 0.3 collective-permute-start.15
  38.5 0.0 collective-permute-done.10.cross_ref
  38.5 0.0 collective-permute-done.11.chip_ref
  38.5 1.2 %shard_map.75 = (bf16[416,640]{1,0:T(8,128)(2,1)S(1)}, bf16[416,640]{1,0:T(8,128)(2,1)S(1)}, bf16[7,112,640]{2,1,0:T(8,128)(2,1)S(1)}, bf16[7,112,640]{2,1,0:T(8,128)(2,1)S(1)}) custom-call(f32[160,640]{1,0:T(8,128)S(1)} %get-tuple-element.78.field_ref, f32[60,640]{1,0:T(8,128)S(1)} %collective-permute-done.10.cross_ref, ...), custom_call_target="tpu_custom_call" | custom-call | flops 770703360 | tf_op jit(solution)/shard_map/pallas_call | solution.py:56
  39.8 1.1 %shard_map.76.early_ref = f32[112,640]{1,0:T(8,128)S(1)} custom-call(bf16[7,112,640]{2,1,0:T(8,128)(2,1)S(1)} %get-tuple-element.82.ihigh_ref, bf16[7,112,640]{2,1,0:T(8,128)(2,1)S(1)} %get-tuple-element.83.ilow_ref, bf16[7,640,256]{2,1,0:T(8,128)(2,1)S(1)} %get-tuple-element.68.mhigh_ref.refs_0_.refs_3_, ...), custom_call_target="tpu_custom_call" | custom-call | flops 786432000 | tf_op jit(solution)/shard_map/pallas_call | solution.py:56
  40.9 1.2 %collective-permute-done.14.cross_ref = f32[90,128]{1,0:T(8,128)S(1)} collective-permute-done((f32[90,128]{1,0:T(8,128)S(1)}, f32[90,128]{1,0:T(8,128)S(1)}, u32[]{:S(2)}, u32[]{:S(2)}) %collective-permute-start.14) | collective-permute-done | bytes 46112 | tf_op jit(solution)/shard_map/ppermute | solution.py:291
  42.1 0.0 collective-permute-done.15.chip_ref
  42.1 0.7 %shard_map.78 = (bf16[7,48,640]{2,1,0:T(8,128)(2,1)S(1)}, bf16[7,48,640]{2,1,0:T(8,128)(2,1)S(1)}) custom-call(f32[24,640]{1,0:T(8,128)S(1)} %collective-permute-done.12.first_ref, f32[24,640]{1,0:T(8,128)S(1)} %collective-permute-done.13.second_ref, f32[90,128]{1,0:T(8,128)S(1)} %collective-permute-done.14.cross_ref, ...), custom_call_target="tpu_custom_call" | custom-call | flops 330301440 | tf_op jit(solution)/shard_map/pallas_call | solution.py:56
  42.8 4.9 %shard_map.79 = f32[160,640]{1,0:T(8,128)} custom-call(f32[112,640]{1,0:T(8,128)S(1)} %shard_map.76.early_ref, bf16[7,112,640]{2,1,0:T(8,128)(2,1)S(1)} %get-tuple-element.82.ihigh_ref, bf16[7,112,640]{2,1,0:T(8,128)(2,1)S(1)} %get-tuple-element.83.ilow_ref, bf16[7,48,640]{2,1,0:T(8,128)(2,1)S(1)} %get-tuple-element.91.ohigh_ref, ...), custom_call_target="tpu_custom_call" | custom-call | flops 2752512000 | tf_op jit(solution)/shard_map/pallas_call | solution.py:56
  (3 shorter events, 0.1 us)
Async XLA Ops:
  0.6 8.3 %slice-start = ((s8[11468800]{0:T(1024)(128)(4,1)}), s8[4194304]{0:T(1024)(128)(4,1)S(1)}, s32[]{:S(2)}) async-start(s8[11468800]{0:T(1024)(128)(4,1)} %bitcast.4), calls=%async_computation | async-start | bytes 8388608
  0.6 1.2 %copy-start.1 = (f32[1,20,8,640]{3,2,1,0:T(8,128)S(1)}, f32[1,20,8,640]{3,2,1,0:T(8,128)}, u32[]{:S(2)}) copy-start(f32[1,20,8,640]{3,2,1,0:T(8,128)} %param.4) | copy-start | bytes 1228804
  1.8 5.6 %copy-start = (f32[20,8,320]{2,1,0:T(8,128)S(1)}, f32[20,8,320]{2,1,0:T(8,128)}, u32[]{:S(2)}) copy-start(f32[20,8,320]{2,1,0:T(8,128)} %param.5) | copy-start | bytes 614404
  1.8 7.1 %slice-start.1 = ((s8[11468800]{0:T(1024)(128)(4,1)}), s8[4194304]{0:T(1024)(128)(4,1)S(1)}, s32[]{:S(2)}) async-start(s8[11468800]{0:T(1024)(128)(4,1)} %bitcast.4), calls=%async_computation.1 | async-start | bytes 8388608
  1.8 7.1 %slice-start.2 = ((s8[11468800]{0:T(1024)(128)(4,1)}), s8[3080192]{0:T(1024)(128)(4,1)S(1)}, s32[]{:S(2)}) async-start(s8[11468800]{0:T(1024)(128)(4,1)} %bitcast.4), calls=%async_computation.2 | async-start | bytes 6160384
  1.9 10.8 %collective-permute-start = (f32[60,640]{1,0:T(8,128)S(1)}, f32[60,640]{1,0:T(8,128)S(1)}, u32[]{:S(2)}, u32[]{:S(2)}) collective-permute-start(f32[60,640]{1,0:T(8,128)S(1)} %get-tuple-element.50), channel_id=1, source_target_pairs={{0,12},{4,8},{8,4},{12,0},{1,13},{5,9},{9,5},{13,1},{2,14},{6,10},... | collective-permute-start | bytes 460808 | tf_op jit(solution)/shard_map/ppermute | solution.py:291
  4.4 8.3 %collective-permute-start.1 = (f32[60,640]{1,0:T(8,128)S(1)}, f32[60,640]{1,0:T(8,128)S(1)}, u32[]{:S(2)}, u32[]{:S(2)}) collective-permute-start(f32[60,640]{1,0:T(8,128)S(1)} %get-tuple-element.51), channel_id=1, source_target_pairs={{0,4},{4,0},{8,12},{12,8},{1,5},{5,1},{9,13},{13,9},{2,6},{6,2},{1... | collective-permute-start | bytes 460808 | tf_op jit(solution)/shard_map/ppermute | solution.py:291
  5.1 6.7 %collective-permute-start.2 = (f32[24,640]{1,0:T(8,128)S(1)}, f32[24,640]{1,0:T(8,128)S(1)}, u32[]{:S(2)}, u32[]{:S(2)}) collective-permute-start(f32[24,640]{1,0:T(8,128)S(1)} %get-tuple-element.55), channel_id=1, source_target_pairs={{0,1},{1,0},{2,3},{3,2},{4,5},{5,4},{6,7},{7,6},{8,9},{9,8},{10,11... | collective-permute-start | bytes 184328 | tf_op jit(solution)/shard_map/ppermute | solution.py:302
  6.7 5.1 %collective-permute-start.3 = (f32[24,640]{1,0:T(8,128)S(1)}, f32[24,640]{1,0:T(8,128)S(1)}, u32[]{:S(2)}, u32[]{:S(2)}) collective-permute-start(f32[24,640]{1,0:T(8,128)S(1)} %get-tuple-element.56), channel_id=1, source_target_pairs={{0,0},{1,2},{2,1},{3,3},{4,4},{5,6},{6,5},{7,7},{8,8},{9,10},{10,9... | collective-permute-start | bytes 184328 | tf_op jit(solution)/shard_map/ppermute | solution.py:302
  7.4 16.4 %collective-permute-start.7 = (f32[160,320]{1,0:T(8,128)S(1)}, f32[160,320]{1,0:T(8,128)S(1)}, u32[]{:S(2)}, u32[]{:S(2)}) collective-permute-start(f32[160,320]{1,0:T(8,128)S(1)} %bitcast.6), channel_id=1, source_target_pairs={{0,16},{16,0},{1,17},{17,1},{2,18},{18,2},{3,19},{19,3},{4,20},{20... | collective-permute-start | bytes 614408 | tf_op jit(solution)/shard_map/ppermute | solution.py:510
  9.8 0.9 %copy-start.2 = (f32[7,7,7,80]{3,2,1,0:T(8,128)S(1)}, f32[7,7,7,80]{3,2,1,0:T(8,128)}, u32[]{:S(2)}) copy-start(f32[7,7,7,80]{3,2,1,0:T(8,128)} %stencils_ref.3) | copy-start | bytes 329284
  11.9 3.7 %collective-permute-start.4 = (f32[90,128]{1,0:T(8,128)S(1)}, f32[90,128]{1,0:T(8,128)S(1)}, u32[]{:S(2)}, u32[]{:S(2)}) collective-permute-start(f32[90,128]{1,0:T(8,128)S(1)} %get-tuple-element.57), channel_id=1, source_target_pairs={{0,12},{4,8},{8,4},{12,0},{1,13},{5,9},{9,5},{13,1},{2,14},{6,10},... | collective-permute-start | bytes 138248 | tf_op jit(solution)/shard_map/ppermute | solution.py:291
  12.0 3.7 %collective-permute-start.5 = (f32[90,128]{1,0:T(8,128)S(1)}, f32[90,128]{1,0:T(8,128)S(1)}, u32[]{:S(2)}, u32[]{:S(2)}) collective-permute-start(f32[90,128]{1,0:T(8,128)S(1)} %get-tuple-element.58), channel_id=1, source_target_pairs={{0,4},{4,0},{8,12},{12,8},{1,5},{5,1},{9,13},{13,9},{2,6},{6,2},{1... | collective-permute-start | bytes 138248 | tf_op jit(solution)/shard_map/ppermute | solution.py:291
  17.8 7.1 %collective-permute-start.9 = (f32[160,256]{1,0:T(8,128)S(1)}, f32[160,256]{1,0:T(8,128)S(1)}, u32[]{:S(2)}, u32[]{:S(2)}) collective-permute-start(f32[160,256]{1,0:T(8,128)S(1)} %get-tuple-element.75.own_ref.refs_1_), channel_id=1, source_target_pairs={{0,16},{16,0},{1,17},{17,1},{2,18},{18,2},{3,19},{19,3},{4,20},{20... | collective-permute-start | bytes 491528 | tf_op jit(solution)/shard_map/ppermute | solution.py:524
  19.9 8.2 %collective-permute-start.8 = (f32[160,256]{1,0:T(8,128)S(1)}, f32[160,256]{1,0:T(8,128)S(1)}, u32[]{:S(2)}, u32[]{:S(2)}) collective-permute-start(f32[160,256]{1,0:T(8,128)S(1)} %get-tuple-element.70.own_ref.refs_0_), channel_id=1, source_target_pairs={{0,16},{16,0},{1,17},{17,1},{2,18},{18,2},{3,19},{19,3},{4,20},{20... | collective-permute-start | bytes 491528 | tf_op jit(solution)/shard_map/ppermute | solution.py:524
  23.2 5.8 %collective-permute-start.6 = (f32[160,128]{1,0:T(8,128)S(1)}, f32[160,128]{1,0:T(8,128)S(1)}, u32[]{:S(2)}, u32[]{:S(2)}) collective-permute-start(f32[160,128]{1,0:T(8,128)S(1)} %get-tuple-element.66.own_ref.refs_2_), channel_id=1, source_target_pairs={{0,16},{16,0},{1,17},{17,1},{2,18},{18,2},{3,19},{19,3},{4,20},{20... | collective-permute-start | bytes 245768 | tf_op jit(solution)/shard_map/ppermute | solution.py:524
  29.2 9.4 %collective-permute-start.10 = (f32[60,640]{1,0:T(8,128)S(1)}, f32[60,640]{1,0:T(8,128)S(1)}, u32[]{:S(2)}, u32[]{:S(2)}) collective-permute-start(f32[60,640]{1,0:T(8,128)S(1)} %get-tuple-element.79), channel_id=1, source_target_pairs={{0,12},{4,8},{8,4},{12,0},{1,13},{5,9},{9,5},{13,1},{2,14},{6,10},... | collective-permute-start | bytes 460808 | tf_op jit(solution)/shard_map/ppermute | solution.py:291
  29.3 9.2 %collective-permute-start.11 = (f32[60,640]{1,0:T(8,128)S(1)}, f32[60,640]{1,0:T(8,128)S(1)}, u32[]{:S(2)}, u32[]{:S(2)}) collective-permute-start(f32[60,640]{1,0:T(8,128)S(1)} %get-tuple-element.80), channel_id=1, source_target_pairs={{0,4},{4,0},{8,12},{12,8},{1,5},{5,1},{9,13},{13,9},{2,6},{6,2},{1... | collective-permute-start | bytes 460808 | tf_op jit(solution)/shard_map/ppermute | solution.py:291
  30.6 7.5 %collective-permute-start.12 = (f32[24,640]{1,0:T(8,128)S(1)}, f32[24,640]{1,0:T(8,128)S(1)}, u32[]{:S(2)}, u32[]{:S(2)}) collective-permute-start(f32[24,640]{1,0:T(8,128)S(1)} %get-tuple-element.84), channel_id=1, source_target_pairs={{0,1},{1,0},{2,3},{3,2},{4,5},{5,4},{6,7},{7,6},{8,9},{9,8},{10,11... | collective-permute-start | bytes 184328 | tf_op jit(solution)/shard_map/ppermute | solution.py:302
  35.0 3.1 %collective-permute-start.13 = (f32[24,640]{1,0:T(8,128)S(1)}, f32[24,640]{1,0:T(8,128)S(1)}, u32[]{:S(2)}, u32[]{:S(2)}) collective-permute-start(f32[24,640]{1,0:T(8,128)S(1)} %get-tuple-element.85), channel_id=1, source_target_pairs={{0,0},{1,2},{2,1},{3,3},{4,4},{5,6},{6,5},{7,7},{8,8},{9,10},{10,9... | collective-permute-start | bytes 184328 | tf_op jit(solution)/shard_map/ppermute | solution.py:302
  38.1 4.0 %collective-permute-start.14 = (f32[90,128]{1,0:T(8,128)S(1)}, f32[90,128]{1,0:T(8,128)S(1)}, u32[]{:S(2)}, u32[]{:S(2)}) collective-permute-start(f32[90,128]{1,0:T(8,128)S(1)} %get-tuple-element.86), channel_id=1, source_target_pairs={{0,12},{4,8},{8,4},{12,0},{1,13},{5,9},{9,5},{13,1},{2,14},{6,10},... | collective-permute-start | bytes 138248 | tf_op jit(solution)/shard_map/ppermute | solution.py:291
  38.2 3.9 %collective-permute-start.15 = (f32[90,128]{1,0:T(8,128)S(1)}, f32[90,128]{1,0:T(8,128)S(1)}, u32[]{:S(2)}, u32[]{:S(2)}) collective-permute-start(f32[90,128]{1,0:T(8,128)S(1)} %get-tuple-element.87), channel_id=1, source_target_pairs={{0,4},{4,0},{8,12},{12,8},{1,5},{5,1},{9,13},{13,9},{2,6},{6,2},{1... | collective-permute-start | bytes 138248 | tf_op jit(solution)/shard_map/ppermute | solution.py:291
